TPU v7x, 32 devices: a whole 2x2x4 slice. The times are simulated.
32 devices in a mesh: dp: 4 (over y, x), seg: 8 (over z, core).
Axes of the slice: x: 2, y: 2, z: 4, core: 2. Of those that a mesh axis runs over, the one named last changes fastest.
Arguments:
- inputs: bfloat16 [4, 4096, 768], P('dp', 'seg'), may hold values from -6 to 6
- doc_ids: int32 [4, 32], P('dp'), may hold values from 0 to 7, never falling along the last dimension, each value on 1 to 16 neighbouring positions
- cotangent: bfloat16 [4, 4096, 768], P('dp', 'seg'), may hold values from -6 to 6
- query_weight: bfloat16 [2, 768, 768], P(None, 'dp'), may hold values from -0.21875 to 0.21875
- query_bias: bfloat16 [2, 768], replicated, may hold values from -3 to 3
- key_weight: bfloat16 [2, 768, 768], P(None, 'dp'), may hold values from -0.21875 to 0.21875
- value_weight: bfloat16 [2, 768, 768], P(None, 'dp'), may hold values from -0.21875 to 0.21875
- value_bias: bfloat16 [2, 768], replicated, may hold values from -3 to 3
- out_weight: bfloat16 [2, 768, 768], P(None, 'dp'), may hold values from -1.75 to 1.75
- out_bias: bfloat16 [2, 768], replicated, may hold values from -3 to 3
- first_gain: bfloat16 [2, 768], replicated, may hold values from 0.5 to 1.5
- first_shift: bfloat16 [2, 768], replicated, may hold values from -2 to 2
- inner_weight: bfloat16 [2, 768, 3072], P(None, 'dp'), may hold values from -0.21875 to 0.21875
- inner_bias: bfloat16 [2, 3072], replicated, may hold values from -3 to 3
- outer_weight: bfloat16 [2, 3072, 768], P(None, 'dp'), may hold values from -0.109375 to 0.109375
- outer_bias: bfloat16 [2, 768], replicated, may hold values from -3 to 3
- second_gain: bfloat16 [2, 768], replicated, may hold values from 0.5 to 1.5
- second_shift: bfloat16 [2, 768], replicated, may hold values from -2 to 2
- segment_embed: bfloat16 [32, 768], replicated, may hold values from -3 to 3
Outputs:
- output: bfloat16 [4, 4096, 768], P('dp', 'seg')
- input_grad: bfloat16 [4, 4096, 768], P('dp', 'seg')
- grad_query_weight: float32 [2, 768, 768], P(None, 'dp')
- grad_query_bias: float32 [2, 768], P(None, 'dp')
- grad_key_weight: float32 [2, 768, 768], P(None, 'dp')
- grad_value_weight: float32 [2, 768, 768], P(None, 'dp')
- grad_value_bias: float32 [2, 768], P(None, 'dp')
- grad_out_weight: float32 [2, 768, 768], P(None, 'dp')
- grad_out_bias: float32 [2, 768], P(None, 'dp')
- grad_first_gain: float32 [2, 768], P(None, 'dp')
- grad_first_shift: float32 [2, 768], P(None, 'dp')
- grad_inner_weight: float32 [2, 768, 3072], P(None, 'dp')
- grad_inner_bias: float32 [2, 3072], P(None, 'dp')
- grad_outer_weight: float32 [2, 3072, 768], P(None, 'dp')
- grad_outer_bias: float32 [2, 768], P(None, 'dp')
- grad_second_gain: float32 [2, 768], P(None, 'dp')
- grad_second_shift: float32 [2, 768], P(None, 'dp')
- grad_segment_embed: float32 [32, 768], P(None, 'dp')
Inputs may be any that keep to these rules, and one draw needn't show every extreme that they name: `doc_ids`: along each row document numbers never fall; each document covers one to half of 32 consecutive segments, and some document of each row covers exactly half of 32.
All inputs are finite; a program needn't handle non-finite values.
Results may differ from a plain program's by a relative error of at most 0.02.
Values may be sent and summed in bfloat16 or wider, within the bound.
A program may use at most 256 MiB of HBM per device.

v0:
```python
import jax
import jax.numpy as jnp
from jax import lax
from jax.sharding import PartitionSpec as P

HEADS = 12
HEAD_DIM = 64
SEG_LEN = 128


epsilon = 1e-05


def normalize(values, gain, shift):
    centred = values - jnp.mean(values, axis=-1, keepdims=True)
    spread = jnp.mean(centred * centred, axis=-1, keepdims=True)
    return centred * lax.rsqrt(spread + epsilon) * gain + shift


def gelu_exact(values):
    return jax.nn.gelu(values, approximate=False)


def project(values, weight):
    return jnp.einsum("gnd,de->gne", values, weight, preferred_element_type=jnp.float32)


def back_project(values, weight):
    return jnp.einsum("gne,de->gnd", values, weight, preferred_element_type=jnp.float32)


def weight_grad(source, grads):
    return jnp.einsum("gnd,gne->de", source, grads, preferred_element_type=jnp.float32)


def row_total(values):
    return jnp.sum(values.astype(jnp.float32), axis=(0, 1))


def keep_pair(first_part, second_part):
    return (first_part, second_part)


def forward_layer(params, source, allowed, spread_keys):
    (
        query_weight,
        query_bias,
        key_weight,
        value_weight,
        value_bias,
        out_weight,
        out_bias,
        first_gain,
        first_shift,
        inner_weight,
        inner_bias,
        outer_weight,
        outer_bias,
        second_gain,
        second_shift,
    ) = params
    groups, length, width = source.shape
    queries = (project(source, query_weight) + query_bias.astype(jnp.float32)).astype(jnp.bfloat16)
    key_rows = project(source, key_weight).astype(jnp.bfloat16)
    value_rows = (project(source, value_weight) + value_bias.astype(jnp.float32)).astype(
        jnp.bfloat16
    )
    key_all, value_all = spread_keys(key_rows, value_rows)
    key_length = key_all.shape[1]
    query_heads = queries.reshape(groups, length, HEADS, HEAD_DIM)
    key_heads = key_all.reshape(groups, key_length, HEADS, HEAD_DIM)
    value_heads = value_all.reshape(groups, key_length, HEADS, HEAD_DIM)
    scores = (
        jnp.einsum("gqhe,gkhe->ghqk", query_heads, key_heads, preferred_element_type=jnp.float32)
        * 0.125
    )
    if allowed is not None:
        scores = jnp.where(allowed[:, None], scores, -1e30)
    attend = jax.nn.softmax(scores, axis=-1)
    attend_low = attend.astype(jnp.bfloat16)
    mixed = jnp.einsum(
        "ghqk,gkhe->gqhe", attend_low, value_heads, preferred_element_type=jnp.float32
    )
    mixed = mixed.astype(jnp.bfloat16).reshape(groups, length, width)
    branch = project(mixed, out_weight) + out_bias.astype(jnp.float32)
    hidden, first_pull = jax.vjp(
        normalize,
        source.astype(jnp.float32) + branch,
        first_gain.astype(jnp.float32),
        first_shift.astype(jnp.float32),
    )
    hidden_low = hidden.astype(jnp.bfloat16)
    inner = project(hidden_low, inner_weight) + inner_bias.astype(jnp.float32)
    active, gelu_pull = jax.vjp(gelu_exact, inner)
    active_low = active.astype(jnp.bfloat16)
    outer = project(active_low, outer_weight) + outer_bias.astype(jnp.float32)
    result, second_pull = jax.vjp(
        normalize, hidden + outer, second_gain.astype(jnp.float32), second_shift.astype(jnp.float32)
    )
    stored = (
        source,
        query_heads,
        key_heads,
        value_heads,
        attend,
        attend_low,
        mixed,
        first_pull,
        hidden_low,
        gelu_pull,
        active_low,
        second_pull,
    )
    return (result, stored)


def backward_layer(params, stored, grad_result, collect_keys):
    (
        query_weight,
        query_bias,
        key_weight,
        value_weight,
        value_bias,
        out_weight,
        out_bias,
        first_gain,
        first_shift,
        inner_weight,
        inner_bias,
        outer_weight,
        outer_bias,
        second_gain,
        second_shift,
    ) = params
    (
        source,
        query_heads,
        key_heads,
        value_heads,
        attend,
        attend_low,
        mixed,
        first_pull,
        hidden_low,
        gelu_pull,
        active_low,
        second_pull,
    ) = stored
    groups, length, width = source.shape
    key_length = key_heads.shape[1]
    grad_second_sum, grad_second_gain, grad_second_shift = second_pull(grad_result)
    grad_outer = grad_second_sum.astype(jnp.bfloat16)
    grad_outer_bias = row_total(grad_outer)
    grad_outer_weight = weight_grad(active_low, grad_outer)
    grad_active = back_project(grad_outer, outer_weight).astype(jnp.bfloat16)
    (grad_inner,) = gelu_pull(grad_active.astype(jnp.float32))
    grad_inner_low = grad_inner.astype(jnp.bfloat16)
    grad_inner_bias = row_total(grad_inner_low)
    grad_inner_weight = weight_grad(hidden_low, grad_inner_low)
    grad_hidden = grad_second_sum + back_project(grad_inner_low, inner_weight)
    grad_first_sum, grad_first_gain, grad_first_shift = first_pull(grad_hidden)
    grad_branch = grad_first_sum.astype(jnp.bfloat16)
    grad_out_bias = row_total(grad_branch)
    grad_out_weight = weight_grad(mixed, grad_branch)
    grad_mixed = back_project(grad_branch, out_weight).astype(jnp.bfloat16)
    grad_mixed = grad_mixed.reshape(groups, length, HEADS, HEAD_DIM)
    grad_attend = jnp.einsum(
        "gqhe,gkhe->ghqk", grad_mixed, value_heads, preferred_element_type=jnp.float32
    )
    grad_attend = grad_attend.astype(jnp.bfloat16).astype(jnp.float32)
    grad_value = jnp.einsum(
        "ghqk,gqhe->gkhe", attend_low, grad_mixed, preferred_element_type=jnp.float32
    )
    grad_value = grad_value.reshape(groups, key_length, width)
    grad_scores = attend * (grad_attend - jnp.sum(attend * grad_attend, axis=-1, keepdims=True))
    grad_scores = grad_scores.astype(jnp.bfloat16)
    grad_query = (
        jnp.einsum("ghqk,gkhe->gqhe", grad_scores, key_heads, preferred_element_type=jnp.float32)
        * 0.125
    )
    grad_query = grad_query.astype(jnp.bfloat16).reshape(groups, length, width)
    grad_key = (
        jnp.einsum("ghqk,gqhe->gkhe", grad_scores, query_heads, preferred_element_type=jnp.float32)
        * 0.125
    )
    grad_key = grad_key.reshape(groups, key_length, width)
    grad_key, grad_value = collect_keys(grad_key, grad_value)
    grad_key = grad_key.astype(jnp.bfloat16)
    grad_value = grad_value.astype(jnp.bfloat16)
    grad_source = (
        grad_first_sum
        + back_project(grad_query, query_weight)
        + back_project(grad_key, key_weight)
        + back_project(grad_value, value_weight)
    )
    gradients = (
        weight_grad(source, grad_query),
        row_total(grad_query),
        weight_grad(source, grad_key),
        weight_grad(source, grad_value),
        row_total(grad_value),
        grad_out_weight,
        grad_out_bias,
        grad_first_gain,
        grad_first_shift,
        grad_inner_weight,
        grad_inner_bias,
        grad_outer_weight,
        grad_outer_bias,
        grad_second_gain,
        grad_second_shift,
    )
    return (grad_source, gradients)


def shards(
    inputs,
    doc_ids,
    cotangent,
    query_weight,
    query_bias,
    key_weight,
    value_weight,
    value_bias,
    out_weight,
    out_bias,
    first_gain,
    first_shift,
    inner_weight,
    inner_bias,
    outer_weight,
    outer_bias,
    second_gain,
    second_shift,
    segment_embed,
):
    seg_count = lax.axis_size("seg")
    seg_index = lax.axis_index("seg")
    group_rows, local_length, width = inputs.shape
    seg_local = local_length // SEG_LEN
    query_full, key_full, value_full, out_full, inner_full, outer_full = (
        lax.all_gather(query_weight, "dp", axis=1, tiled=True),
        lax.all_gather(key_weight, "dp", axis=1, tiled=True),
        lax.all_gather(value_weight, "dp", axis=1, tiled=True),
        lax.all_gather(out_weight, "dp", axis=1, tiled=True),
        lax.all_gather(inner_weight, "dp", axis=1, tiled=True),
        lax.all_gather(outer_weight, "dp", axis=1, tiled=True),
    )
    stacked = (
        query_full,
        query_bias,
        key_full,
        value_full,
        value_bias,
        out_full,
        out_bias,
        first_gain,
        first_shift,
        inner_full,
        inner_bias,
        outer_full,
        outer_bias,
        second_gain,
        second_shift,
    )
    first_params = tuple((weight[0] for weight in stacked))
    cross_params = tuple((weight[1] for weight in stacked))
    pieces = inputs.reshape(group_rows * seg_local, SEG_LEN, width)
    segment_out, segment_stored = forward_layer(first_params, pieces, None, keep_pair)
    segment_grid = segment_out.reshape(group_rows, seg_local, SEG_LEN, width)
    position = lax.dynamic_slice_in_dim(segment_embed, seg_index * seg_local, seg_local, 0).astype(
        jnp.float32
    )
    heads_in = (segment_grid[:, :, 0, :] + position).astype(jnp.bfloat16)
    row_input = lax.all_gather(heads_in, "seg", axis=1, tiled=True)
    allowed = doc_ids[:, :, None] == doc_ids[:, None, :]
    cross_out, cross_stored = forward_layer(cross_params, row_input, allowed, keep_pair)
    returned = lax.dynamic_slice_in_dim(cross_out, seg_index * seg_local, seg_local, 1).astype(
        jnp.bfloat16
    )
    output = jnp.concatenate(
        [returned[:, :, None, :], segment_grid[:, :, 1:, :].astype(jnp.bfloat16)], axis=2
    )
    output = output.reshape(group_rows, local_length, width)
    cot_grid = cotangent.reshape(group_rows, seg_local, SEG_LEN, width)
    cot_heads = cot_grid[:, :, 0, :]
    grad_cross = lax.all_gather(cot_heads, "seg", axis=1, tiled=True)
    grad_row_input, cross_grads = backward_layer(
        cross_params, cross_stored, grad_cross.astype(jnp.float32), keep_pair
    )
    grad_row_low = grad_row_input.astype(jnp.bfloat16)
    factor = 1.0 / seg_count
    embed_grad = jnp.sum(grad_row_low.astype(jnp.float32), axis=0) * factor
    cross_grads = tuple((part * factor for part in cross_grads))
    grad_heads = lax.dynamic_slice_in_dim(grad_row_low, seg_index * seg_local, seg_local, 1)
    grad_grid = jnp.concatenate(
        [grad_heads[:, :, None, :].astype(jnp.float32), cot_grid[:, :, 1:, :].astype(jnp.float32)],
        axis=2,
    )
    grad_grid = grad_grid.reshape(group_rows * seg_local, SEG_LEN, width)
    grad_pieces, segment_grads = backward_layer(first_params, segment_stored, grad_grid, keep_pair)
    input_grad = grad_pieces.astype(jnp.bfloat16).reshape(group_rows, local_length, width)
    shares = (
        lax.psum_scatter(segment_grads[0], "dp", scatter_dimension=0, tiled=True),
        lax.psum_scatter(segment_grads[1], "dp", scatter_dimension=0, tiled=True),
        lax.psum_scatter(segment_grads[2], "dp", scatter_dimension=0, tiled=True),
        lax.psum_scatter(segment_grads[3], "dp", scatter_dimension=0, tiled=True),
        lax.psum_scatter(segment_grads[4], "dp", scatter_dimension=0, tiled=True),
        lax.psum_scatter(segment_grads[5], "dp", scatter_dimension=0, tiled=True),
        lax.psum_scatter(segment_grads[6], "dp", scatter_dimension=0, tiled=True),
        lax.psum_scatter(segment_grads[7], "dp", scatter_dimension=0, tiled=True),
        lax.psum_scatter(segment_grads[8], "dp", scatter_dimension=0, tiled=True),
        lax.psum_scatter(segment_grads[9], "dp", scatter_dimension=0, tiled=True),
        lax.psum_scatter(segment_grads[10], "dp", scatter_dimension=0, tiled=True),
        lax.psum_scatter(segment_grads[11], "dp", scatter_dimension=0, tiled=True),
        lax.psum_scatter(segment_grads[12], "dp", scatter_dimension=0, tiled=True),
        lax.psum_scatter(segment_grads[13], "dp", scatter_dimension=0, tiled=True),
        lax.psum_scatter(segment_grads[14], "dp", scatter_dimension=0, tiled=True),
        lax.psum_scatter(cross_grads[0], "dp", scatter_dimension=0, tiled=True),
        lax.psum_scatter(cross_grads[1], "dp", scatter_dimension=0, tiled=True),
        lax.psum_scatter(cross_grads[2], "dp", scatter_dimension=0, tiled=True),
        lax.psum_scatter(cross_grads[3], "dp", scatter_dimension=0, tiled=True),
        lax.psum_scatter(cross_grads[4], "dp", scatter_dimension=0, tiled=True),
        lax.psum_scatter(cross_grads[5], "dp", scatter_dimension=0, tiled=True),
        lax.psum_scatter(cross_grads[6], "dp", scatter_dimension=0, tiled=True),
        lax.psum_scatter(cross_grads[7], "dp", scatter_dimension=0, tiled=True),
        lax.psum_scatter(cross_grads[8], "dp", scatter_dimension=0, tiled=True),
        lax.psum_scatter(cross_grads[9], "dp", scatter_dimension=0, tiled=True),
        lax.psum_scatter(cross_grads[10], "dp", scatter_dimension=0, tiled=True),
        lax.psum_scatter(cross_grads[11], "dp", scatter_dimension=0, tiled=True),
        lax.psum_scatter(cross_grads[12], "dp", scatter_dimension=0, tiled=True),
        lax.psum_scatter(cross_grads[13], "dp", scatter_dimension=0, tiled=True),
        lax.psum_scatter(cross_grads[14], "dp", scatter_dimension=0, tiled=True),
        lax.psum_scatter(embed_grad, "dp", scatter_dimension=1, tiled=True),
    )
    summed = lax.psum(
        (
            shares[0],
            shares[1],
            shares[2],
            shares[3],
            shares[4],
            shares[5],
            shares[6],
            shares[7],
            shares[8],
            shares[9],
            shares[10],
            shares[11],
            shares[12],
            shares[13],
            shares[14],
            shares[15],
            shares[16],
            shares[17],
            shares[18],
            shares[19],
            shares[20],
            shares[21],
            shares[22],
            shares[23],
            shares[24],
            shares[25],
            shares[26],
            shares[27],
            shares[28],
            shares[29],
            shares[30],
        ),
        "seg",
    )
    totals = tuple((jnp.stack([summed[index], summed[index + 15]]) for index in range(15)))
    totals = totals + (summed[30],)
    return (output, input_grad) + tuple(totals)


def solution(mesh):
    placed = (
        P("dp", "seg", None),
        P("dp", None),
        P("dp", "seg", None),
        P(None, "dp", None),
        P(),
        P(None, "dp", None),
        P(None, "dp", None),
        P(),
        P(None, "dp", None),
        P(),
        P(),
        P(),
        P(None, "dp", None),
        P(),
        P(None, "dp", None),
        P(),
        P(),
        P(),
        P(),
    )
    return jax.shard_map(
        shards,
        mesh=mesh,
        in_specs=placed,
        out_specs=(
            P("dp", "seg", None),
            P("dp", "seg", None),
            P(None, "dp", None),
            P(None, "dp"),
            P(None, "dp", None),
            P(None, "dp", None),
            P(None, "dp"),
            P(None, "dp", None),
            P(None, "dp"),
            P(None, "dp"),
            P(None, "dp"),
            P(None, "dp", None),
            P(None, "dp"),
            P(None, "dp", None),
            P(None, "dp"),
            P(None, "dp"),
            P(None, "dp"),
            P(None, "dp"),
        ),
        check_vma=False,
    )
```

profile of v0, /device:TPU:1, one launch (start us, length us, event | category | flops | bytes accessed | tf_op | source)
XLA Modules:
  0.0 1614.1 jit_solution(5747079479511893777)
XLA Ops:
  11.4 15.5 all-gather.1
  32.0 17.2 %all-gather.10.cloned.1.call-done = bf16[2,768,768]{2,1,0:T(8,128)(2,1)} async-done(((bf16[2,192,768]{2,1,0:T(8,128)(2,1)}), bf16[2,768,768]{2,1,0:T(8,128)(2,1)}) %all-gather.10.cloned.1.call-update) | async-done | bytes 2359312 | tf_op jit(solution)/shard_map/all_gather | solution.py:244
  52.3 36.0 %all-gather.12.cloned.1.call-done = bf16[2,768,768]{2,1,0:T(8,128)(2,1)} async-done(((bf16[2,192,768]{2,1,0:T(8,128)(2,1)}), bf16[2,768,768]{2,1,0:T(8,128)(2,1)}) %all-gather.12.cloned.1.call-update) | async-done | bytes 2359312 | tf_op jit(solution)/shard_map/all_gather | solution.py:242
  90.8 36.8 %all-gather.14.cloned.1.call-done = bf16[2,768,768]{2,1,0:T(8,128)(2,1)} async-done(((bf16[2,192,768]{2,1,0:T(8,128)(2,1)}), bf16[2,768,768]{2,1,0:T(8,128)(2,1)}) %all-gather.14.cloned.1.call-update) | async-done | bytes 2359312 | tf_op jit(solution)/shard_map/all_gather | solution.py:243
  130.0 2.9 fusion.106
  132.9 2.7 convolution_convert_fusion.5
  135.7 31.0 %all-gather.16.cloned.1.call-done = bf16[2,768,768]{2,1,0:T(8,128)(2,1)} async-done(((bf16[2,192,768]{2,1,0:T(8,128)(2,1)}), bf16[2,768,768]{2,1,0:T(8,128)(2,1)}) %all-gather.16.cloned.1.call-update) | async-done | bytes 2359312 | tf_op jit(solution)/shard_map/all_gather | solution.py:245
  169.2 95.4 %all-gather.18.cloned.1.call-done = bf16[2,768,3072]{2,1,0:T(8,128)(2,1)} async-done(((bf16[2,192,3072]{2,1,0:T(8,128)(2,1)}), bf16[2,768,3072]{2,1,0:T(8,128)(2,1)}) %all-gather.18.cloned.1.call-update) | async-done | bytes 9437200 | tf_op jit(solution)/shard_map/all_gather | solution.py:246
  264.6 6.9 fusion.33
  271.5 2.8 copy-done.7
  274.3 15.7 multiply_convert_fusion
  290.0 72.5 %all-gather.20.cloned.1.call-done = bf16[2,3072,768]{2,1,0:T(8,128)(2,1)} async-done(((bf16[2,768,768]{2,1,0:T(8,128)(2,1)}), bf16[2,3072,768]{2,1,0:T(8,128)(2,1)}) %all-gather.20.cloned.1.call-update) | async-done | bytes 9437200 | tf_op jit(solution)/shard_map/all_gather | solution.py:247
  362.5 6.0 fusion.108
  371.7 14.7 all-gather.2
  400.6 3.4 fusion.22
  404.1 4.6 fusion.46
  423.1 2.4 convert_reduce_fusion.6
  439.0 9.9 multiply_reduce_fusion.1
  450.5 8.9 convert_reduce_fusion
  459.4 3.6 multiply_reduce_fusion.2
  467.7 3.2 convert_reduce_fusion.3
  474.0 3.1 copy.176
  478.3 2.9 fusion.25
  486.0 3.0 copy.168
  489.3 2.4 multiply_convert_fusion.1
  494.8 3.1 copy.172
  501.6 2.8 convolution_multiply_fusion.2
  510.5 7.2 convolution_bitcast_fusion.1
  519.6 6.2 convolution_bitcast_fusion
  526.8 5.9 convolution_multiply_fusion
  533.7 5.0 convolution_multiply_fusion.1
  551.9 2.6 reduce-scatter.40.cloned.1.call-done
  556.7 38.3 %reduce-scatter.44.cloned.1.call-done = f32[192,768]{1,0:T(8,128)} async-done(((f32[768,768]{1,0:T(8,128)}), f32[192,768]{1,0:T(8,128)}) %reduce-scatter.44.cloned.1.call-update) | async-done | bytes 589840
  597.1 38.1 %reduce-scatter.52.cloned.1.call-done = f32[192,768]{1,0:T(8,128)} async-done(((f32[768,768]{1,0:T(8,128)}), f32[192,768]{1,0:T(8,128)}) %reduce-scatter.52.cloned.1.call-update) | async-done | bytes 589840
  637.5 38.2 %reduce-scatter.54.cloned.1.call-done = f32[192,768]{1,0:T(8,128)} async-done(((f32[768,768]{1,0:T(8,128)}), f32[192,768]{1,0:T(8,128)}) %reduce-scatter.54.cloned.1.call-update) | async-done | bytes 589840
  677.9 38.1 %reduce-scatter.50.cloned.1.call-done = f32[192,768]{1,0:T(8,128)} async-done(((f32[768,768]{1,0:T(8,128)}), f32[192,768]{1,0:T(8,128)}) %reduce-scatter.50.cloned.1.call-update) | async-done | bytes 589840
  718.3 38.8 %reduce-scatter.42.cloned.1.call-done = f32[192,768]{1,0:T(8,128)} async-done(((f32[768,768]{1,0:T(8,128)}), f32[192,768]{1,0:T(8,128)}) %reduce-scatter.42.cloned.1.call-update) | async-done | bytes 589840
  759.3 38.1 %reduce-scatter.46.cloned.1.call-done = f32[192,768]{1,0:T(8,128)} async-done(((f32[768,768]{1,0:T(8,128)}), f32[192,768]{1,0:T(8,128)}) %reduce-scatter.46.cloned.1.call-update) | async-done | bytes 589840
  799.6 95.7 %reduce-scatter.32.cloned.1.call-done = f32[192,3072]{1,0:T(8,128)} async-done(((f32[768,3072]{1,0:T(8,128)}), f32[192,3072]{1,0:T(8,128)}) %reduce-scatter.32.cloned.1.call-update) | async-done | bytes 2359312 | tf_op jit(solution)/shard_map/reduce_scatter | solution.py:313
  895.3 97.9 %reduce-scatter.36.cloned.1.call-done = f32[768,768]{1,0:T(8,128)} async-done(((f32[3072,768]{1,0:T(8,128)}), f32[768,768]{1,0:T(8,128)}) %reduce-scatter.36.cloned.1.call-update) | async-done | bytes 2359312 | tf_op jit(solution)/shard_map/reduce_scatter | solution.py:315
  993.2 97.9 %reduce-scatter.38.cloned.1.call-done = f32[768,768]{1,0:T(8,128)} async-done(((f32[3072,768]{1,0:T(8,128)}), f32[768,768]{1,0:T(8,128)}) %reduce-scatter.38.cloned.1.call-update) | async-done | bytes 2359312 | tf_op jit(solution)/shard_map/reduce_scatter | solution.py:330
  1091.1 97.9 %reduce-scatter.34.cloned.1.call-done = f32[192,3072]{1,0:T(8,128)} async-done(((f32[768,3072]{1,0:T(8,128)}), f32[192,3072]{1,0:T(8,128)}) %reduce-scatter.34.cloned.1.call-update) | async-done | bytes 2359312 | tf_op jit(solution)/shard_map/reduce_scatter | solution.py:328
  1199.3 44.0 %all-reduce.26.cloned.1.call-done = (f32[768]{0:T(1024)}, f32[768]{0:T(1024)}, f32[768]{0:T(1024)}, f32[768]{0:T(1024)}, f32[768]{0:T(1024)}, /*index=5*/f32[768...) async-done(((f32[768]{0:T(1024)}, f32[768]{0:T(1024)}, ...) | async-done | bytes 73744
  1256.8 13.6 reduce-scatter.56.cloned.1.call-done
  1271.4 26.9 %all-reduce.18 = (f32[1,192]{1,0:T(1,128)S(1)}, f32[1,192]{1,0:T(1,128)S(1)}, f32[1,192]{1,0:T(1,128)S(1)}, f32[1,192]{1,0:T(1,128)S(1)}, f32[1,192]{1,0:T(1,128...) all-reduce(f32[1,192]{1,0:T(1,128)S(1)} %bitcast.354, ...), channel_id=1, replica_groups=mesh['dp'=4,'seg'=8] {'seg'}, use_global_device_ids=true, to_apply=%region_31.32 | all-reduce | flops 10752 | bytes 86016 | tf_op jit(solution)/shard_map/psum | solution.py:336
  1303.6 286.2 %all-reduce.24.cloned.1.call-done = (f32[1,192,768]{1,2,0:T(8,128)}, f32[1,192,768]{1,2,0:T(8,128)}, f32[1,192,768]{1,2,0:T(8,128)}, f32[1,192,768]{1,2,0:T(8,12...) async-done(((f32[1,192,768]{1,2,0:T(8,128)}, ...) | async-done | bytes 14155792 | tf_op jit(solution)/shard_map/psum | solution.py:336
  1599.1 5.2 pad_maximum_fusion
  1604.3 2.5 pad_maximum_fusion.1
  (434 shorter events, 163.1 us)
Async XLA Ops:
  7.2 41.9 %all-gather.10.cloned.1.call-start = ((), (), s32[]{:S(2)}) async-start(), calls=%async_computation.13 | async-start | bytes 2949120 | tf_op jit(solution)/shard_map/all_gather | solution.py:244
  7.9 80.4 %all-gather.12.cloned.1.call-start = ((), (), s32[]{:S(2)}) async-start(), calls=%async_computation.14 | async-start | bytes 2949120 | tf_op jit(solution)/shard_map/all_gather | solution.py:242
  8.7 118.9 %all-gather.14.cloned.1.call-start = ((), (), s32[]{:S(2)}) async-start(), calls=%async_computation.15 | async-start | bytes 2949120 | tf_op jit(solution)/shard_map/all_gather | solution.py:243
  9.4 157.2 %all-gather.16.cloned.1.call-start = ((), (), s32[]{:S(2)}) async-start(), calls=%async_computation.16 | async-start | bytes 2949120 | tf_op jit(solution)/shard_map/all_gather | solution.py:245
  10.0 16.8 %copy-start.83 = (bf16[2,768]{1,0:T(2,128)(2,1)S(1)}, bf16[2,768]{1,0:T(2,128)(2,1)}, u32[]{:S(2)}) copy-start(bf16[2,768]{1,0:T(2,128)(2,1)} %param.23) | copy-start | bytes 9220
  10.0 16.8 %copy-start.84 = (bf16[2,768]{1,0:T(2,128)(2,1)S(1)}, bf16[2,768]{1,0:T(2,128)(2,1)}, u32[]{:S(2)}) copy-start(bf16[2,768]{1,0:T(2,128)(2,1)} %param.26) | copy-start | bytes 9220
  10.0 16.9 %copy-start.85 = (bf16[2,768]{1,0:T(2,128)(2,1)S(1)}, bf16[2,768]{1,0:T(2,128)(2,1)}, u32[]{:S(2)}) copy-start(bf16[2,768]{1,0:T(2,128)(2,1)} %param.28) | copy-start | bytes 9220
  10.0 17.5 %copy-start.86 = (bf16[2,768]{1,0:T(2,128)(2,1)S(1)}, bf16[2,768]{1,0:T(2,128)(2,1)}, u32[]{:S(2)}) copy-start(bf16[2,768]{1,0:T(2,128)(2,1)} %param.29) | copy-start | bytes 9220
  10.0 18.1 %copy-start.87 = (bf16[2,768]{1,0:T(2,128)(2,1)S(1)}, bf16[2,768]{1,0:T(2,128)(2,1)}, u32[]{:S(2)}) copy-start(bf16[2,768]{1,0:T(2,128)(2,1)} %param.34) | copy-start | bytes 9220
  10.1 18.1 %copy-start.88 = (bf16[2,768]{1,0:T(2,128)(2,1)S(1)}, bf16[2,768]{1,0:T(2,128)(2,1)}, u32[]{:S(2)}) copy-start(bf16[2,768]{1,0:T(2,128)(2,1)} %param.30) | copy-start | bytes 9220
  10.1 18.7 %copy-start.89 = (bf16[2,768]{1,0:T(2,128)(2,1)S(1)}, bf16[2,768]{1,0:T(2,128)(2,1)}, u32[]{:S(2)}) copy-start(bf16[2,768]{1,0:T(2,128)(2,1)} %param.36) | copy-start | bytes 9220
  10.1 18.7 %copy-start.90 = (bf16[2,768]{1,0:T(2,128)(2,1)S(1)}, bf16[2,768]{1,0:T(2,128)(2,1)}, u32[]{:S(2)}) copy-start(bf16[2,768]{1,0:T(2,128)(2,1)} %param.35) | copy-start | bytes 9220
  10.1 19.3 %copy-start.99 = (s32[1,32]{1,0:T(1,128)S(1)}, s32[1,32]{1,0:T(1,128)}, u32[]{:S(2)}) copy-start(s32[1,32]{1,0:T(1,128)} %param.20) | copy-start | bytes 388
  10.1 254.5 %all-gather.18.cloned.1.call-start = ((), (), s32[]{:S(2)}) async-start(), calls=%async_computation.17 | async-start | bytes 11796480 | tf_op jit(solution)/shard_map/all_gather | solution.py:246
  10.7 20.7 %copy-start.66 = (bf16[2,3072]{1,0:T(2,128)(2,1)S(1)}, bf16[2,3072]{1,0:T(2,128)(2,1)}, u32[]{:S(2)}) copy-start(bf16[2,3072]{1,0:T(2,128)(2,1)} %param.32) | copy-start | bytes 36868
  10.7 38.4 %copy-start.3 = (bf16[1,512,768]{2,1,0:T(8,128)(2,1)S(1)}, bf16[1,512,768]{2,1,0:T(8,128)(2,1)}, u32[]{:S(2)}) copy-start(bf16[1,512,768]{2,1,0:T(8,128)(2,1)} %param.19) | copy-start | bytes 2359300
  10.7 351.8 %all-gather.20.cloned.1.call-start = ((), (), s32[]{:S(2)}) async-start(), calls=%async_computation.18 | async-start | bytes 11796480 | tf_op jit(solution)/shard_map/all_gather | solution.py:247
  11.3 538.4 %reduce-scatter.48.cloned.1.call-start = ((), (), s32[]{:S(2)}) async-start(), calls=%async_computation.27 | async-start | bytes 2949120
  28.1 334.4 %copy-start.81 = (f32[768]{0:T(1024)}, f32[768]{0:T(1024)S(1)}, u32[]{:S(2)}) copy-start(f32[768]{0:T(1024)S(1)} %get-tuple-element.91) | copy-start | bytes 9220
  28.8 333.7 %copy-start.96 = (f32[768]{0:T(1024)}, f32[768]{0:T(1024)S(1)}, u32[]{:S(2)}) copy-start(f32[768]{0:T(1024)S(1)} %get-tuple-element.207) | copy-start | bytes 9220
  29.4 340.1 %copy-start.58 = (f32[768]{0:T(1024)}, f32[768]{0:T(1024)S(1)}, u32[]{:S(2)}) copy-start(f32[768]{0:T(1024)S(1)} %get-tuple-element.209) | copy-start | bytes 9220
  32.0 239.5 %copy-start.64 = (f32[1,3072]{1,0:T(1,128)}, f32[1,3072]{1,0:T(1,128)S(1)}, u32[]{:S(2)}) copy-start(f32[1,3072]{1,0:T(1,128)S(1)} %get-tuple-element.178) | copy-start | bytes 36868
  90.8 39.2 %copy-start.14 = (bf16[4,128,768]{1,2,0:T(8,128)(2,1)}, bf16[4,128,768]{1,2,0:T(8,128)(2,1)S(1)}, u32[]{:S(2)}) copy-start(bf16[4,128,768]{1,2,0:T(8,128)(2,1)S(1)} %copy.115) | copy-start | bytes 2359300
  135.7 33.5 %copy-start.17 = (bf16[4,12,64,128]{3,2,1,0:T(8,128)(2,1)}, bf16[4,12,64,128]{3,2,1,0:T(8,128)(2,1)S(1)}, u32[]{:S(2)}) copy-start(bf16[4,12,64,128]{3,2,1,0:T(8,128)(2,1)S(1)} %convolution_convert_fusion.5) | copy-start | bytes 2359300
  168.8 193.7 %copy-start.71 = (f32[4,128]{1,0:T(4,128)}, f32[4,128]{1,0:T(4,128)S(1)}, u32[]{:S(2)}) copy-start(f32[4,128]{1,0:T(4,128)S(1)} %broadcast_multiply_fusion.11) | copy-start | bytes 6148
  169.2 95.4 %copy-start.73 = (f32[4,128]{1,0:T(4,128)}, f32[4,128]{1,0:T(4,128)S(1)}, u32[]{:S(2)}) copy-start(f32[4,128]{1,0:T(4,128)S(1)} %multiply_reduce_fusion.6) | copy-start | bytes 6148
  169.2 193.3 %copy-start.93 = (f32[4,128]{1,0:T(4,128)}, f32[4,128]{1,0:T(4,128)S(1)}, u32[]{:S(2)}) copy-start(f32[4,128]{1,0:T(4,128)S(1)} %fusion.95) | copy-start | bytes 6148
  400.6 11.4 copy-start.101
  404.1 10.3 slice-start.2
  404.1 10.3 slice-start.3
  417.7 9.9 copy-start.100
  431.7 18.7 %slice-start = ((s8[6291456]{0:T(1024)(128)(4,1)}), s8[4194304]{0:T(1024)(128)(4,1)S(1)}, s32[]{:S(2)}) async-start(s8[6291456]{0:T(1024)(128)(4,1)} %bitcast.309), calls=%async_computation.34 | async-start | bytes 8388608
  435.6 13.3 copy-start.76
  439.0 11.4 slice-start.1
  477.1 77.3 %reduce-scatter.40.cloned.1.call-start = ((), (), s32[]{:S(2)}) async-start(), calls=%async_computation.23 | async-start | bytes 2949120
  489.0 105.9 %reduce-scatter.44.cloned.1.call-start = ((), (), s32[]{:S(2)}) async-start(), calls=%async_computation.25 | async-start | bytes 2949120
  497.9 137.3 %reduce-scatter.52.cloned.1.call-start = ((), (), s32[]{:S(2)}) async-start(), calls=%async_computation.29 | async-start | bytes 2949120
  501.5 174.2 %reduce-scatter.54.cloned.1.call-start = ((), (), s32[]{:S(2)}) async-start(), calls=%async_computation.30 | async-start | bytes 2949120
  504.4 211.6 %reduce-scatter.50.cloned.1.call-start = ((), (), s32[]{:S(2)}) async-start(), calls=%async_computation.28 | async-start | bytes 2949120
  506.4 250.6 %reduce-scatter.42.cloned.1.call-start = ((), (), s32[]{:S(2)}) async-start(), calls=%async_computation.24 | async-start | bytes 2949120
  508.4 289.0 %reduce-scatter.46.cloned.1.call-start = ((), (), s32[]{:S(2)}) async-start(), calls=%async_computation.26 | async-start | bytes 2949120
  510.4 384.9 %reduce-scatter.32.cloned.1.call-start = ((), (), s32[]{:S(2)}) async-start(), calls=%async_computation.19 | async-start | bytes 11796480 | tf_op jit(solution)/shard_map/reduce_scatter | solution.py:313
  517.7 475.5 %reduce-scatter.36.cloned.1.call-start = ((), (), s32[]{:S(2)}) async-start(), calls=%async_computation.21 | async-start | bytes 11796480 | tf_op jit(solution)/shard_map/reduce_scatter | solution.py:315
  525.8 565.2 %reduce-scatter.38.cloned.1.call-start = ((), (), s32[]{:S(2)}) async-start(), calls=%async_computation.22 | async-start | bytes 11796480 | tf_op jit(solution)/shard_map/reduce_scatter | solution.py:330
  532.7 656.3 %reduce-scatter.34.cloned.1.call-start = ((), (), s32[]{:S(2)}) async-start(), calls=%async_computation.20 | async-start | bytes 11796480 | tf_op jit(solution)/shard_map/reduce_scatter | solution.py:328
  538.8 704.5 %all-reduce.26.cloned.1.call-start = ((), (), s32[]{:S(2)}) async-start(), calls=%async_computation.33 | async-start | bytes 180224
  548.3 722.1 %reduce-scatter.56.cloned.1.call-start = ((), (), s32[]{:S(2)}) async-start(), calls=%async_computation.31 | async-start | bytes 491520
  549.3 1040.4 %all-reduce.24.cloned.1.call-start = ((), (), s32[]{:S(2)}) async-start(), calls=%async_computation.32 | async-start | bytes 31457280 | tf_op jit(solution)/shard_map/psum | solution.py:336
  (85 other events, 314.6 us)
Sparse Core Ops, SparseCore 0:
  9.8 39.2 all-gather.9
  51.0 37.3 all-gather.11
  90.2 37.3 all-gather.13
  129.3 37.3 all-gather.15
  168.3 96.1 all-gather.17
  266.3 96.1 all-gather.19
  477.3 36.6 reduce-scatter.47
  517.1 37.3 reduce-scatter.39
  557.5 37.3 reduce-scatter.43
  597.8 37.3 reduce-scatter.51
  638.3 37.3 reduce-scatter.53
  678.6 37.3 reduce-scatter.49
  719.6 37.3 reduce-scatter.41
  760.0 37.3 reduce-scatter.45
  800.3 94.9 reduce-scatter.31
  898.3 94.8 reduce-scatter.35
  996.2 94.8 reduce-scatter.37
  1094.0 94.8 reduce-scatter.33
  1194.9 48.3 all-reduce.25
  1245.9 24.4 reduce-scatter.55
  1275.0 314.7 all-reduce.23
where the time goes:
time: 1630 us; the launch traced here: 1610 us
  waiting for transfers between devices  1260 us (77%)
  matrix products  130 us (8%)
  local copies, waits for them, and re-layouts  81.3 us (5%)
  other arithmetic  69.1 us (4%)
  blocking collectives  57.1 us (4%)
  between operations  17.5 us (1%)
    unnamed x31, waiting for transfers between devices  294 us
    psum x1, waiting for transfers between devices, shards(): lax.psum((shares[0], shares[1], shares[2], shares[3], shares[4], shares[5...  286 us
    reduce_scatter x1, waiting for transfers between devices, shards(): lax.psum_scatter(segment_grads[11], 'dp', scatter_dimension=0, tiled=True)  97.9 us
    reduce_scatter x1, waiting for transfers between devices, shards(): lax.psum_scatter(cross_grads[9], 'dp', scatter_dimension=0, tiled=True)  97.9 us
    reduce_scatter x1, waiting for transfers between devices, shards(): lax.psum_scatter(cross_grads[11], 'dp', scatter_dimension=0, tiled=True)  97.9 us
    reduce_scatter x1, waiting for transfers between devices, shards(): lax.psum_scatter(segment_grads[9], 'dp', scatter_dimension=0, tiled=True)  95.7 us
    all_gather x1, waiting for transfers between devices, shards(): lax.all_gather(inner_weight, 'dp', axis=1, tiled=True)  95.4 us
    all_gather x1, waiting for transfers between devices, shards(): lax.all_gather(outer_weight, 'dp', axis=1, tiled=True)  72.5 us
  transfers between devices with their start and end apart: 21, of which 20 were waited for; matrix products, arithmetic and copies ran while one was open for 9% of the time, Pallas kernels for 0%

commit v1 on v0

--- a/solution.py
+++ b/solution.py
@@ -1,7 +1,308 @@
+import functools
+
 import jax
 import jax.numpy as jnp
 from jax import lax
+from jax.experimental import pallas as pl
+from jax.experimental.pallas import tpu as pltpu
 from jax.sharding import PartitionSpec as P
+
+MESH = pl.DeviceIdType.MESH
+ANY = pl.BlockSpec(memory_space=pl.ANY)
+BF = jnp.bfloat16
+F32 = jnp.float32
+
+
+def place():
+    d = lax.axis_index("dp")
+    s = lax.axis_index("seg")
+    return d, s
+
+
+def greet(peers):
+    barrier = pltpu.get_barrier_semaphore()
+    for peer in peers:
+        pl.semaphore_signal(barrier, inc=1, device_id=peer, device_id_type=MESH)
+    pl.semaphore_wait(barrier, len(peers))
+
+
+def remote(src, dst, send, recv, peer):
+    return pltpu.make_async_remote_copy(
+        src_ref=src, dst_ref=dst, send_sem=send, recv_sem=recv, device_id=peer, device_id_type=MESH
+    )
+
+
+def plane_peers(d, s):
+    c = s % 2
+    x, y = d % 2, d // 2
+    dx = 2 * y + 1 - x
+    dy = 2 * (1 - y) + x
+    first = dx * (1 - c) + dy * c
+    second = dy * (1 - c) + dx * c
+    return c, first, second, s + 1 - 2 * c
+
+
+def gather_kernel(pieces, tensors, block, *refs):
+    n = tensors
+    shards, outs = refs[:n], refs[n : 2 * n]
+    bounce = refs[2 * n : 3 * n]
+    load_sem, store_sem, own_send, own_recv, fwd_send, fwd_recv, core_send, core_recv = refs[3 * n :]
+    d, s = place()
+    c, first, second, other = plane_peers(d, s)
+    diagonal = 3 - d
+    greet([(first, s), (second, s), (d, other)])
+
+    def cols(ref):
+        half = ref.shape[-1] // 2
+        return pl.ds(pl.multiple_of(c * half, half), half)
+
+    def mine(p):
+        i, r0, rn = pieces[p]
+        return shards[i].at[block, pl.ds(r0, rn), cols(shards[i])]
+
+    def slot(p, src):
+        i, r0, rn = pieces[p]
+        return outs[i].at[src, pl.ds(r0, rn), cols(outs[i])]
+
+    count = len(pieces)
+    owns = []
+    for p in range(count):
+        a = remote(mine(p), slot(p, d), own_send.at[0, p], own_recv.at[0, p], (first, s))
+        b = remote(mine(p), slot(p, d), own_send.at[1, p], own_recv.at[1, p], (second, s))
+        a.start()
+        b.start()
+        owns.append((a, b))
+    loads = []
+    for i in range(n):
+        cp = pltpu.make_async_copy(shards[i].at[block], bounce[i], load_sem.at[i])
+        cp.start()
+        loads.append(cp)
+    stores = []
+    for i in range(n):
+        loads[i].wait()
+        cp = pltpu.make_async_copy(bounce[i], outs[i].at[d], store_sem.at[i])
+        cp.start()
+        stores.append(cp)
+    fwds, cores = [], []
+
+    def share(p, src, k):
+        cp = remote(slot(p, src), slot(p, src), core_send.at[k, p], core_recv.at[k, p], (d, other))
+        cp.start()
+        cores.append(cp)
+
+    for p in range(count):
+        got = remote(slot(p, first), slot(p, first), own_send.at[0, p], own_recv.at[0, p], (first, s))
+        got.wait_recv()
+        f = remote(slot(p, first), slot(p, first), fwd_send.at[p], fwd_recv.at[p], (second, s))
+        f.start()
+        fwds.append(f)
+        share(p, first, 0)
+        got = remote(slot(p, second), slot(p, second), own_send.at[1, p], own_recv.at[1, p], (second, s))
+        got.wait_recv()
+        share(p, second, 1)
+        if p > 0:
+            fwd_wait(p - 1, slot, fwd_send, fwd_recv, diagonal, second, s)
+            share(p - 1, diagonal, 2)
+    fwd_wait(count - 1, slot, fwd_send, fwd_recv, diagonal, second, s)
+    share(count - 1, diagonal, 2)
+    for a, b in owns:
+        a.wait_send()
+        b.wait_send()
+    for f in fwds:
+        f.wait_send()
+    for cp in cores:
+        cp.wait()
+    for cp in stores:
+        cp.wait()
+
+
+def fwd_wait(p, slot, fwd_send, fwd_recv, diagonal, second, s):
+    remote(slot(p, diagonal), slot(p, diagonal), fwd_send.at[p], fwd_recv.at[p], (second, s)).wait_recv()
+
+
+def gather(shards, block, collective_id):
+    pieces = []
+    for i, w in enumerate(shards):
+        rows = w.shape[1]
+        parts = max(1, (rows * w.shape[2]) // (192 * 1536))
+        for p in range(parts):
+            pieces.append((i, p * rows // parts, rows // parts))
+    n, count = len(shards), len(pieces)
+    return pl.pallas_call(
+        functools.partial(gather_kernel, pieces, n, block),
+        out_shape=[jax.ShapeDtypeStruct((4,) + w.shape[1:], w.dtype) for w in shards],
+        in_specs=[ANY] * n,
+        out_specs=[ANY] * n,
+        scratch_shapes=[pltpu.VMEM(w.shape[1:], w.dtype) for w in shards]
+        + [
+            pltpu.SemaphoreType.DMA((n,)),
+            pltpu.SemaphoreType.DMA((n,)),
+            pltpu.SemaphoreType.DMA((2, count)),
+            pltpu.SemaphoreType.DMA((2, count)),
+            pltpu.SemaphoreType.DMA((count,)),
+            pltpu.SemaphoreType.DMA((count,)),
+            pltpu.SemaphoreType.DMA((3, count)),
+            pltpu.SemaphoreType.DMA((3, count)),
+        ],
+        compiler_params=pltpu.CompilerParams(collective_id=collective_id, has_side_effects=True),
+        name="gather_weights",
+    )(*shards)
+
+
+def add_into(dst, a, b, rows):
+    step = 48
+
+    def body(i, carry):
+        r = pl.ds(pl.multiple_of(i * step, 16), step)
+        dst[r, :] = (a[r, :].astype(F32) + b[r, :].astype(F32)).astype(dst.dtype)
+        return carry
+
+    lax.fori_loop(0, rows // step, body, 0)
+
+
+def reduce_kernel(nc, r, g, out, own, recv0, recv1, recv2, recv3, recv4, fin, load_sem, out_sem,
+                  send0, rcv0, send1, rcv1, send2, rcv2, send3, rcv3, send4, rcv4, send5, rcv5, send6, rcv6, send7, rcv7):
+    d, s = place()
+    c, first, second, other = plane_peers(d, s)
+    x, y = d % 2, d // 2
+    a = x * (1 - c) + y * c
+    b = y * (1 - c) + x * c
+    z = s // 2
+    z0, z1 = z % 2, z // 2
+    znear = (z + 1 - 2 * z0) * 2 + c
+    zfar = (z + 2 - 4 * z1) * 2 + c
+    h, q = r // 2, r // 4
+    greet([(first, s), (second, s), (d, other), (d, znear), (d, zfar)])
+
+    def quarter(aa, bb):
+        return aa * (1 + c) + bb * (2 - c)
+
+    def rows(core, k):
+        return pl.ds(pl.multiple_of(core * (nc * r) + k * r, 16), r)
+
+    started = []
+
+    def go(cp):
+        cp.start()
+        started.append(cp)
+
+    loads = []
+    for k in range(nc):
+        go(remote(g.at[:, rows(1 - c, k), :], recv0.at[k], send0.at[k], rcv0.at[k], (d, other)))
+        cp = pltpu.make_async_copy(g.at[:, rows(c, k), :], own.at[k], load_sem.at[k])
+        cp.start()
+        loads.append(cp)
+
+    def arrived(ref, sem):
+        pltpu.make_async_copy(ref, ref, sem).wait()
+
+    def piece(k, i0, i1):
+        return fin.at[c, k, pl.ds(pl.multiple_of(i0 * h + i1 * q, 16), q), :]
+
+    outs = []
+
+    def stage(t, k):
+        if t == 1:
+            arrived(recv0.at[k], rcv0.at[k])
+            loads[k].wait()
+            for bb in range(2):
+                away = quarter(1 - a, bb)
+                add_into(own.at[k, away], own.at[k, away], recv0.at[k, away], r)
+                go(remote(own.at[k, away], recv1.at[k, bb], send1.at[k, bb], rcv1.at[k, bb], (first, s)))
+            for bb in range(2):
+                keep = quarter(a, bb)
+                add_into(own.at[k, keep], own.at[k, keep], recv0.at[k, keep], r)
+        elif t == 2:
+            for bb in range(2):
+                arrived(recv1.at[k, bb], rcv1.at[k, bb])
+            away, keep = quarter(a, 1 - b), quarter(a, b)
+            add_into(own.at[k, away], own.at[k, away], recv1.at[k, 1 - b], r)
+            go(remote(own.at[k, away], recv2.at[k], send2.at[k], rcv2.at[k], (second, s)))
+            add_into(own.at[k, keep], own.at[k, keep], recv1.at[k, b], r)
+        elif t == 3:
+            arrived(recv2.at[k], rcv2.at[k])
+            keep = quarter(a, b)
+            away = pl.ds(pl.multiple_of((1 - z0) * h, 16), h)
+            mine = pl.ds(pl.multiple_of(z0 * h, 16), h)
+            add_into(own.at[k, keep, away], own.at[k, keep, away], recv2.at[k, away], h)
+            go(remote(own.at[k, keep, away], recv3.at[k], send3.at[k], rcv3.at[k], (d, znear)))
+            add_into(own.at[k, keep, mine], own.at[k, keep, mine], recv2.at[k, mine], h)
+        elif t == 4:
+            arrived(recv3.at[k], rcv3.at[k])
+            keep = quarter(a, b)
+            away = pl.ds(pl.multiple_of(z0 * h + (1 - z1) * q, 16), q)
+            mine = pl.ds(pl.multiple_of(z0 * h + z1 * q, 16), q)
+            raway = pl.ds(pl.multiple_of((1 - z1) * q, 16), q)
+            rmine = pl.ds(pl.multiple_of(z1 * q, 16), q)
+            add_into(own.at[k, keep, away], own.at[k, keep, away], recv3.at[k, raway], q)
+            go(remote(own.at[k, keep, away], recv4.at[k], send4.at[k], rcv4.at[k], (d, zfar)))
+            add_into(own.at[k, keep, mine], own.at[k, keep, mine], recv3.at[k, rmine], q)
+        elif t == 5:
+            arrived(recv4.at[k], rcv4.at[k])
+            keep = quarter(a, b)
+            mine = pl.ds(pl.multiple_of(z0 * h + z1 * q, 16), q)
+            add_into(piece(k, z0, z1), own.at[k, keep, mine], recv4.at[k], q)
+            go(remote(piece(k, z0, z1), piece(k, z0, z1), send5.at[k], rcv5.at[k], (d, zfar)))
+        elif t == 6:
+            arrived(piece(k, z0, 1 - z1), rcv5.at[k])
+            half = fin.at[c, k, pl.ds(pl.multiple_of(z0 * h, 16), h), :]
+            go(remote(half, half, send6.at[k], rcv6.at[k], (d, znear)))
+        elif t == 7:
+            half = fin.at[c, k, pl.ds(pl.multiple_of((1 - z0) * h, 16), h), :]
+            arrived(half, rcv6.at[k])
+            go(remote(fin.at[c, k], fin.at[c, k], send7.at[k], rcv7.at[k], (d, other)))
+            cp = pltpu.make_async_copy(fin.at[c, k], out.at[rows(c, k), :], out_sem.at[0, k])
+            cp.start()
+            outs.append(cp)
+        elif t == 8:
+            arrived(fin.at[1 - c, k], rcv7.at[k])
+            cp = pltpu.make_async_copy(fin.at[1 - c, k], out.at[rows(1 - c, k), :], out_sem.at[1, k])
+            cp.start()
+            outs.append(cp)
+
+    for slot in range(nc + 8):
+        for t in range(8, 0, -1):
+            k = slot - (t - 1)
+            if 0 <= k < nc:
+                stage(t, k)
+    for cp in started:
+        cp.wait_send()
+    for cp in outs:
+        cp.wait()
+
+
+def reduce(g, nc, collective_id):
+    _, total, width = g.shape
+    r = total // 2 // nc
+    dma = pltpu.SemaphoreType.DMA
+    return pl.pallas_call(
+        functools.partial(reduce_kernel, nc, r),
+        out_shape=jax.ShapeDtypeStruct((total, width), g.dtype),
+        in_specs=[ANY],
+        out_specs=ANY,
+        scratch_shapes=[
+            pltpu.VMEM((nc, 4, r, width), g.dtype),
+            pltpu.VMEM((nc, 4, r, width), g.dtype),
+            pltpu.VMEM((nc, 2, r, width), g.dtype),
+            pltpu.VMEM((nc, r, width), g.dtype),
+            pltpu.VMEM((nc, r // 2, width), g.dtype),
+            pltpu.VMEM((nc, r // 4, width), g.dtype),
+            pltpu.VMEM((2, nc, r, width), g.dtype),
+            dma((nc,)),
+            dma((2, nc)),
+            dma((nc,)), dma((nc,)),
+            dma((nc, 2)), dma((nc, 2)),
+            dma((nc,)), dma((nc,)),
+            dma((nc,)), dma((nc,)),
+            dma((nc,)), dma((nc,)),
+            dma((nc,)), dma((nc,)),
+            dma((nc,)), dma((nc,)),
+            dma((nc,)), dma((nc,)),
+        ],
+        compiler_params=pltpu.CompilerParams(collective_id=collective_id, has_side_effects=True, vmem_limit_bytes=60 << 20),
+        name="reduce_grads",
+    )(g)
+
 
 HEADS = 12
 HEAD_DIM = 64
@@ -374,6 +675,132 @@
     return (output, input_grad) + tuple(totals)
 
 
+def square_shards(
+    inputs,
+    doc_ids,
+    cotangent,
+    query_weight,
+    query_bias,
+    key_weight,
+    value_weight,
+    value_bias,
+    out_weight,
+    out_bias,
+    first_gain,
+    first_shift,
+    inner_weight,
+    inner_bias,
+    outer_weight,
+    outer_bias,
+    second_gain,
+    second_shift,
+    segment_embed,
+):
+    seg_count = lax.axis_size("seg")
+    seg_index = lax.axis_index("seg")
+    group_rows, local_length, width = inputs.shape
+    seg_local = local_length // SEG_LEN
+    weights = (query_weight, key_weight, value_weight, out_weight, inner_weight, outer_weight)
+    first_full = gather(weights, 0, 1)
+    cross_full = gather(weights, 1, 2)
+    query_full, key_full, value_full, out_full, inner_full, outer_full = (
+        (one.reshape(-1, one.shape[-1]), two.reshape(-1, two.shape[-1]))
+        for one, two in zip(first_full, cross_full)
+    )
+    stacked = (
+        query_full,
+        query_bias,
+        key_full,
+        value_full,
+        value_bias,
+        out_full,
+        out_bias,
+        first_gain,
+        first_shift,
+        inner_full,
+        inner_bias,
+        outer_full,
+        outer_bias,
+        second_gain,
+        second_shift,
+    )
+    first_params = tuple((weight[0] for weight in stacked))
+    cross_params = tuple((weight[1] for weight in stacked))
+    pieces = inputs.reshape(group_rows * seg_local, SEG_LEN, width)
+    segment_out, segment_stored = forward_layer(first_params, pieces, None, keep_pair)
+    segment_grid = segment_out.reshape(group_rows, seg_local, SEG_LEN, width)
+    position = lax.dynamic_slice_in_dim(segment_embed, seg_index * seg_local, seg_local, 0).astype(
+        jnp.float32
+    )
+    heads_in = (segment_grid[:, :, 0, :] + position).astype(jnp.bfloat16)
+    row_input = lax.all_gather(heads_in, "seg", axis=1, tiled=True)
+    allowed = doc_ids[:, :, None] == doc_ids[:, None, :]
+    cross_out, cross_stored = forward_layer(cross_params, row_input, allowed, keep_pair)
+    returned = lax.dynamic_slice_in_dim(cross_out, seg_index * seg_local, seg_local, 1).astype(
+        jnp.bfloat16
+    )
+    output = jnp.concatenate(
+        [returned[:, :, None, :], segment_grid[:, :, 1:, :].astype(jnp.bfloat16)], axis=2
+    )
+    output = output.reshape(group_rows, local_length, width)
+    cot_grid = cotangent.reshape(group_rows, seg_local, SEG_LEN, width)
+    cot_heads = cot_grid[:, :, 0, :]
+    grad_cross = lax.all_gather(cot_heads, "seg", axis=1, tiled=True)
+    grad_row_input, cross_grads = backward_layer(
+        cross_params, cross_stored, grad_cross.astype(jnp.float32), keep_pair
+    )
+    grad_row_low = grad_row_input.astype(jnp.bfloat16)
+    factor = 1.0 / seg_count
+    embed_grad = jnp.sum(grad_row_low.astype(jnp.float32), axis=0) * factor
+    cross_grads = tuple((part * factor for part in cross_grads))
+    grad_heads = lax.dynamic_slice_in_dim(grad_row_low, seg_index * seg_local, seg_local, 1)
+    grad_grid = jnp.concatenate(
+        [grad_heads[:, :, None, :].astype(jnp.float32), cot_grid[:, :, 1:, :].astype(jnp.float32)],
+        axis=2,
+    )
+    grad_grid = grad_grid.reshape(group_rows * seg_local, SEG_LEN, width)
+    grad_pieces, segment_grads = backward_layer(first_params, segment_stored, grad_grid, keep_pair)
+    input_grad = grad_pieces.astype(jnp.bfloat16).reshape(group_rows, local_length, width)
+    matrices = (0, 2, 3, 5, 9, 11)
+    own = lax.axis_index("dp")
+    summed = {}
+    for block, grads in ((0, segment_grads), (1, cross_grads)):
+        packed = []
+        for i in matrices:
+            part = grads[i].reshape(4, -1, grads[i].shape[-1])
+            if part.shape[2] != width:
+                part = part.reshape(4, part.shape[1], -1, width).transpose(0, 2, 1, 3)
+                part = part.reshape(4, -1, width)
+            packed.append(part.astype(jnp.bfloat16))
+        total = reduce(jnp.concatenate(packed, axis=1), 6, 3 + block).astype(jnp.float32)
+        at = 0
+        for i, part in zip(matrices, packed):
+            rows = part.shape[1]
+            piece = total[at : at + rows]
+            at += rows
+            if grads[i].shape[1] != width:
+                piece = piece.reshape(-1, grads[i].shape[0] // 4, width).transpose(1, 0, 2)
+                piece = piece.reshape(grads[i].shape[0] // 4, -1)
+            summed[i, block] = piece
+    vectors = [i for i in range(15) if i not in matrices]
+    flat = jnp.concatenate(
+        [grads[i] for grads in (segment_grads, cross_grads) for i in vectors]
+        + [embed_grad.reshape(-1)]
+    )
+    flat = lax.psum(flat, ("dp", "seg"))
+    at = 0
+    for block in range(2):
+        for i in vectors:
+            size = segment_grads[i].shape[0]
+            share = size // 4
+            summed[i, block] = lax.dynamic_slice_in_dim(flat, at + own * share, share, 0)
+            at += size
+    embed = lax.dynamic_slice_in_dim(flat[at:].reshape(embed_grad.shape), own * (width // 4), width // 4, 1)
+    totals = tuple((jnp.stack([summed[index, 0], summed[index, 1]]) for index in range(15)))
+    totals = totals + (embed,)
+    return (output, input_grad) + tuple(totals)
+
+
 def solution(mesh):
     placed = (
         P("dp", "seg", None),
@@ -396,8 +823,9 @@
         P(),
         P(),
     )
+    square = mesh.shape["dp"] == 4 and mesh.shape["seg"] == 8
     return jax.shard_map(
-        shards,
+        square_shards if square else shards,
         mesh=mesh,
         in_specs=placed,
         out_specs=(

time: 1630 us -> 661 us (0.41)
  waiting for transfers between devices: 1260 us -> 0.02 us
  Pallas kernels: 0 us -> 341 us
  blocking collectives: 57.1 us -> 28.3 us
  matrix products: 130 us -> 108 us
    reduce_scatter x4 -> x0, waiting for transfers between devices: 389 us -> none  [the longest x1 97.9 us: shards(): lax.psum_scatter(segment_grads[11], 'dp', scatter_dimension=0, tiled=True)]
    pallas_call x0 -> x4, Pallas kernels: none -> 341 us  [the longest x2 209 us: reduce(): pl.pallas_call(functools.partial(reduce_kernel, nc, r), out_shape=jax.Sha...]
    unnamed x31 -> x1, waiting for transfers between devices: 294 us -> 0.02 us
    all_gather x6 -> x0, waiting for transfers between devices: 289 us -> none  [the longest x1 95.4 us: shards(): lax.all_gather(inner_weight, 'dp', axis=1, tiled=True)]
    psum x1, waiting for transfers between devices: 286 us -> 0.01 us  [square_shards(): flat = lax.psum(flat, ('dp', 'seg'))]
    unnamed x261 -> x298, local copies, waits for them, and re-layouts: 68.5 us -> 26.5 us
    psum x1 -> x0, blocking collectives: 26.9 us -> none  [shards(): lax.psum((shares[0], shares[1], shares[2], shares[3], shares[4], shares[5...]
    convert_element_type x3 -> x4, local copies, waits for them, and re-layouts: 1.89 us -> 25.9 us  [square_shards(): packed.append(part.astype(jnp.bfloat16))]
  transfers between devices with their start and end apart: 21 -> 1, of which waited for: 20 -> 0; matrix products, arithmetic and copies ran while one was open for 9% -> 20% of each run, Pallas kernels for 0% -> 32%
where the time goes in v1:
time: 661 us; the launch traced here: 651 us
  Pallas kernels  341 us (52%)
  matrix products  108 us (16%)
  local copies, waits for them, and re-layouts  92.9 us (14%)
  other arithmetic  64.6 us (10%)
  blocking collectives  28.3 us (4%)
  between operations  16.2 us (2%)
    pallas_call x2, Pallas kernels, reduce(): pl.pallas_call(functools.partial(reduce_kernel, nc, r), out_shape=jax.Sha...  209 us
    pallas_call x2, Pallas kernels, gather(): pl.pallas_call(functools.partial(gather_kernel, pieces, n, block), out_sh...  132 us
    dot_general x12, matrix products, back_project(): jnp.einsum('gne,de->gnd', values, weight, preferred_element_type=jnp.floa...  30.6 us
    dot_general x12, matrix products, project(): jnp.einsum('gnd,de->gne', values, weight, preferred_element_type=jnp.floa...  29.1 us
    dot_general x12, matrix products, weight_grad(): jnp.einsum('gnd,gne->de', source, grads, preferred_element_type=jnp.float32)  26.6 us
    unnamed x298, local copies, waits for them, and re-layouts  26.5 us
    convert_element_type x4, local copies, waits for them, and re-layouts, square_shards(): packed.append(part.astype(jnp.bfloat16))  25.9 us
    another operation x15, other arithmetic, square_shards(): jnp.stack([summed[index, 0], summed[index, 1]])  19.1 us
  transfers between devices with their start and end apart: 1, of which 0 were waited for; matrix products, arithmetic and copies ran while one was open for 20% of the time, Pallas kernels for 32%

profile of v1, /device:TPU:1, one launch (start us, length us, event | category | flops | bytes accessed | tf_op | source)
XLA Modules:
  0.0 651.0 jit_solution(10125546384473014935)
XLA Ops:
  7.2 67.1 %gather_weights.2 = (bf16[4,192,768]{2,1,0:T(8,128)(2,1)}, bf16[4,192,768]{2,1,0:T(8,128)(2,1)}, bf16[4,192,768]{2,1,0:T(8,128)(2,1)}, bf16[4,192,768]{2,1,0:T(8...) custom-call(bf16[2,192,768]{2,1,0:T(8,128)(2,1)} %refs_0_.3, bf16[2,192,768]{2,1,0:T(8,128)(2,1)} %refs_1_.3, ...), custom_call_target="tpu_custom_call" | custom-call | tf_op jit(solution)/shard_map/gather_weights/pallas_call | solution.py:131
  74.4 65.3 %gather_weights.3 = (bf16[4,192,768]{2,1,0:T(8,128)(2,1)}, bf16[4,192,768]{2,1,0:T(8,128)(2,1)}, bf16[4,192,768]{2,1,0:T(8,128)(2,1)}, bf16[4,192,768]{2,1,0:T(8...) custom-call(bf16[2,192,768]{2,1,0:T(8,128)(2,1)} %refs_0_.3, bf16[2,192,768]{2,1,0:T(8,128)(2,1)} %refs_1_.3, ...), custom_call_target="tpu_custom_call" | custom-call | tf_op jit(solution)/shard_map/gather_weights/pallas_call | solution.py:131
  143.4 2.6 fusion.96
  146.1 3.5 add_convert_fusion.2
  153.4 4.6 fusion.24
  158.0 15.5 %multiply_convert_fusion.2 = (bf16[4,128,3072]{2,1,0:T(8,128)(2,1)S(1)}, f32[4,128,3072]{2,1,0:T(8,128)}) fusion(f32[4,128,3072]{2,1,0:T(8,128)S(1)} %get-tuple-element.130, f32[3072]{0:T(1024)S(1)} %bitcast.362, u8[128,3072]{1,0:T(8,128)(4,1)S(1)} %get-tuple-element.43, u8[128,3072]{1,0:T(8,128)(4,1)S(1)} %get-tuple-element.42), kind=kLoop, calls=%fused_computation.23 | loop fusion | flops 111673344 | bytes 16527360 | tf_op jit(solution)/shard_map/convert_element_type | solution.py:396
  173.6 2.8 fusion.98
  180.8 14.2 %all-gather.2 = bf16[8,4,768]{2,1,0:T(4,128)(2,1)S(1)} all-gather(bf16[1,4,768]{2,1,0:T(4,128)(2,1)S(1)} %fusion.81), channel_id=2, replica_groups=mesh['dp'=4,'seg'=8] {'seg'}, dimensions={0}, use_global_device_ids=true | all-gather | bytes 55296 | tf_op jit(solution)/shard_map/all_gather | solution.py:736
  205.8 3.4 convolution_add_fusion
  209.3 3.9 convolution_add_fusion.1
  214.9 14.1 %all-gather.1 = bf16[1,32,1,768]{3,2,0,1:T(2,128)(2,1)S(1)} all-gather(bf16[1,4,1,768]{3,2,0,1:T(2,128)(2,1)S(1)} %slice_bitcast_fusion.10), channel_id=3, replica_groups=mesh['dp'=4,'seg'=8] {'seg'}, dimensions={1}, use_global_device_ids=true | all-gather | bytes 55296 | tf_op jit(solution)/shard_map/all_gather | solution.py:748
  232.0 2.4 convert_reduce_fusion.5
  248.0 2.4 fusion.106
  252.2 2.4 fusion.107
  256.3 1.9 fusion.108
  262.4 9.7 %convert_reduce_fusion = (f32[3072]{0:T(1024)S(1)}, bf16[4,128,3072]{2,1,0:T(8,128)(2,1)S(1)}) fusion(f32[4,128,3072]{2,1,0:T(8,128)} %get-tuple-element.97, bf16[4,128,768]{2,1,0:T(8,128)(2,1)S(1)} %get-tuple-element.77, bf16[3072,768,1]{1,0,2:T(8,128)(2,1)} %bitcast.388, f32[4,128,3072]{2,1,0:T(8,128)} %copy-done.7, f32[3072]{0:T(1024)S(1)} %bitcast.363), kind=kOutput, calls=%fused_computation.22 | convolution fusion | flops 2445800448 | bytes 21258240 | tf_op jit(solution)/shard_map/gne,de->gnd/dot_general | solution.py:330
  272.2 3.1 multiply_reduce_fusion.2
  279.5 4.1 convert_reduce_fusion.3
  283.6 2.0 fusion.16
  286.8 3.1 fusion.18
  292.7 3.3 multiply_convert_fusion.7
  296.1 4.8 bitcast_convert_fusion.1
  300.9 4.5 bitcast_convert_fusion
  310.5 3.6 multiply_convert_fusion.1
  314.1 4.3 multiply_convert_fusion
  322.1 9.7 %convert_element_type.680 = bf16[4,192,4,768]{3,2,1,0:T(4,128)(2,1)} reshape(bf16[768,3072]{1,0:T(8,128)(2,1)} %bitcast_convert_fusion.1) | data formatting | bytes 9437184 | tf_op jit(solution)/shard_map/convert_element_type | solution.py:774
  331.8 3.2 copy.150
  339.1 2.4 constant_dynamic-update-slice_fusion.1
  341.6 2.5 constant_dynamic-update-slice_fusion.g
  344.1 105.7 %reduce_grads.2 = bf16[2304,768]{1,0:T(8,128)(2,1)} custom-call(bf16[4,2304,768]{2,1,0:T(8,128)(2,1)} %constant_dynamic-update-slice_fusion.g), custom_call_target="tpu_custom_call" | custom-call | tf_op jit(solution)/shard_map/reduce_grads/pallas_call | solution.py:278
  449.8 5.5 convert_element_type.685
  457.7 9.7 %convert_element_type.695 = bf16[4,192,4,768]{3,2,1,0:T(4,128)(2,1)} reshape(bf16[768,3072]{1,0:T(8,128)(2,1)} %multiply_convert_fusion.1) | data formatting | bytes 9437184 | tf_op jit(solution)/shard_map/convert_element_type | solution.py:774
  467.5 3.2 copy.152
  474.6 2.4 constant_dynamic-update-slice_fusion.6
  477.3 2.5 constant_dynamic-update-slice_fusion.5.g
  479.8 103.2 %reduce_grads.3 = bf16[2304,768]{1,0:T(8,128)(2,1)} custom-call(bf16[4,2304,768]{2,1,0:T(8,128)(2,1)} %constant_dynamic-update-slice_fusion.5.g), custom_call_target="tpu_custom_call" | custom-call | tf_op jit(solution)/shard_map/reduce_grads/pallas_call | solution.py:278
  583.0 2.7 convert_element_type.700
  587.7 3.2 slice_bitcast_fusion.1
  590.9 3.0 slice_bitcast_fusion.3
  597.9 2.0 fusion.109
  599.8 2.0 fusion.110
  602.0 2.9 copy.153
  604.9 3.9 stack_reshape.6
  608.8 2.9 copy.154
  611.8 3.9 stack_reshape.7
  615.7 4.2 pad_maximum_fusion.1
  619.8 5.2 pad_maximum_fusion
  631.2 1.9 add_convert_fusion
  (440 shorter events, 97.8 us)
Async XLA Ops:
  7.2 627.8 %all-reduce.2.cloned.1.call-start = ((), (), s32[]{:S(2)}) async-start(), calls=%async_computation | async-start | bytes 344064 | tf_op jit(solution)/shard_map/psum | solution.py:790
  74.4 65.4 %copy-start.99 = (bf16[2,768]{1,0:T(2,128)(2,1)S(1)}, bf16[2,768]{1,0:T(2,128)(2,1)}, u32[]{:S(2)}) copy-start(bf16[2,768]{1,0:T(2,128)(2,1)} %param.23) | copy-start | bytes 9220
  74.4 65.4 %copy-start.100 = (bf16[2,768]{1,0:T(2,128)(2,1)S(1)}, bf16[2,768]{1,0:T(2,128)(2,1)}, u32[]{:S(2)}) copy-start(bf16[2,768]{1,0:T(2,128)(2,1)} %param.26) | copy-start | bytes 9220
  74.4 65.4 %copy-start.101 = (bf16[2,768]{1,0:T(2,128)(2,1)S(1)}, bf16[2,768]{1,0:T(2,128)(2,1)}, u32[]{:S(2)}) copy-start(bf16[2,768]{1,0:T(2,128)(2,1)} %param.28) | copy-start | bytes 9220
  74.4 65.5 %copy-start.37 = (bf16[1,512,768]{2,1,0:T(8,128)(2,1)S(1)}, bf16[1,512,768]{2,1,0:T(8,128)(2,1)}, u32[]{:S(2)}) copy-start(bf16[1,512,768]{2,1,0:T(8,128)(2,1)} %param.19) | copy-start | bytes 2359300
  74.4 65.5 %copy-start.117 = (bf16[4,192,768]{2,1,0:T(8,128)(2,1)S(1)}, bf16[4,192,768]{2,1,0:T(8,128)(2,1)}, u32[]{:S(2)}) copy-start(bf16[4,192,768]{2,1,0:T(8,128)(2,1)} %get-tuple-element.32) | copy-start | bytes 3538948
  146.0 7.4 %slice-start.6 = ((s8[4718592]{0:T(1024)(128)(4,1)}), s8[4194304]{0:T(1024)(128)(4,1)S(1)}, s32[]{:S(2)}) async-start(s8[4718592]{0:T(1024)(128)(4,1)} %bitcast.382), calls=%async_computation.7 | async-start | bytes 8388608
  152.3 21.2 %copy-start.85 = (f32[4,128]{1,0:T(4,128)}, f32[4,128]{1,0:T(4,128)S(1)}, u32[]{:S(2)}) copy-start(f32[4,128]{1,0:T(4,128)S(1)} %broadcast_multiply_fusion.4) | copy-start | bytes 6148
  152.3 21.2 %slice-start.10 = ((s8[4718592]{0:T(1024)(128)(4,1)}), s8[4194304]{0:T(1024)(128)(4,1)S(1)}, s32[]{:S(2)}) async-start(s8[4718592]{0:T(1024)(128)(4,1)} %bitcast.389), calls=%async_computation.11 | async-start | bytes 8388608
  153.2 20.3 %copy-start.110 = (f32[4,128]{1,0:T(4,128)}, f32[4,128]{1,0:T(4,128)S(1)}, u32[]{:S(2)}) copy-start(f32[4,128]{1,0:T(4,128)S(1)} %fusion.83) | copy-start | bytes 6148
  153.3 20.3 %copy-start.97 = (f32[768]{0:T(1024)}, f32[768]{0:T(1024)S(1)}, u32[]{:S(2)}) copy-start(f32[768]{0:T(1024)S(1)} %get-tuple-element.61) | copy-start | bytes 9220
  153.3 4.7 copy-start.78
  153.4 20.2 %copy-start.112 = (f32[768]{0:T(1024)}, f32[768]{0:T(1024)S(1)}, u32[]{:S(2)}) copy-start(f32[768]{0:T(1024)S(1)} %get-tuple-element.154) | copy-start | bytes 9220
  153.4 20.2 %slice-start.11 = ((s8[4718592]{0:T(1024)(128)(4,1)}), s8[524288]{0:T(1024)(128)(4,1)S(1)}, s32[]{:S(2)}) async-start(s8[4718592]{0:T(1024)(128)(4,1)} %bitcast.389), calls=%async_computation.12 | async-start | bytes 1048576
  158.0 15.5 %copy-start.7 = (f32[4,128,3072]{2,1,0:T(8,128)}, f32[4,128,3072]{2,1,0:T(8,128)S(1)}, u32[]{:S(2)}) copy-start(f32[4,128,3072]{2,1,0:T(8,128)S(1)} %get-tuple-element.130) | copy-start | bytes 18874372
  178.0 52.7 %copy-start.74 = (f32[768]{0:T(1024)}, f32[768]{0:T(1024)S(1)}, u32[]{:S(2)}) copy-start(f32[768]{0:T(1024)S(1)} %get-tuple-element.157) | copy-start | bytes 9220
  180.0 18.5 %copy-start.114 = (s32[1,32]{1,0:T(1,128)S(1)}, s32[1,32]{1,0:T(1,128)}, u32[]{:S(2)}) copy-start(s32[1,32]{1,0:T(1,128)} %param.20) | copy-start | bytes 388
  195.0 8.3 %copy-start.16 = (bf16[32,768]{1,0:T(8,128)(2,1)}, bf16[32,768]{1,0:T(8,128)(2,1)S(1)}, u32[]{:S(2)}) copy-start(bf16[32,768]{1,0:T(8,128)(2,1)S(1)} %reshape.868) | copy-start | bytes 147460
  203.3 5.9 copy-start.54
  205.8 26.2 %slice-start.12 = ((s8[4718592]{0:T(1024)(128)(4,1)}), s8[4194304]{0:T(1024)(128)(4,1)S(1)}, s32[]{:S(2)}) async-start(s8[4718592]{0:T(1024)(128)(4,1)} %bitcast.393), calls=%async_computation.13 | async-start | bytes 8388608
  209.3 22.8 %copy-start.65 = (f32[32,3072]{1,0:T(8,128)}, f32[32,3072]{1,0:T(8,128)S(1)}, u32[]{:S(2)}) copy-start(f32[32,3072]{1,0:T(8,128)S(1)} %convolution_add_fusion) | copy-start | bytes 1179652
  209.3 22.7 %slice-start.13 = ((s8[4718592]{0:T(1024)(128)(4,1)}), s8[524288]{0:T(1024)(128)(4,1)S(1)}, s32[]{:S(2)}) async-start(s8[4718592]{0:T(1024)(128)(4,1)} %bitcast.393), calls=%async_computation.14 | async-start | bytes 1048576
  209.3 25.1 %slice-start = ((s8[4718592]{0:T(1024)(128)(4,1)}), s8[4194304]{0:T(1024)(128)(4,1)S(1)}, s32[]{:S(2)}) async-start(s8[4718592]{0:T(1024)(128)(4,1)} %bitcast.302), calls=%async_computation.1 | async-start | bytes 8388608
  234.4 4.7 copy-start.8
  235.9 4.6 copy-start.109
  240.5 6.1 copy-start.14
  248.0 10.2 %copy-start.56 = (bf16[32,768]{1,0:T(8,128)(2,1)}, bf16[32,768]{1,0:T(8,128)(2,1)S(1)}, u32[]{:S(2)}) copy-start(bf16[32,768]{1,0:T(8,128)(2,1)S(1)} %reshape.835) | copy-start | bytes 147460
  248.0 10.2 %copy-start.116 = (f32[32]{0:T(128)S(1)}, f32[32]{0:T(128)}, u32[]{:S(2)}) copy-start(f32[32]{0:T(128)} %copy-done.115) | copy-start | bytes 388
  250.4 9.6 %copy-start.73 = (f32[768]{0:T(1024)S(1)}, f32[768]{0:T(1024)}, u32[]{:S(2)}) copy-start(f32[768]{0:T(1024)} %copy-done.72) | copy-start | bytes 9220
  250.4 9.6 %copy-start.77 = (f32[4,128]{1,0:T(4,128)S(1)}, f32[4,128]{1,0:T(4,128)}, u32[]{:S(2)}) copy-start(f32[4,128]{1,0:T(4,128)} %copy-done.76) | copy-start | bytes 6148
  250.4 9.7 %copy-start.84 = (f32[4,128]{1,0:T(4,128)S(1)}, f32[4,128]{1,0:T(4,128)}, u32[]{:S(2)}) copy-start(f32[4,128]{1,0:T(4,128)} %copy-done.83) | copy-start | bytes 6148
  256.3 4.7 copy-start.90
  261.7 10.4 %slice-start.8 = ((s8[4718592]{0:T(1024)(128)(4,1)}), s8[4194304]{0:T(1024)(128)(4,1)S(1)}, s32[]{:S(2)}) async-start(s8[4718592]{0:T(1024)(128)(4,1)} %bitcast.385), calls=%async_computation.9 | async-start | bytes 8388608
  261.9 10.2 %copy-start.48 = (bf16[4,128,768]{2,1,0:T(8,128)(2,1)}, bf16[4,128,768]{2,1,0:T(8,128)(2,1)S(1)}, u32[]{:S(2)}) copy-start(bf16[4,128,768]{2,1,0:T(8,128)(2,1)S(1)} %get-tuple-element.77) | copy-start | bytes 2359300
  262.4 9.7 %copy-start.86 = (f32[4,128]{1,0:T(4,128)S(1)}, f32[4,128]{1,0:T(4,128)}, u32[]{:S(2)}) copy-start(f32[4,128]{1,0:T(4,128)} %copy-done.85) | copy-start | bytes 6148
  262.4 9.7 %copy-start.98 = (f32[768]{0:T(1024)S(1)}, f32[768]{0:T(1024)}, u32[]{:S(2)}) copy-start(f32[768]{0:T(1024)} %copy-done.97) | copy-start | bytes 9220
  262.4 9.7 %copy-start.111 = (f32[4,128]{1,0:T(4,128)S(1)}, f32[4,128]{1,0:T(4,128)}, u32[]{:S(2)}) copy-start(f32[4,128]{1,0:T(4,128)} %copy-done.110) | copy-start | bytes 6148
  262.4 9.7 %slice-start.9 = ((s8[4718592]{0:T(1024)(128)(4,1)}), s8[524288]{0:T(1024)(128)(4,1)S(1)}, s32[]{:S(2)}) async-start(s8[4718592]{0:T(1024)(128)(4,1)} %bitcast.385), calls=%async_computation.10 | async-start | bytes 1048576
  291.5 4.6 copy-start.113
  296.1 4.8 copy-start.19
  296.1 4.8 copy-start.49
  300.9 5.1 copy-start.57
  305.4 5.1 copy-start.36
  305.4 5.0 copy-start.62
  449.8 5.5 copy-start
  619.8 5.2 copy-start.26
  619.8 5.2 copy-start.29
  619.8 10.3 %copy-start.53 = (bf16[4,12,64,128]{3,2,1,0:T(8,128)(2,1)S(1)}, bf16[4,12,64,128]{3,2,1,0:T(8,128)(2,1)}, u32[]{:S(2)}) copy-start(bf16[4,12,64,128]{3,2,1,0:T(8,128)(2,1)} %get-tuple-element.145) | copy-start | bytes 2359300
  (92 other events, 222.6 us)
Sparse Core Ops, SparseCore 0:
  292.8 125.6 all-reduce.1

commit v2 on v0

--- a/solution.py
+++ b/solution.py
@@ -1,6 +1,10 @@
+import functools
+
 import jax
 import jax.numpy as jnp
 from jax import lax
+from jax.experimental import pallas as pl
+from jax.experimental.pallas import tpu as pltpu
 from jax.sharding import PartitionSpec as P
 
 HEADS = 12
@@ -374,6 +378,1039 @@
     return (output, input_grad) + tuple(totals)
 
 
+MESH = pl.DeviceIdType.MESH
+ANY = pl.BlockSpec(memory_space=pl.ANY)
+BF = jnp.bfloat16
+F32 = jnp.float32
+
+
+def place():
+    d = lax.axis_index("dp")
+    s = lax.axis_index("seg")
+    return d, s
+
+
+def greet(peers):
+    barrier = pltpu.get_barrier_semaphore()
+    for peer in peers:
+        pl.semaphore_signal(barrier, inc=1, device_id=peer, device_id_type=MESH)
+    pl.semaphore_wait(barrier, len(peers))
+
+
+def remote(src, dst, send, recv, peer):
+    return pltpu.make_async_remote_copy(
+        src_ref=src, dst_ref=dst, send_sem=send, recv_sem=recv, device_id=peer, device_id_type=MESH
+    )
+
+
+def plane_peers(d, s):
+    c = s % 2
+    x, y = d % 2, d // 2
+    dx = 2 * y + 1 - x
+    dy = 2 * (1 - y) + x
+    first = dx * (1 - c) + dy * c
+    second = dy * (1 - c) + dx * c
+    return c, first, second, s + 1 - 2 * c
+
+
+def window(d):
+    return pl.multiple_of((3 * d) // 2 * 128, 128), d % 2 * 64
+
+
+def everyone(d, s):
+    me = d * 8 + s
+    ahead = [lax.rem(me + j, 32) for j in range(1, 32)]
+    behind = [lax.rem(me + 32 - j, 32) for j in range(1, 32)]
+    return me, ahead, behind
+
+
+def gather_kernel(pieces, tensors, block, *refs):
+    n = tensors
+    shards, (cot, docs), refs = refs[:n], refs[n : n + 2], refs[n + 2 :]
+    outs, wins, (cot_all, docs_all), refs = refs[:n], refs[n : n + 4], refs[n + 4 : n + 6], refs[n + 6 :]
+    bounce, wbounce, (first_rows, heads, ids), refs = refs[:n], refs[n : n + 4], refs[n + 4 : n + 7], refs[n + 7 :]
+    load_sem, store_sem, own_send, own_recv, fwd_send, fwd_recv, core_send, core_recv = refs[:8]
+    wload_sem, wstore_sem, win_send, win_recv, wcore_send, wcore_recv, row_sem, all_send, all_recv, ids_send, ids_recv = refs[8:]
+    d, s = place()
+    c, first, second, other = plane_peers(d, s)
+    diagonal = 3 - d
+    me, ahead, behind = everyone(d, s)
+    segs = first_rows.shape[0]
+    row_loads = [pltpu.make_async_copy(cot.at[0, pl.ds(i * 128, 8)], first_rows.at[i], row_sem.at[i]) for i in range(segs)]
+    row_loads.append(pltpu.make_async_copy(docs, ids, row_sem.at[segs]))
+    for cp in row_loads:
+        cp.start()
+    for cp in row_loads:
+        cp.wait()
+    heads[...] = jnp.concatenate([first_rows[i].astype(F32)[0:1] for i in range(segs)], axis=0).astype(BF)
+    greet([(i // 8, i % 8) for i in ahead])
+
+    def cols(ref):
+        half = ref.shape[-1] // 2
+        return pl.ds(pl.multiple_of(c * half, half), half)
+
+    def mine(p):
+        i, r0, rn = pieces[p]
+        return shards[i].at[block, pl.ds(r0, rn), cols(shards[i])]
+
+    def slot(p, src):
+        i, r0, rn = pieces[p]
+        return outs[i].at[src, pl.ds(r0, rn), cols(outs[i])]
+
+    count = len(pieces)
+    owns = []
+    for p in range(count):
+        a = remote(mine(p), slot(p, d), own_send.at[0, p], own_recv.at[0, p], (first, s))
+        b = remote(mine(p), slot(p, d), own_send.at[1, p], own_recv.at[1, p], (second, s))
+        a.start()
+        b.start()
+        owns.append((a, b))
+    loads = []
+    for i in range(n):
+        cp = pltpu.make_async_copy(shards[i].at[block], bounce[i], load_sem.at[i])
+        cp.start()
+        loads.append(cp)
+    stores = []
+    for i in range(n):
+        loads[i].wait()
+        cp = pltpu.make_async_copy(bounce[i], outs[i].at[d], store_sem.at[i])
+        cp.start()
+        stores.append(cp)
+    far = (diagonal, first, second)
+
+    def columns(w, dev, core):
+        width = wins[w].shape[-1]
+        at = window(dev)[0] if w < 3 else dev * width
+        return pl.ds(pl.multiple_of(at + core * (width // 2), 128), width // 2)
+
+    origins = (shards[0], shards[1], shards[2], shards[4])
+    small = []
+    for k, peer in enumerate(far):
+        cp = remote(ids, docs_all.at[d], ids_send.at[k], ids_recv.at[k], (peer, s))
+        cp.start()
+        small.append(cp)
+        for w in range(4):
+            cp = remote(
+                origins[w].at[1, :, columns(w, peer, c)], wins[w].at[d, :, cols(wins[w])],
+                win_send.at[k, w], win_recv.at[k, w], (peer, s),
+            )
+            cp.start()
+            small.append(cp)
+    for j, i in enumerate(ahead):
+        cp = remote(heads, cot_all.at[me], all_send.at[j], all_recv.at[j], (i // 8, i % 8))
+        cp.start()
+        small.append(cp)
+    wloads = []
+    for w in range(4):
+        width = wins[w].shape[-1]
+        at = window(d)[0] if w < 3 else d * width
+        cp = pltpu.make_async_copy(origins[w].at[1, :, pl.ds(pl.multiple_of(at, 128), width)], wbounce[w], wload_sem.at[w])
+        cp.start()
+        wloads.append(cp)
+    for w in range(4):
+        wloads[w].wait()
+        cp = pltpu.make_async_copy(wbounce[w], wins[w].at[d], wstore_sem.at[w])
+        cp.start()
+        stores.append(cp)
+    for src, dst, i in ((heads, cot_all.at[me], 4), (ids, docs_all.at[d], 5)):
+        cp = pltpu.make_async_copy(src, dst, wstore_sem.at[i])
+        cp.start()
+        stores.append(cp)
+    fwds, cores = [], []
+
+    def share(p, src, k):
+        cp = remote(slot(p, src), slot(p, src), core_send.at[k, p], core_recv.at[k, p], (d, other))
+        cp.start()
+        cores.append(cp)
+
+    for p in range(count):
+        got = remote(slot(p, first), slot(p, first), own_send.at[0, p], own_recv.at[0, p], (first, s))
+        got.wait_recv()
+        f = remote(slot(p, first), slot(p, first), fwd_send.at[p], fwd_recv.at[p], (second, s))
+        f.start()
+        fwds.append(f)
+        share(p, first, 0)
+        got = remote(slot(p, second), slot(p, second), own_send.at[1, p], own_recv.at[1, p], (second, s))
+        got.wait_recv()
+        share(p, second, 1)
+        if p > 0:
+            fwd_wait(p - 1, slot, fwd_send, fwd_recv, diagonal, second, s)
+            share(p - 1, diagonal, 2)
+    fwd_wait(count - 1, slot, fwd_send, fwd_recv, diagonal, second, s)
+    share(count - 1, diagonal, 2)
+    for k, peer in enumerate(far):
+        for w in range(4):
+            got = wins[w].at[peer, :, cols(wins[w])]
+            remote(got, got, win_send.at[k, w], win_recv.at[k, w], (peer, s)).wait_recv()
+            cp = remote(got, got, wcore_send.at[k, w], wcore_recv.at[k, w], (d, other))
+            cp.start()
+            cores.append(cp)
+        remote(ids, docs_all.at[peer], ids_send.at[k], ids_recv.at[k], (peer, s)).wait_recv()
+    for j, i in enumerate(behind):
+        remote(heads, cot_all.at[i], all_send.at[j], all_recv.at[j], (i // 8, i % 8)).wait_recv()
+    for cp in small:
+        cp.wait_send()
+    for a, b in owns:
+        a.wait_send()
+        b.wait_send()
+    for f in fwds:
+        f.wait_send()
+    for cp in cores:
+        cp.wait()
+    for cp in stores:
+        cp.wait()
+
+
+def fwd_wait(p, slot, fwd_send, fwd_recv, diagonal, second, s):
+    remote(slot(p, diagonal), slot(p, diagonal), fwd_send.at[p], fwd_recv.at[p], (second, s)).wait_recv()
+
+
+def gather(shards, cot, docs, collective_id):
+    pieces = []
+    for i, w in enumerate(shards):
+        rows = w.shape[1]
+        parts = max(1, (rows * w.shape[2]) // (192 * 1536))
+        for p in range(parts):
+            pieces.append((i, p * rows // parts, rows // parts))
+    n, count = len(shards), len(pieces)
+    S, VM, dma = jax.ShapeDtypeStruct, pltpu.VMEM, pltpu.SemaphoreType.DMA
+    rows, width = shards[0].shape[1:]
+    segs = cot.shape[1] // 128
+    wins = [(rows, 256)] * 3 + [(rows, shards[4].shape[2] // 4)]
+    return pl.pallas_call(
+        functools.partial(gather_kernel, pieces, n, 0),
+        out_shape=[S((4,) + w.shape[1:], w.dtype) for w in shards]
+        + [S((4,) + w, BF) for w in wins]
+        + [S((32, segs, width), BF), S((4,) + docs.shape, docs.dtype)],
+        in_specs=[ANY] * (n + 2),
+        out_specs=[ANY] * (n + 6),
+        scratch_shapes=[VM(w.shape[1:], w.dtype) for w in shards]
+        + [VM(w, BF) for w in wins]
+        + [VM((segs, 8, width), BF), VM((segs, width), BF), VM(docs.shape, docs.dtype)]
+        + [dma((n,)), dma((n,)), dma((2, count)), dma((2, count)), dma((count,)), dma((count,)), dma((3, count)), dma((3, count))]
+        + [dma((4,)), dma((6,)), dma((3, 4)), dma((3, 4)), dma((3, 4)), dma((3, 4)), dma((segs + 1,)), dma((31,)), dma((31,)), dma((3,)), dma((3,))],
+        compiler_params=pltpu.CompilerParams(collective_id=collective_id, has_side_effects=True),
+        name="gather_weights",
+    )(*shards, cot, docs)
+
+
+def add_into(dst, a, b, rows):
+    step = 48
+
+    def body(i, carry):
+        r = pl.ds(pl.multiple_of(i * step, 16), step)
+        dst[r, :] = (a[r, :].astype(F32) + b[r, :].astype(F32)).astype(dst.dtype)
+        return carry
+
+    lax.fori_loop(0, rows // step, body, 0)
+
+
+def reduce_kernel(nc, r, g, vec, out, vec_out, own, recv0, recv1, recv2, recv3, recv4, fin, load_sem, out_sem,
+                  send0, rcv0, send1, rcv1, send2, rcv2, send3, rcv3, send4, rcv4, send5, rcv5, send6, rcv6, send7, rcv7, vsum, vgot, vsend, vrcv):
+    d, s = place()
+    c, first, second, other = plane_peers(d, s)
+    x, y = d % 2, d // 2
+    a = x * (1 - c) + y * c
+    b = y * (1 - c) + x * c
+    z = s // 2
+    z0, z1 = z % 2, z // 2
+    znear = (z + 1 - 2 * z0) * 2 + c
+    zfar = (z + 2 - 4 * z1) * 2 + c
+    h, q = r // 2, r // 4
+    greet([(first, s), (second, s), (d, other), (d, znear), (d, zfar)])
+
+    def quarter(aa, bb):
+        return aa * (1 + c) + bb * (2 - c)
+
+    def rows(core, k):
+        return pl.ds(pl.multiple_of(core * (nc * r) + k * r, 16), r)
+
+    started = []
+
+    def go(cp):
+        cp.start()
+        started.append(cp)
+
+    loads = []
+    for k in range(nc):
+        go(remote(g.at[:, rows(1 - c, k), :], recv0.at[k], send0.at[k], rcv0.at[k], (d, other)))
+        cp = pltpu.make_async_copy(g.at[:, rows(c, k), :], own.at[k], load_sem.at[k])
+        cp.start()
+        loads.append(cp)
+
+    def arrived(ref, sem):
+        pltpu.make_async_copy(ref, ref, sem).wait()
+
+    def piece(k, i0, i1):
+        return fin.at[c, k, pl.ds(pl.multiple_of(i0 * h + i1 * q, 16), q), :]
+
+    outs = []
+
+    def stage(t, k):
+        if t == 1:
+            arrived(recv0.at[k], rcv0.at[k])
+            loads[k].wait()
+            for bb in range(2):
+                away = quarter(1 - a, bb)
+                add_into(own.at[k, away], own.at[k, away], recv0.at[k, away], r)
+                go(remote(own.at[k, away], recv1.at[k, bb], send1.at[k, bb], rcv1.at[k, bb], (first, s)))
+            for bb in range(2):
+                keep = quarter(a, bb)
+                add_into(own.at[k, keep], own.at[k, keep], recv0.at[k, keep], r)
+        elif t == 2:
+            for bb in range(2):
+                arrived(recv1.at[k, bb], rcv1.at[k, bb])
+            away, keep = quarter(a, 1 - b), quarter(a, b)
+            add_into(own.at[k, away], own.at[k, away], recv1.at[k, 1 - b], r)
+            go(remote(own.at[k, away], recv2.at[k], send2.at[k], rcv2.at[k], (second, s)))
+            add_into(own.at[k, keep], own.at[k, keep], recv1.at[k, b], r)
+        elif t == 3:
+            arrived(recv2.at[k], rcv2.at[k])
+            keep = quarter(a, b)
+            away = pl.ds(pl.multiple_of((1 - z0) * h, 16), h)
+            mine = pl.ds(pl.multiple_of(z0 * h, 16), h)
+            add_into(own.at[k, keep, away], own.at[k, keep, away], recv2.at[k, away], h)
+            go(remote(own.at[k, keep, away], recv3.at[k], send3.at[k], rcv3.at[k], (d, znear)))
+            add_into(own.at[k, keep, mine], own.at[k, keep, mine], recv2.at[k, mine], h)
+        elif t == 4:
+            arrived(recv3.at[k], rcv3.at[k])
+            keep = quarter(a, b)
+            away = pl.ds(pl.multiple_of(z0 * h + (1 - z1) * q, 16), q)
+            mine = pl.ds(pl.multiple_of(z0 * h + z1 * q, 16), q)
+            raway = pl.ds(pl.multiple_of((1 - z1) * q, 16), q)
+            rmine = pl.ds(pl.multiple_of(z1 * q, 16), q)
+            add_into(own.at[k, keep, away], own.at[k, keep, away], recv3.at[k, raway], q)
+            go(remote(own.at[k, keep, away], recv4.at[k], send4.at[k], rcv4.at[k], (d, zfar)))
+            add_into(own.at[k, keep, mine], own.at[k, keep, mine], recv3.at[k, rmine], q)
+        elif t == 5:
+            arrived(recv4.at[k], rcv4.at[k])
+            keep = quarter(a, b)
+            mine = pl.ds(pl.multiple_of(z0 * h + z1 * q, 16), q)
+            add_into(piece(k, z0, z1), own.at[k, keep, mine], recv4.at[k], q)
+            go(remote(piece(k, z0, z1), piece(k, z0, z1), send5.at[k], rcv5.at[k], (d, zfar)))
+        elif t == 6:
+            arrived(piece(k, z0, 1 - z1), rcv5.at[k])
+            half = fin.at[c, k, pl.ds(pl.multiple_of(z0 * h, 16), h), :]
+            go(remote(half, half, send6.at[k], rcv6.at[k], (d, znear)))
+        elif t == 7:
+            half = fin.at[c, k, pl.ds(pl.multiple_of((1 - z0) * h, 16), h), :]
+            arrived(half, rcv6.at[k])
+            go(remote(fin.at[c, k], fin.at[c, k], send7.at[k], rcv7.at[k], (d, other)))
+            cp = pltpu.make_async_copy(fin.at[c, k], out.at[rows(c, k), :], out_sem.at[0, k])
+            cp.start()
+            outs.append(cp)
+        elif t == 8:
+            arrived(fin.at[1 - c, k], rcv7.at[k])
+            cp = pltpu.make_async_copy(fin.at[1 - c, k], out.at[rows(1 - c, k), :], out_sem.at[1, k])
+            cp.start()
+            outs.append(cp)
+
+    hops = [(d, other), (first, s), (second, s), (d, znear), (d, zfar)]
+    vsum[0] = vec[...]
+
+    def vector_hop(j):
+        if j > 0:
+            arrived(vgot.at[j - 1], vrcv.at[j - 1])
+            vsum[j] = vsum[j - 1] + vgot[j - 1]
+        if j < 5:
+            go(remote(vsum.at[j], vgot.at[j], vsend.at[j], vrcv.at[j], hops[j]))
+
+    for slot in range(nc + 8):
+        for t in range(8, 0, -1):
+            k = slot - (t - 1)
+            if 0 <= k < nc:
+                stage(t, k)
+        if slot < 6:
+            vector_hop(slot)
+    vec_out[...] = vsum[5]
+    for cp in started:
+        cp.wait_send()
+    for cp in outs:
+        cp.wait()
+
+
+def reduce(g, vec, nc, collective_id):
+    _, total, width = g.shape
+    r = total // 2 // nc
+    dma = pltpu.SemaphoreType.DMA
+    return pl.pallas_call(
+        functools.partial(reduce_kernel, nc, r),
+        out_shape=[jax.ShapeDtypeStruct((total, width), g.dtype), jax.ShapeDtypeStruct(vec.shape, vec.dtype)],
+        in_specs=[ANY, pl.BlockSpec(memory_space=pltpu.VMEM)],
+        out_specs=[ANY, pl.BlockSpec(memory_space=pltpu.VMEM)],
+        scratch_shapes=[
+            pltpu.VMEM((nc, 4, r, width), g.dtype),
+            pltpu.VMEM((nc, 4, r, width), g.dtype),
+            pltpu.VMEM((nc, 2, r, width), g.dtype),
+            pltpu.VMEM((nc, r, width), g.dtype),
+            pltpu.VMEM((nc, r // 2, width), g.dtype),
+            pltpu.VMEM((nc, r // 4, width), g.dtype),
+            pltpu.VMEM((2, nc, r, width), g.dtype),
+            dma((nc,)),
+            dma((2, nc)),
+            dma((nc,)), dma((nc,)),
+            dma((nc, 2)), dma((nc, 2)),
+            dma((nc,)), dma((nc,)),
+            dma((nc,)), dma((nc,)),
+            dma((nc,)), dma((nc,)),
+            dma((nc,)), dma((nc,)),
+            dma((nc,)), dma((nc,)),
+            dma((nc,)), dma((nc,)),
+            pltpu.VMEM((6,) + vec.shape, vec.dtype),
+            pltpu.VMEM((5,) + vec.shape, vec.dtype),
+            dma((5,)), dma((5,)),
+        ],
+        compiler_params=pltpu.CompilerParams(collective_id=collective_id, has_side_effects=True, vmem_limit_bytes=60 << 20),
+        name="reduce_grads",
+    )(g, vec)
+
+
+TILE = 256
+
+
+def dot(a, b):
+    return lax.dot_general(a, b, (((1,), (0,)), ((), ())), preferred_element_type=F32)
+
+
+def dot_nt(a, b):
+    return lax.dot_general(a, b, (((1,), (1,)), ((), ())), preferred_element_type=F32)
+
+
+def dot_tn(a, b):
+    return lax.dot_general(a, b, (((0,), (0,)), ((), ())), preferred_element_type=F32)
+
+
+def tiles(i, size=TILE):
+    return pl.ds(pl.multiple_of(i * size, size), size)
+
+
+def standard(r):
+    centred = r - jnp.mean(r, axis=-1, keepdims=True)
+    rstd = lax.rsqrt(jnp.mean(centred * centred, axis=-1, keepdims=True) + epsilon)
+    return centred * rstd, rstd
+
+
+def standard_back(grad, xhat, rstd):
+    return rstd * (
+        grad
+        - jnp.mean(grad, axis=-1, keepdims=True)
+        - xhat * jnp.mean(grad * xhat, axis=-1, keepdims=True)
+    )
+
+
+def gelu_parts(u):
+    phi = 0.5 * (1.0 + lax.erf(u * 0.7071067811865476))
+    return u * phi, phi + u * (0.3989422804014327 * jnp.exp(-0.5 * u * u))
+
+
+def head_masks():
+    lane = lax.broadcasted_iota(jnp.int32, (1, 128), 1)
+    low = (lane < 64).astype(F32)
+    return (low.astype(BF), (1.0 - low).astype(BF))
+
+
+def row_sum(v):
+    return jnp.sum(v, axis=0, keepdims=True)
+
+
+def forward_kernel(x, wq, wk, wv, wo, wi, w2, qb, vb, ob, g1, c1, ib, b2, g2, c2,
+                   q_o, k_o, v_o, p_o, o_o, hb_o, e_o, gp_o, x1_o, r1_o, x2_o, r2_o, y_o, cls_o,
+                   vq, vk, vv, vo, vi, v2, x1, x2, in_sem, p_s, e_s, gp_s, out_sem):
+    loads = [
+        pltpu.make_async_copy(src, dst, in_sem.at[i])
+        for i, (src, dst) in enumerate(((wq, vq), (wk, vk), (wv, vv), (wo, vo), (wi, vi), (w2, v2)))
+    ]
+    for cp in loads:
+        cp.start()
+    rows, width = x.shape
+    segs = rows // 128
+    nt = width // TILE
+    loads[0].wait()
+    loads[1].wait()
+    loads[2].wait()
+
+    def qkv(t, carry):
+        lanes = tiles(t)
+        q_o[:, lanes] = (dot(x[...], vq[:, lanes]) + qb[0:1, lanes].astype(F32)).astype(BF)
+        k_o[:, lanes] = dot(x[...], vk[:, lanes]).astype(BF)
+        v_o[:, lanes] = (dot(x[...], vv[:, lanes]) + vb[0:1, lanes].astype(F32)).astype(BF)
+        return carry
+
+    lax.fori_loop(0, nt, qkv, 0)
+    masks = head_masks()
+
+    def attend(hp, carry):
+        lanes = tiles(hp, 128)
+        for s in range(segs):
+            here = slice(s * 128, s * 128 + 128)
+            qs, ks, vs = q_o[here, lanes], k_o[here, lanes], v_o[here, lanes]
+            mixed = None
+            for h in range(2):
+                scores = dot_nt(qs * masks[h], ks)
+                top = jnp.max(scores, axis=-1, keepdims=True)
+                weight = jnp.exp((scores - top) * 0.125)
+                share = (weight * (1.0 / jnp.sum(weight, axis=-1, keepdims=True))).astype(BF)
+                p_s[hp, s, h] = share
+                part = dot(share, vs * masks[h])
+                mixed = part if mixed is None else mixed + part
+            o_o[here, lanes] = mixed.astype(BF)
+        return carry
+
+    lax.fori_loop(0, width // 128, attend, 0)
+    p_copy = pltpu.make_async_copy(p_s, p_o, out_sem.at[0])
+    p_copy.start()
+    loads[3].wait()
+
+    def out(t, carry):
+        lanes = tiles(t)
+        x1[:, lanes] = dot(o_o[...], vo[:, lanes]) + ob[0:1, lanes].astype(F32) + x[:, lanes].astype(F32)
+        return carry
+
+    lax.fori_loop(0, nt, out, 0)
+
+    def first(i, carry):
+        r = tiles(i, 64)
+        xhat, rstd = standard(x1[r, :])
+        x1_o[r, :] = xhat
+        r1_o[r, :] = jnp.broadcast_to(rstd, (64, 128))
+        hidden = xhat * g1[0:1, :].astype(F32) + c1[0:1, :].astype(F32)
+        hb_o[r, :] = hidden.astype(BF)
+        x2[r, :] = hidden + b2[0:1, :].astype(F32)
+        return carry
+
+    lax.fori_loop(0, rows // 64, first, 0)
+    loads[4].wait()
+    loads[5].wait()
+
+    def ffn(t, carry):
+        lanes = tiles(t)
+        u = dot(hb_o[...], vi[:, lanes]) + ib[0:1, lanes].astype(F32)
+        e, gp = gelu_parts(u)
+        e_s[:, lanes] = e.astype(BF)
+        gp_s[:, lanes] = gp.astype(BF)
+        return carry
+
+    lax.fori_loop(0, vi.shape[1] // TILE, ffn, 0)
+    e_copy = pltpu.make_async_copy(e_s, e_o, out_sem.at[1])
+    gp_copy = pltpu.make_async_copy(gp_s, gp_o, out_sem.at[2])
+    e_copy.start()
+    gp_copy.start()
+
+    def outer(t, carry):
+        lanes = tiles(t)
+        x2[:, lanes] += dot(e_s[...], v2[:, lanes])
+        return carry
+
+    lax.fori_loop(0, nt, outer, 0)
+
+    def second(i, carry):
+        r = tiles(i, 64)
+        xhat, rstd = standard(x2[r, :])
+        x2_o[r, :] = xhat
+        r2_o[r, :] = jnp.broadcast_to(rstd, (64, 128))
+        y_o[r, :] = (xhat * g2[0:1, :].astype(F32) + c2[0:1, :].astype(F32)).astype(BF)
+        return carry
+
+    lax.fori_loop(0, rows // 64, second, 0)
+    for s in range(segs):
+        cls_o[s : s + 1, :] = x2_o[s * 128 : s * 128 + 1, :] * g2[0:1, :].astype(F32) + c2[0:1, :].astype(F32)
+    p_copy.wait()
+    e_copy.wait()
+    gp_copy.wait()
+
+
+def forward(x, weights, vectors):
+    rows, width = x.shape
+    ff = weights[4].shape[1]
+    segs, pairs = rows // 128, width // 128
+    S = jax.ShapeDtypeStruct
+    V = pl.BlockSpec(memory_space=pltpu.VMEM)
+    low, full = S((rows, width), BF), S((rows, width), F32)
+    wide = S((rows, ff), BF)
+    probs = S((pairs, segs, 2, 128, 128), BF)
+    col = S((rows, 128), F32)
+    return pl.pallas_call(
+        forward_kernel,
+        out_shape=[low, low, low, probs, low, low, wide, wide, full, col, full, col, low, S((segs, width), F32)],
+        in_specs=[V] + [ANY] * 6 + [V] * 9,
+        out_specs=[V, V, V, ANY, V, V, ANY, ANY, V, V, V, V, V, V],
+        scratch_shapes=[pltpu.VMEM(w.shape, BF) for w in weights]
+        + [pltpu.VMEM((rows, width), F32)] * 2
+        + [
+            pltpu.SemaphoreType.DMA((6,)),
+            pltpu.VMEM(probs.shape, BF),
+            pltpu.VMEM(wide.shape, BF),
+            pltpu.VMEM(wide.shape, BF),
+            pltpu.SemaphoreType.DMA((3,)),
+        ],
+        compiler_params=pltpu.CompilerParams(vmem_limit_bytes=60 << 20),
+        name="segment_forward",
+    )(x, *weights, *vectors)
+
+
+def backward_kernel(x, cot, dcl, q, k, v, p, o, hb, e, gp, x1, r1, x2, r2, y, z, wq, wk, wv, wo, wi, w2, g1, g2,
+                    dx_o, y_o, g_o, vec_o,
+                    vq, vk, vv, vo, vi, v2, e_s, gp_s, p_s, gs, dr2, acc, df, ht, da, do, dq, dk, dv, in_sem, out_sem):
+    loads = [
+        pltpu.make_async_copy(src, dst, in_sem.at[i])
+        for i, (src, dst) in enumerate(
+            ((w2, v2), (e, e_s), (gp, gp_s), (wi, vi), (wo, vo), (p, p_s), (wq, vq), (wk, vk), (wv, vv))
+        )
+    ]
+    for cp in loads:
+        cp.start()
+    rows, width = x.shape
+    segs, nt = rows // 128, width // TILE
+    ff = vi.shape[1]
+    share = width // 4
+    vec_o[...] = jnp.zeros_like(vec_o)
+
+    def second(i, carry):
+        gain_sum, shift_sum, bias_sum = carry
+        r = tiles(i, 64)
+        dy, out = cot[r, :].astype(F32), y[r, :].astype(F32)
+        at = lax.broadcasted_iota(jnp.int32, (64, 1), 0) + i * 64
+        for s in range(segs):
+            dy = jnp.where(at == s * 128, dcl[s : s + 1, :], dy)
+            out = jnp.where(at == s * 128, z[s : s + 1, :], out)
+        y_o[r, :] = out.astype(BF)
+        xhat = x2[r, :]
+        back = standard_back(dy * g2[0:1, :].astype(F32), xhat, r2[r, 0:1])
+        dr2[r, :] = back
+        low = back.astype(BF)
+        df[r, :] = low
+        return (gain_sum + row_sum(dy * xhat), shift_sum + row_sum(dy), bias_sum + row_sum(low.astype(F32)))
+
+    zero = jnp.zeros((1, width), F32)
+    sums = lax.fori_loop(0, rows // 64, second, (zero, zero, zero))
+    vec_o[6:7, :], vec_o[7:8, :], vec_o[5:6, :] = sums
+    ht[...] = hb[...].T
+    acc[...] = dr2[...]
+    for i in range(4):
+        loads[i].wait()
+
+    def ffn(t, carry):
+        wide = tiles(t)
+        block, lanes = t // nt, tiles(t % nt)
+        de = dot_nt(df[...], v2[wide, :]).astype(BF).astype(F32)
+        du = (de * gp_s[:, wide].astype(F32)).astype(BF)
+        vec_o[pl.ds(8 + block, 1), lanes] = row_sum(du.astype(F32))
+        back = dot_tn(e_s[:, wide], df[...])
+        gs[block, pl.ds(pl.multiple_of(8 * share + (t % nt) * TILE, TILE), TILE), :] = back.astype(BF)
+        inner = dot(ht[...], du).astype(BF)
+        for d in range(4):
+            gs[d, pl.ds(pl.multiple_of(4 * share + block * share, 64), share), lanes] = inner[d * share : d * share + share]
+        acc[...] += dot_nt(du, vi[:, wide])
+        return carry
+
+    lax.fori_loop(0, ff // TILE, ffn, 0)
+    half = 4 * share
+    copies = [pltpu.make_async_copy(gs.at[:, half:, :], g_o.at[:, half:, :], out_sem.at[0])]
+    copies[0].start()
+
+    def first(i, carry):
+        gain_sum, shift_sum, bias_sum = carry
+        r = tiles(i, 64)
+        dh = acc[r, :]
+        xhat = x1[r, :]
+        back = standard_back(dh * g1[0:1, :].astype(F32), xhat, r1[r, 0:1])
+        dr2[r, :] = back
+        low = back.astype(BF)
+        da[r, :] = low
+        return (gain_sum + row_sum(dh * xhat), shift_sum + row_sum(dh), bias_sum + row_sum(low.astype(F32)))
+
+    sums = lax.fori_loop(0, rows // 64, first, (zero, zero, zero))
+    vec_o[3:4, :], vec_o[4:5, :], vec_o[2:3, :] = sums
+    loads[4].wait()
+    do[...] = dot_nt(da[...], vo[...]).astype(BF)
+
+    def spread(at, lhs, rhs):
+        back = dot_tn(lhs, rhs).astype(BF)
+        for d in range(4):
+            gs[d, at * share : at * share + share, :] = back[d * share : d * share + share]
+
+    spread(3, o[...], da[...])
+    loads[5].wait()
+    masks = head_masks()
+
+    def attend(hp, carry):
+        lanes = tiles(hp, 128)
+        for s in range(segs):
+            here = slice(s * 128, s * 128 + 128)
+            qs, ks, vs, dos = q[here, lanes], k[here, lanes], v[here, lanes], do[here, lanes]
+            dqs = dks = dvs = 0.0
+            for h in range(2):
+                pl_ = p_s[hp, s, h]
+                pf = pl_.astype(F32)
+                dom = dos * masks[h]
+                dp = dot_nt(dom, vs).astype(BF).astype(F32)
+                ds = (pf * (dp - jnp.sum(pf * dp, axis=-1, keepdims=True))).astype(BF)
+                dqs += dot(ds, ks * masks[h])
+                dks += dot_tn(ds, qs * masks[h])
+                dvs += dot_tn(pl_, dom)
+            dq[here, lanes] = (dqs * 0.125).astype(BF)
+            dk[here, lanes] = (dks * 0.125).astype(BF)
+            dv[here, lanes] = dvs.astype(BF)
+        return carry
+
+    lax.fori_loop(0, width // 128, attend, 0)
+    vec_o[0:1, :] = row_sum(dq[...].astype(F32))
+    vec_o[1:2, :] = row_sum(dv[...].astype(F32))
+    ht[...] = x[...].T
+    for i in range(6, 9):
+        loads[i].wait()
+
+    def weights(at, rhs):
+        back = dot(ht[...], rhs[...]).astype(BF)
+        for d in range(4):
+            gs[d, at * share : at * share + share, :] = back[d * share : d * share + share]
+
+    weights(0, dq)
+    weights(1, dk)
+    weights(2, dv)
+    copies.append(pltpu.make_async_copy(gs.at[:, :half, :], g_o.at[:, :half, :], out_sem.at[1]))
+    copies[1].start()
+
+    def source(t, carry):
+        r = tiles(t)
+        dx = dr2[:, r] + dot_nt(dq[...], vq[r, :]) + dot_nt(dk[...], vk[r, :]) + dot_nt(dv[...], vv[r, :])
+        dx_o[:, r] = dx.astype(BF)
+        return carry
+
+    lax.fori_loop(0, nt, source, 0)
+    for cp in copies:
+        cp.wait()
+
+
+def backward(x, cot, dcl, saved, y, z, weights, g1, g2):
+    q, k, v, p, o, hb, e, gp, x1, r1, x2, r2 = saved
+    rows, width = x.shape
+    ff = weights[4].shape[1]
+    S = jax.ShapeDtypeStruct
+    V = pl.BlockSpec(memory_space=pltpu.VMEM)
+    packed = S((4, width // 4 * 4 + 2 * ff // 4, width), BF)
+    VM = pltpu.VMEM
+    low, full = VM((rows, width), BF), VM((rows, width), F32)
+    return pl.pallas_call(
+        backward_kernel,
+        out_shape=[S((rows, width), BF), S((rows, width), BF), packed, S((16, width), F32)],
+        in_specs=[V, V, V, V, V, V, ANY, V, V, ANY, ANY, V, V, V, V, V, V] + [ANY] * 6 + [V] * 2,
+        out_specs=[V, V, ANY, V],
+        scratch_shapes=[VM(w.shape, BF) for w in weights]
+        + [
+            VM((rows, ff), BF),
+            VM((rows, ff), BF),
+            VM(p.shape, BF),
+            VM(packed.shape, BF),
+            full, full, low,
+            VM((width, rows), BF),
+            low, low, low, low, low,
+            pltpu.SemaphoreType.DMA((9,)),
+            pltpu.SemaphoreType.DMA((2,)),
+        ],
+        compiler_params=pltpu.CompilerParams(vmem_limit_bytes=63 << 20),
+        name="segment_backward",
+    )(x, cot, dcl, q, k, v, p, o, hb, e, gp, x1, r1, x2, r2, y, z, *weights, g1, g2)
+
+
+def cross_kernel(cls, emb, cot_all, docs, wq, wk, wv, wi, out_w, outer_w,
+                 qb, vb, ob, g1, c1, ib, b2, g2, c2,
+                 z_o, dcl_o, xw_o, hw_o, ow_o, e_o, dqkv_o, du_o, da_o, df_o, vec_o, emb_o,
+                 vq, vk, vv, vi, vo, v2, heads, xall, rows_s, p_s, dqkv_s, du_s, send1, got1, send2, got2,
+                 in_sem, all_send, all_recv, s1, r1, s2, r2, qs_send, qs_recv, us_send, us_recv, o_sem):
+    d, s = place()
+    c, first, second, other = plane_peers(d, s)
+    start, off = window(d)
+    me, ahead, behind = everyone(d, s)
+    far = [3 - d, first, second]
+    lane_w = pl.ds(start, 256)
+    loads = [
+        pltpu.make_async_copy(src, dst, in_sem.at[i])
+        for i, (src, dst) in enumerate(
+            (
+                (wq, vq), (wk, vk), (wv, vv),
+                (out_w.at[1], vo.at[pl.ds(pl.multiple_of(off, 64), 192)]),
+                (wi, vi), (outer_w.at[1], v2),
+            )
+        )
+    ]
+    for cp in loads:
+        cp.start()
+    vo[pl.ds(pl.multiple_of(192 * (1 - d % 2), 64), 64), :] = jnp.zeros((64, 768), BF)
+    pick = lax.broadcasted_iota(jnp.int32, (8, 32), 0) + 4 * s == lax.broadcasted_iota(jnp.int32, (8, 32), 1)
+    position = dot(pick.astype(BF), emb[...])
+    heads[...] = (cls[...] + position[0:4]).astype(BF)
+    greet([(i // 8, i % 8) for i in ahead])
+    sent = []
+    for j, i in enumerate(ahead):
+        cp = remote(heads, xall.at[me], all_send.at[j], all_recv.at[j], (i // 8, i % 8))
+        cp.start()
+        sent.append(cp)
+    xall[me] = heads[...]
+    dys = []
+    for i in range(32):
+        rows_s[4 * i : 4 * i + 4, :] = cot_all[i].astype(F32)
+    dy = rows_s[...]
+    ids = lax.broadcasted_iota(jnp.int32, (8, 128), 1) // 32 * 1024
+    ids = ids.astype(F32)
+    lane = lax.broadcasted_iota(jnp.int32, (32, 128), 1)
+    key = lax.broadcasted_iota(jnp.int32, (32, 128), 0)
+    for r in range(4):
+        numbers = jnp.broadcast_to(docs[r], (8, 32)).astype(F32).astype(BF)
+        ids = ids + dot(numbers, (lane == key + 32 * r).astype(BF))
+    across = jnp.broadcast_to(ids[0:1], (128, 128))
+    allowed = across == across.T
+    for j, i in enumerate(behind):
+        remote(heads, xall.at[i], all_send.at[j], all_recv.at[j], (i // 8, i % 8)).wait_recv()
+    for i in range(32):
+        rows_s[4 * i : 4 * i + 4, :] = xall[i].astype(F32)
+    xf = rows_s[...]
+    x = xf.astype(BF)
+
+    def total(n, partial):
+        send1[n] = partial.astype(BF)
+        one = remote(send1.at[n], got1.at[n], s1.at[n], r1.at[n], (first, s))
+        one.start()
+        one.wait_recv()
+        both = send1[n].astype(F32) + got1[n].astype(F32)
+        send2[n] = both.astype(BF)
+        two = remote(send2.at[n], got2.at[n], s2.at[n], r2.at[n], (second, s))
+        two.start()
+        two.wait_recv()
+        sent.append(one)
+        sent.append(two)
+        return send2[n].astype(F32) + got2[n].astype(F32)
+
+    def vector(ref, lanes=slice(None)):
+        return ref[1:2, lanes].astype(F32)
+
+    for i in range(3):
+        loads[i].wait()
+    q = (dot(x, vq[...]) + vector(qb, lane_w)).astype(BF)
+    k = dot(x, vk[...]).astype(BF)
+    v = (dot(x, vv[...]) + vector(vb, lane_w)).astype(BF)
+    masks = head_masks()
+    mixed = []
+    for pair in range(2):
+        l = slice(pair * 128, pair * 128 + 128)
+        both = None
+        for h in range(2):
+            scores = jnp.where(allowed, dot_nt(q[:, l] * masks[h], k[:, l]) * 0.125, -1e30)
+            weight = jnp.exp(scores - jnp.max(scores, axis=-1, keepdims=True))
+            share = (weight * (1.0 / jnp.sum(weight, axis=-1, keepdims=True))).astype(BF)
+            p_s[2 * pair + h] = share
+            part = dot(share, v[:, l] * masks[h])
+            both = part if both is None else both + part
+        mixed.append(both.astype(BF))
+    loads[3].wait()
+    ow = jnp.concatenate(mixed, axis=1)
+    ow_o[...] = ow
+    branch = total(0, dot(ow, vo[...]))
+    xhat1, rstd1 = standard(xf + branch + vector(ob))
+    hidden = xhat1 * vector(g1) + vector(c1)
+    hb = hidden.astype(BF)
+    rows_s[...] = hidden
+    hw_o[...] = rows_s[:, lane_w].astype(BF)
+    rows_s[...] = xf
+    xw_o[...] = rows_s[:, lane_w].astype(BF)
+    loads[4].wait()
+    loads[5].wait()
+    wide = pl.ds(pl.multiple_of(d * 768, 768), 768)
+    e, gp = gelu_parts(dot(hb, vi[...]) + vector(ib, wide))
+    e = e.astype(BF)
+    e_o[...] = e
+    outer = total(1, dot(e, v2[...]))
+    xhat2, rstd2 = standard(hidden + outer + vector(b2))
+    z = (xhat2 * vector(g2) + vector(c2)).astype(BF)
+    own = lax.broadcasted_iota(jnp.int32, (8, 128), 0) + 4 * me == lax.broadcasted_iota(jnp.int32, (8, 128), 1)
+    own = own.astype(BF)
+    z_o[...] = dot(own, z)
+    vec_o[6:7, :] = row_sum(dy * xhat2)
+    vec_o[7:8, :] = row_sum(dy)
+    dr2 = standard_back(dy * vector(g2), xhat2, rstd2)
+    df = dr2.astype(BF)
+    df_o[...] = df
+    vec_o[5:6, :] = row_sum(df.astype(F32))
+    du = (dot_nt(df, v2[...]).astype(BF).astype(F32) * gp).astype(BF)
+    du_s[d] = du
+    dh = dr2 + total(2, dot_nt(du, vi[...]))
+    for n, peer in enumerate(far):
+        cp = remote(du_s.at[d], du_s.at[d], us_send.at[n], us_recv.at[n], (peer, s))
+        cp.start()
+        sent.append(cp)
+    vec_o[3:4, :] = row_sum(dh * xhat1)
+    vec_o[4:5, :] = row_sum(dh)
+    dr1 = standard_back(dh * vector(g1), xhat1, rstd1)
+    da = dr1.astype(BF)
+    da_o[...] = da
+    vec_o[2:3, :] = row_sum(da.astype(F32))
+    do = dot_nt(da, vo[...]).astype(BF)
+    dqs, dks, dvs = [], [], []
+    for pair in range(2):
+        l = slice(pair * 128, pair * 128 + 128)
+        dqp = dkp = dvp = 0.0
+        for h in range(2):
+            share = p_s[2 * pair + h]
+            pf = share.astype(F32)
+            dom = do[:, l] * masks[h]
+            dp = dot_nt(dom, v[:, l]).astype(BF).astype(F32)
+            ds = (pf * (dp - jnp.sum(pf * dp, axis=-1, keepdims=True))).astype(BF)
+            dqp += dot(ds, k[:, l] * masks[h])
+            dkp += dot_tn(ds, q[:, l] * masks[h])
+            dvp += dot_tn(share, dom)
+        dqs.append((dqp * 0.125).astype(BF))
+        dks.append((dkp * 0.125).astype(BF))
+        dvs.append(dvp.astype(BF))
+    dq, dk, dv = (jnp.concatenate(t, axis=1) for t in (dqs, dks, dvs))
+    dqkv_s[d, :, 0:256] = dq
+    dqkv_s[d, :, 256:512] = dk
+    dqkv_s[d, :, 512:768] = dv
+    dx = dr1 + total(3, dot_nt(dq, vq[...]) + dot_nt(dk, vk[...]) + dot_nt(dv, vv[...]))
+    for n, peer in enumerate(far):
+        cp = remote(dqkv_s.at[d], dqkv_s.at[d], qs_send.at[n], qs_recv.at[n], (peer, s))
+        cp.start()
+        sent.append(cp)
+    dcl = dx.astype(BF)
+    dcl_o[...] = dot(own, dcl)
+    back = dcl.astype(F32)
+    emb_o[...] = back[0:32] + back[32:64] + back[64:96] + back[96:128]
+    for n, peer in enumerate(far):
+        remote(du_s.at[peer], du_s.at[peer], us_send.at[n], us_recv.at[n], (peer, s)).wait_recv()
+        remote(dqkv_s.at[peer], dqkv_s.at[peer], qs_send.at[n], qs_recv.at[n], (peer, s)).wait_recv()
+    outs = [pltpu.make_async_copy(du_s, du_o, o_sem.at[0]), pltpu.make_async_copy(dqkv_s, dqkv_o, o_sem.at[1])]
+    for cp in outs:
+        cp.start()
+    for cp in sent:
+        cp.wait_send()
+    for cp in outs:
+        cp.wait()
+
+
+def cross(cls, emb, cot_all, docs, wq, wk, wv, wi, out_w, outer_w, vectors, collective_id):
+    S = jax.ShapeDtypeStruct
+    V = pl.BlockSpec(memory_space=pltpu.VMEM)
+    VM, dma = pltpu.VMEM, pltpu.SemaphoreType.DMA
+    low, win, four = S((128, 768), BF), S((128, 256), BF), S((4, 128, 768), BF)
+    return pl.pallas_call(
+        cross_kernel,
+        out_shape=[
+            S((8, 768), F32), S((8, 768), F32), win, win, win, low, four, four, low, low,
+            S((8, 768), F32), S((32, 768), F32),
+        ],
+        in_specs=[V] * 4 + [ANY] * 6 + [V] * 9,
+        out_specs=[V] * 6 + [ANY] * 2 + [V] * 4,
+        scratch_shapes=[
+            VM((768, 256), BF), VM((768, 256), BF), VM((768, 256), BF), VM((768, 768), BF), VM((256, 768), BF), VM((768, 768), BF),
+            VM((4, 768), BF), VM((32, 4, 768), BF), VM((128, 768), F32), VM((4, 128, 128), BF),
+            VM((4, 128, 768), BF), VM((4, 128, 768), BF),
+            VM((4, 128, 768), BF), VM((4, 128, 768), BF), VM((4, 128, 768), BF), VM((4, 128, 768), BF),
+            dma((6,)), dma((31,)), dma((31,)),
+            dma((4,)), dma((4,)), dma((4,)), dma((4,)), dma((3,)), dma((3,)), dma((3,)), dma((3,)), dma((2,)),
+        ],
+        compiler_params=pltpu.CompilerParams(collective_id=collective_id, has_side_effects=True, vmem_limit_bytes=48 << 20),
+        name="cross_block",
+    )(cls, emb, cot_all, docs, wq, wk, wv, wi, out_w, outer_w, *vectors)
+
+
+def finish_kernel(red, vec, emb, xw, hw, ow, e, dqkv, du, da, df, vec1,
+                  gq, gqb, gk, gv, gvb, go, gob, gg1, gc1, gi, gib, g2_, gb2, gg2, gc2, gemb, vec_s):
+    d = lax.axis_index("dp")
+    odd = d % 2 == 1
+    start, _ = window(d)
+
+    def own(w):
+        return jnp.where(odd, w[:, 64:256], w[:, 0:192])
+
+    def whole(at):
+        parts = [dqkv[i, :, at * 256 : at * 256 + 256] for i in range(4)]
+        return jnp.concatenate(
+            [
+                parts[0][:, :128], parts[0][:, 128:] + parts[1][:, :128], parts[1][:, 128:],
+                parts[2][:, :128], parts[2][:, 128:] + parts[3][:, :128], parts[3][:, 128:],
+            ],
+            axis=1,
+        )
+
+    x, h, o = own(xw[...].astype(F32)).astype(BF), own(hw[...].astype(F32)).astype(BF), own(ow[...].astype(F32)).astype(BF)
+    dq, dk, dv = whole(0), whole(1), whole(2)
+    for at, (out, left, right) in enumerate(((gq, x, dq), (gk, x, dk), (gv, x, dv), (go, o, da[...]))):
+        out[0] = red[at * 192 : at * 192 + 192, :].astype(F32)
+        out[1] = dot_tn(left, right)
+    for j in range(4):
+        l = slice(j * 768, j * 768 + 768)
+        gi[0, :, l] = red[768 + j * 192 : 960 + j * 192, :].astype(F32)
+        gi[1, :, l] = dot_tn(h, du[j])
+    g2_[0] = red[1536:2304, :].astype(F32)
+    g2_[1] = dot_tn(e[...], df[...])
+    lanes = pl.ds(start, 256)
+    mine = own(vec[:, lanes])
+    vec_s[...] = vec1[...]
+    vec_s[0:1, :] = row_sum(dq.astype(F32))
+    vec_s[1:2, :] = row_sum(dv.astype(F32))
+    cross = own(vec_s[:, lanes])
+    for r, out in enumerate((gqb, gvb, gob, gg1, gc1, gb2, gg2, gc2)):
+        out[0:1, :] = mine[r : r + 1]
+        out[1:2, :] = cross[r : r + 1]
+    gib[0:1, :] = vec[pl.ds(8 + d, 1), :]
+    gib[1:2, :] = row_sum(du[d].astype(F32))
+    gemb[...] = own(emb[:, lanes])
+
+
+def finish(red, vec, crossed):
+    (_, _, xw, hw, ow, e, dqkv, du, da, df, vec1, emb) = crossed
+    S = jax.ShapeDtypeStruct
+    V = pl.BlockSpec(memory_space=pltpu.VMEM)
+    square, line = S((2, 192, 768), F32), S((2, 192), F32)
+    return pl.pallas_call(
+        finish_kernel,
+        out_shape=[
+            square, line, square, square, line, square, line, line, line,
+            S((2, 192, 3072), F32), S((2, 768), F32), S((2, 768, 768), F32), line, line, line, S((32, 192), F32),
+        ],
+        in_specs=[V] * 12,
+        out_specs=[V] * 16,
+        scratch_shapes=[pltpu.VMEM((8, 768), F32)],
+        compiler_params=pltpu.CompilerParams(vmem_limit_bytes=48 << 20),
+        name="finish_grads",
+    )(red, vec, emb, xw, hw, ow, e, dqkv, du, da, df, vec1)
+
+
+def fast_shards(
+    inputs,
+    doc_ids,
+    cotangent,
+    query_weight,
+    query_bias,
+    key_weight,
+    value_weight,
+    value_bias,
+    out_weight,
+    out_bias,
+    first_gain,
+    first_shift,
+    inner_weight,
+    inner_bias,
+    outer_weight,
+    outer_bias,
+    second_gain,
+    second_shift,
+    segment_embed,
+):
+    weights = (query_weight, key_weight, value_weight, out_weight, inner_weight, outer_weight)
+    vectors = (query_bias, value_bias, out_bias, first_gain, first_shift, inner_bias, outer_bias, second_gain, second_shift)
+    gathered = gather(weights, cotangent, doc_ids, 1)
+    full = [w.reshape(-1, w.shape[-1]) for w in gathered[:6]]
+    windows = [w.reshape(-1, w.shape[-1]) for w in gathered[6:10]]
+    cot_all, docs = gathered[10:]
+    *saved, y, cls = forward(inputs[0], full, vectors)
+    crossed = cross(cls, segment_embed, cot_all, docs, *windows, out_weight, outer_weight, vectors, 2)
+    grad, output, packed, vec = backward(
+        inputs[0], cotangent[0], crossed[1], saved, y, crossed[0], full, first_gain, second_gain
+    )
+    total, vec = reduce(packed, vec, 6, 3)
+    return (output[None], grad[None], *finish(total, vec, crossed))
+
+
 def solution(mesh):
     placed = (
         P("dp", "seg", None),
@@ -396,8 +1433,9 @@
         P(),
         P(),
     )
+    square = mesh.shape["dp"] == 4 and mesh.shape["seg"] == 8
     return jax.shard_map(
-        shards,
+        fast_shards if square else shards,
         mesh=mesh,
         in_specs=placed,
         out_specs=(

time: 1630 us -> 366 us (0.22)
  waiting for transfers between devices: 1260 us -> 0 us
  Pallas kernels: 0 us -> 344 us
  matrix products: 130 us -> 0 us
  other arithmetic: 69.1 us -> 0 us
  local copies, waits for them, and re-layouts: 81.3 us -> 18.7 us
  blocking collectives: 57.1 us -> 0 us
  between operations: 17.5 us -> 1.13 us
    reduce_scatter x4 -> x0, waiting for transfers between devices: 389 us -> none  [the longest x1 97.9 us: shards(): lax.psum_scatter(segment_grads[11], 'dp', scatter_dimension=0, tiled=True)]
    pallas_call x0 -> x6, Pallas kernels: none -> 344 us  [the longest x1 113 us: reduce(): pl.pallas_call(functools.partial(reduce_kernel, nc, r), out_shape=[jax.Sh...]
    unnamed x31 -> x0, waiting for transfers between devices: 294 us -> none
    all_gather x6 -> x0, waiting for transfers between devices: 289 us -> none  [the longest x1 95.4 us: shards(): lax.all_gather(inner_weight, 'dp', axis=1, tiled=True)]
    psum x1 -> x0, waiting for transfers between devices: 286 us -> none  [shards(): lax.psum((shares[0], shares[1], shares[2], shares[3], shares[4], shares[5...]
    dot_general x46 -> x0, matrix products: 125 us -> none  [the longest x12 41.6 us: weight_grad(): jnp.einsum('gnd,gne->de', source, grads, preferred_element_type=jnp.float32)]
    unnamed x261 -> x76, local copies, waits for them, and re-layouts: 68.5 us -> 18.7 us
    all_gather x2 -> x0, blocking collectives: 30.2 us -> none  [the longest x1 15.5 us: shards(): grad_cross = lax.all_gather(cot_heads, 'seg', axis=1, tiled=True)]
  transfers between devices with their start and end apart: 21 -> 0, of which waited for: 20 -> 0; matrix products, arithmetic and copies ran while one was open for 9% -> 0% of each run, Pallas kernels for 0% -> 0%
where the time goes in v2:
time: 366 us; the launch traced here: 363 us
  Pallas kernels  344 us (94%)
  local copies, waits for them, and re-layouts  18.7 us (5%)
    pallas_call x1, Pallas kernels, reduce(): pl.pallas_call(functools.partial(reduce_kernel, nc, r), out_shape=[jax.Sh...  113 us
    pallas_call x1, Pallas kernels, gather(): pl.pallas_call(functools.partial(gather_kernel, pieces, n, 0), out_shape=...  89.1 us
    pallas_call x1, Pallas kernels, cross(): pl.pallas_call(cross_kernel, out_shape=[S((8, 768), F32), S((8, 768), F32...  63.1 us
    pallas_call x1, Pallas kernels, backward(): pl.pallas_call(backward_kernel, out_shape=[S((rows, width), BF), S((rows,...  39.9 us
    pallas_call x1, Pallas kernels, forward(): pl.pallas_call(forward_kernel, out_shape=[low, low, low, probs, low, low,...  32.1 us
    unnamed x76, local copies, waits for them, and re-layouts  18.7 us

profile of v2, /device:TPU:1, one launch (start us, length us, event | category | flops | bytes accessed | tf_op | source)
XLA Modules:
  0.0 363.4 jit_solution(5784315189034251476)
XLA Ops:
  0.7 89.1 %gather_weights.1 = (bf16[4,192,768]{2,1,0:T(8,128)(2,1)}, bf16[4,192,768]{2,1,0:T(8,128)(2,1)}, bf16[4,192,768]{2,1,0:T(8,128)(2,1)}, bf16[4,192,768]{2,1,0:T(8...) custom-call(bf16[2,192,768]{2,1,0:T(8,128)(2,1)} %refs_0_.1, ...), custom_call_target="tpu_custom_call" | custom-call | tf_op jit(solution)/shard_map/gather_weights/pallas_call | solution.py:580
  89.8 0.0 copy-start.1
  89.8 0.0 copy-start.2
  89.8 0.0 copy-start.5
  89.8 0.0 copy-start.6
  89.8 0.0 copy-start.7
  89.8 32.1 %segment_forward.1 = (bf16[512,768]{1,0:T(8,128)(2,1)}, bf16[512,768]{1,0:T(8,128)(2,1)}, bf16[512,768]{1,0:T(8,128)(2,1)}, bf16[6,4,2,128,128]{4,3,2,1,0:T(8,12...) custom-call(bf16[512,768]{1,0:T(8,128)(2,1)} %bitcast.30, ...), custom_call_target="tpu_custom_call" | custom-call | tf_op jit(solution)/shard_map/segment_forward/pallas_call | solution.py:932
  121.9 0.0 copy-done.1
  122.0 0.0 copy-done.2
  122.0 0.0 copy-done.5
  122.0 0.9 copy-done.12
  122.9 0.8 copy-done.21
  123.7 0.7 copy-done.23
  124.4 0.7 copy-done.24
  125.1 0.7 copy-done.25
  125.8 0.7 copy-done.30
  126.5 0.7 copy-done.31
  127.2 0.7 copy-done.32
  127.9 0.7 copy-done.33
  128.6 0.7 copy-done.34
  129.2 0.7 copy-done.35
  129.9 0.7 copy-done.36
  130.6 0.7 copy-done.37
  131.3 63.1 %cross_block.1 = (f32[8,768]{1,0:T(8,128)S(1)}, f32[8,768]{1,0:T(8,128)S(1)}, bf16[128,256]{1,0:T(8,128)(2,1)S(1)}, bf16[128,256]{1,0:T(8,128)(2,1)S(1)}, bf16[1...) custom-call(f32[4,768]{1,0:T(4,128)S(1)} %copy-done.30, ...), custom_call_target="tpu_custom_call" | custom-call | tf_op jit(solution)/shard_map/cross_block/pallas_call | solution.py:1294
  194.4 0.9 copy-done.3
  195.3 0.7 copy-done.8
  195.9 0.7 copy-done.10
  196.6 0.6 copy-done.13
  197.3 0.6 copy-done.15
  197.9 0.6 copy-done.17
  198.5 0.6 copy-done.19
  199.1 0.6 copy-done.26
  199.7 0.6 copy-done.28
  200.3 0.6 copy-done.29
  200.9 39.9 %segment_backward.1 = (bf16[512,768]{1,0:T(8,128)(2,1)}, bf16[512,768]{1,0:T(8,128)(2,1)}, bf16[4,2304,768]{2,1,0:T(8,128)(2,1)}, f32[16,768]{1,0:T(8,128)}) custom-call(bf16[512,768]{1,0:T(8,128)(2,1)} %bitcast.31, bf16[512,768]{1,0:T(8,128)(2,1)} %bitcast.32, f32[8,768]{1,0:T(8,128)} %copy-done.29, bf16[512,768]{1,0:T(8,128)(2,1)} %get-tuple-element.92.q, ...), custom_call_target="tpu_custom_call" | custom-call | tf_op jit(solution)/shard_map/segment_backward/pallas_call | solution.py:1094
  241.0 113.0 %reduce_grads.1 = (bf16[2304,768]{1,0:T(8,128)(2,1)}, f32[16,768]{1,0:T(8,128)}) custom-call(bf16[4,2304,768]{2,1,0:T(8,128)(2,1)} %get-tuple-element.108.g, f32[16,768]{1,0:T(8,128)} %get-tuple-element.109.vec), custom_call_target="tpu_custom_call" | custom-call | tf_op jit(solution)/shard_map/reduce_grads/pallas_call | solution.py:736
  353.9 0.0 copy-done.4
  353.9 0.0 copy-done.9
  354.0 0.0 copy-done.11
  354.0 0.0 copy-done.14
  354.0 0.0 copy-done.16
  354.0 0.0 copy-done.18
  354.0 0.0 copy-done.20
  354.0 0.0 copy-done.27
  354.0 0.0 copy-start
  354.0 2.0 copy-done
  356.0 0.8 copy-done.22
  356.8 6.4 %finish_grads.1 = (f32[2,192,768]{2,1,0:T(8,128)}, f32[2,192]{1,0:T(2,128)}, f32[2,192,768]{2,1,0:T(8,128)}, f32[2,192,768]{2,1,0:T(8,128)}, f32[2,192]{1,0:T(2,...) custom-call(bf16[2304,768]{1,0:T(8,128)(2,1)S(1)} %copy-done, ...), custom_call_target="tpu_custom_call" | custom-call | tf_op jit(solution)/shard_map/finish_grads/pallas_call | solution.py:1364
  (34 shorter events, 0.1 us)
Async XLA Ops:
  89.8 32.2 %copy-start.1 = (bf16[2,192,768]{2,1,0:T(8,128)(2,1)S(1)}, bf16[2,192,768]{2,1,0:T(8,128)(2,1)}, u32[]{:S(2)}) copy-start(bf16[2,192,768]{2,1,0:T(8,128)(2,1)} %out_w.1) | copy-start | bytes 1769476
  89.8 32.2 %copy-start.2 = (bf16[4,192,768]{2,1,0:T(8,128)(2,1)S(1)}, bf16[4,192,768]{2,1,0:T(8,128)(2,1)}, u32[]{:S(2)}) copy-start(bf16[4,192,768]{2,1,0:T(8,128)(2,1)} %get-tuple-element.90) | copy-start | bytes 3538948
  89.8 32.2 %copy-start.5 = (bf16[4,192,256]{2,1,0:T(8,128)(2,1)S(1)}, bf16[4,192,256]{2,1,0:T(8,128)(2,1)}, u32[]{:S(2)}) copy-start(bf16[4,192,256]{2,1,0:T(8,128)(2,1)} %get-tuple-element.87) | copy-start | bytes 1179652
  89.8 32.2 %copy-start.6 = (bf16[4,192,256]{2,1,0:T(8,128)(2,1)S(1)}, bf16[4,192,256]{2,1,0:T(8,128)(2,1)}, u32[]{:S(2)}) copy-start(bf16[4,192,256]{2,1,0:T(8,128)(2,1)} %get-tuple-element.88) | copy-start | bytes 1179652
  89.8 32.2 %copy-start.7 = (bf16[4,192,256]{2,1,0:T(8,128)(2,1)S(1)}, bf16[4,192,256]{2,1,0:T(8,128)(2,1)}, u32[]{:S(2)}) copy-start(bf16[4,192,256]{2,1,0:T(8,128)(2,1)} %get-tuple-element.89) | copy-start | bytes 1179652
  122.0 0.9 copy-start.12
  122.9 0.8 copy-start.21
  123.7 0.7 copy-start.23
  124.4 0.7 copy-start.24
  125.1 0.7 copy-start.25
  125.8 0.7 copy-start.30
  126.5 0.7 copy-start.31
  127.2 0.7 copy-start.32
  127.9 0.7 copy-start.33
  128.6 0.7 copy-start.34
  129.2 0.7 copy-start.35
  129.9 0.7 copy-start.36
  130.6 0.7 copy-start.37
  194.4 0.9 copy-start.3
  195.3 0.7 copy-start.8
  195.9 0.7 copy-start.10
  196.6 0.6 copy-start.13
  197.3 0.6 copy-start.15
  197.9 0.6 copy-start.17
  198.5 0.6 copy-start.19
  199.1 0.6 copy-start.26
  199.7 0.6 copy-start.28
  200.3 0.6 copy-start.29
  240.9 113.0 %copy-start.4 = (bf16[4,128,768]{2,1,0:T(8,128)(2,1)S(1)}, bf16[4,128,768]{2,1,0:T(8,128)(2,1)}, u32[]{:S(2)}) copy-start(bf16[4,128,768]{2,1,0:T(8,128)(2,1)} %copy-done.3) | copy-start | bytes 2359300
  240.9 113.0 %copy-start.9 = (bf16[128,768]{1,0:T(8,128)(2,1)S(1)}, bf16[128,768]{1,0:T(8,128)(2,1)}, u32[]{:S(2)}) copy-start(bf16[128,768]{1,0:T(8,128)(2,1)} %copy-done.8) | copy-start | bytes 589828
  240.9 113.0 %copy-start.11 = (bf16[128,768]{1,0:T(8,128)(2,1)S(1)}, bf16[128,768]{1,0:T(8,128)(2,1)}, u32[]{:S(2)}) copy-start(bf16[128,768]{1,0:T(8,128)(2,1)} %copy-done.10) | copy-start | bytes 589828
  240.9 113.0 %copy-start.14 = (f32[32,768]{1,0:T(8,128)S(1)}, f32[32,768]{1,0:T(8,128)}, u32[]{:S(2)}) copy-start(f32[32,768]{1,0:T(8,128)} %copy-done.13) | copy-start | bytes 294916
  240.9 113.0 %copy-start.16 = (bf16[128,256]{1,0:T(8,128)(2,1)S(1)}, bf16[128,256]{1,0:T(8,128)(2,1)}, u32[]{:S(2)}) copy-start(bf16[128,256]{1,0:T(8,128)(2,1)} %copy-done.15) | copy-start | bytes 196612
  240.9 113.0 %copy-start.18 = (bf16[128,256]{1,0:T(8,128)(2,1)S(1)}, bf16[128,256]{1,0:T(8,128)(2,1)}, u32[]{:S(2)}) copy-start(bf16[128,256]{1,0:T(8,128)(2,1)} %copy-done.17) | copy-start | bytes 196612
  241.0 113.0 %copy-start.20 = (bf16[128,256]{1,0:T(8,128)(2,1)S(1)}, bf16[128,256]{1,0:T(8,128)(2,1)}, u32[]{:S(2)}) copy-start(bf16[128,256]{1,0:T(8,128)(2,1)} %copy-done.19) | copy-start | bytes 196612
  241.0 113.0 %copy-start.27 = (f32[8,768]{1,0:T(8,128)S(1)}, f32[8,768]{1,0:T(8,128)}, u32[]{:S(2)}) copy-start(f32[8,768]{1,0:T(8,128)} %copy-done.26) | copy-start | bytes 73732
  354.0 2.0 copy-start
  356.0 0.8 copy-start.22

commit v3 on v2

--- a/solution.py
+++ b/solution.py
@@ -424,82 +424,42 @@
     return me, ahead, behind
 
 
-def gather_kernel(pieces, tensors, block, *refs):
-    n = tensors
-    shards, (cot, docs), refs = refs[:n], refs[n : n + 2], refs[n + 2 :]
-    outs, wins, (cot_all, docs_all), refs = refs[:n], refs[n : n + 4], refs[n + 4 : n + 6], refs[n + 6 :]
-    bounce, wbounce, (first_rows, heads, ids), refs = refs[:n], refs[n : n + 4], refs[n + 4 : n + 7], refs[n + 7 :]
-    load_sem, store_sem, own_send, own_recv, fwd_send, fwd_recv, core_send, core_recv = refs[:8]
-    wload_sem, wstore_sem, win_send, win_recv, wcore_send, wcore_recv, row_sem, all_send, all_recv, ids_send, ids_recv = refs[8:]
+def start_kernel(pieces, *refs):
+    x, (qb, vb, ob, g1, c1, ib, b2, g2, c2), refs = refs[0], refs[1:10], refs[10:]
+    shards, (cot, docs), refs = refs[:6], refs[6:8], refs[8:]
+    fulls, wins, (cot_all, docs_all), refs = refs[:6], refs[6:10], refs[10:12], refs[12:]
+    saved_o, y_o, cls_o, refs = refs[:12], refs[12], refs[13], refs[14:]
+    full, wbounce, (first_rows, heads, ids), refs = refs[:6], refs[6:10], refs[10:13], refs[13:]
+    (q_s, k_s, v_s, p_s, o_s, h_s, e_s, gp_s, x1, r1, x2, r2), y_s, refs = refs[:12], refs[12], refs[13:]
+    load_sem, link_send, link_recv, core_send, core_recv, wload_sem, store_sem, refs = *refs[:7], refs[7:]
+    win_send, win_recv, wcore_send, wcore_recv, row_sem, all_send, all_recv, ids_send, ids_recv, full_sem, out_sem = refs
+    vq, vk, vv, vo, vi, v2 = full
     d, s = place()
-    c, first, second, other = plane_peers(d, s)
-    diagonal = 3 - d
+    c = s % 2
+    z = s // 2
+    xx, yy = d % 2, d // 2
+    dx, dy, dd = 2 * yy + 1 - xx, 2 * (1 - yy) + xx, 3 - d
+    other = s + 1 - 2 * c
+    even = 1 - z % 2
+    xpeer, ypeer, zpeer = (dx, s), (dy, s), (d, s + 4 * even - 2)
+
+    def either(a, b):
+        return a * even + b * (1 - even)
+
     me, ahead, behind = everyone(d, s)
     segs = first_rows.shape[0]
+    count = len(pieces)
+    loads = [
+        pltpu.make_async_copy(shards[i].at[0], full[i].at[pl.ds(pl.multiple_of(d * shards[i].shape[1], 64), shards[i].shape[1])], load_sem.at[i])
+        for i in range(6)
+    ]
+    for cp in loads:
+        cp.start()
     row_loads = [pltpu.make_async_copy(cot.at[0, pl.ds(i * 128, 8)], first_rows.at[i], row_sem.at[i]) for i in range(segs)]
     row_loads.append(pltpu.make_async_copy(docs, ids, row_sem.at[segs]))
     for cp in row_loads:
         cp.start()
-    for cp in row_loads:
-        cp.wait()
-    heads[...] = jnp.concatenate([first_rows[i].astype(F32)[0:1] for i in range(segs)], axis=0).astype(BF)
-    greet([(i // 8, i % 8) for i in ahead])
-
-    def cols(ref):
-        half = ref.shape[-1] // 2
-        return pl.ds(pl.multiple_of(c * half, half), half)
-
-    def mine(p):
-        i, r0, rn = pieces[p]
-        return shards[i].at[block, pl.ds(r0, rn), cols(shards[i])]
-
-    def slot(p, src):
-        i, r0, rn = pieces[p]
-        return outs[i].at[src, pl.ds(r0, rn), cols(outs[i])]
-
-    count = len(pieces)
-    owns = []
-    for p in range(count):
-        a = remote(mine(p), slot(p, d), own_send.at[0, p], own_recv.at[0, p], (first, s))
-        b = remote(mine(p), slot(p, d), own_send.at[1, p], own_recv.at[1, p], (second, s))
-        a.start()
-        b.start()
-        owns.append((a, b))
-    loads = []
-    for i in range(n):
-        cp = pltpu.make_async_copy(shards[i].at[block], bounce[i], load_sem.at[i])
-        cp.start()
-        loads.append(cp)
-    stores = []
-    for i in range(n):
-        loads[i].wait()
-        cp = pltpu.make_async_copy(bounce[i], outs[i].at[d], store_sem.at[i])
-        cp.start()
-        stores.append(cp)
-    far = (diagonal, first, second)
-
-    def columns(w, dev, core):
-        width = wins[w].shape[-1]
-        at = window(dev)[0] if w < 3 else dev * width
-        return pl.ds(pl.multiple_of(at + core * (width // 2), 128), width // 2)
-
     origins = (shards[0], shards[1], shards[2], shards[4])
-    small = []
-    for k, peer in enumerate(far):
-        cp = remote(ids, docs_all.at[d], ids_send.at[k], ids_recv.at[k], (peer, s))
-        cp.start()
-        small.append(cp)
-        for w in range(4):
-            cp = remote(
-                origins[w].at[1, :, columns(w, peer, c)], wins[w].at[d, :, cols(wins[w])],
-                win_send.at[k, w], win_recv.at[k, w], (peer, s),
-            )
-            cp.start()
-            small.append(cp)
-    for j, i in enumerate(ahead):
-        cp = remote(heads, cot_all.at[me], all_send.at[j], all_recv.at[j], (i // 8, i % 8))
-        cp.start()
-        small.append(cp)
     wloads = []
     for w in range(4):
         width = wins[w].shape[-1]
@@ -507,91 +467,281 @@
         cp = pltpu.make_async_copy(origins[w].at[1, :, pl.ds(pl.multiple_of(at, 128), width)], wbounce[w], wload_sem.at[w])
         cp.start()
         wloads.append(cp)
+    greet([(i // 8, i % 8) for i in ahead])
+
+    def cols(ref):
+        half = ref.shape[-1] // 2
+        return pl.ds(pl.multiple_of(c * half, half), half)
+
+    def mine(p, h):
+        i, r0, rn = pieces[p]
+        return shards[i].at[0, pl.ds(r0 + h * (rn // 2), rn // 2), cols(shards[i])]
+
+    def slot(p, src, h):
+        i, r0, rn = pieces[p]
+        at = src * shards[i].shape[1] + r0 + h * (rn // 2)
+        return full[i].at[pl.ds(pl.multiple_of(at, 16), rn // 2), cols(full[i])]
+
+    started, shared, stores = [], [], []
+
+    def link(kind, p, src, dst, peer):
+        return remote(src, dst, link_send.at[kind, p], link_recv.at[kind, p], peer)
+
+    def go(cp):
+        cp.start()
+        started.append(cp)
+
+    def arrived(kind, p, ref):
+        link(kind, p, ref, ref, zpeer).wait_recv()
+        cp = remote(ref, ref, core_send.at[kind, p], core_recv.at[kind, p], (d, other))
+        cp.start()
+        shared.append((pieces[p][0], cp))
+        started.append(cp)
+
+    def own(p):
+        if p < count:
+            go(link(0, p, mine(p, 1), slot(p, d, 1), xpeer))
+            go(link(1, p, mine(p, 0), slot(p, d, 0), ypeer))
+
+    loaded = set()
+
+    def step(p):
+        own(p + 3)
+        if p < count:
+            i = pieces[p][0]
+            if i not in loaded:
+                loads[i].wait()
+                loaded.add(i)
+            arrived(0, p, slot(p, dx, 1))
+            arrived(1, p, slot(p, dy, 0))
+            ref = slot(p, either(d, dy), 0)
+            go(link(2, p, ref, ref, xpeer))
+            ref = slot(p, either(d, dx), 1)
+            go(link(3, p, ref, ref, ypeer))
+        if 0 <= p - 1 < count:
+            for kind, src, h in ((2, either(dx, dd), 0), (3, either(dy, dd), 1)):
+                ref = slot(p - 1, src, h)
+                arrived(kind, p - 1, ref)
+                go(link(kind + 2, p - 1, ref, ref, zpeer))
+        if 0 <= p - 2 < count:
+            arrived(4, p - 2, slot(p - 2, either(dd, dx), 0))
+            arrived(5, p - 2, slot(p - 2, either(dd, dy), 1))
+
+    ready = set()
+
+    def whole(i):
+        for j, cp in shared:
+            if j == i:
+                cp.wait_recv()
+        assert i not in ready
+        ready.add(i)
+        cp = pltpu.make_async_copy(full[i], fulls[i], full_sem.at[i])
+        cp.start()
+        stores.append(cp)
+
+    def save(n, ref):
+        cp = pltpu.make_async_copy(ref, y_o if n == 12 else saved_o[n], out_sem.at[n])
+        cp.start()
+        stores.append(cp)
+
+    rows, width = x.shape
+    nt = width // TILE
+    for p in range(3):
+        own(p)
+    at = 0
+
+    def advance(upto):
+        nonlocal at
+        while at < min(upto, count + 2):
+            step(at)
+            at += 1
+
+    last = {i: max(p for p in range(count) if pieces[p][0] == i) for i in range(6)}
+    advance(last[2] + 3)
+    for i in range(3):
+        whole(i)
+
+    for t in range(nt):
+        lanes = slice(t * TILE, t * TILE + TILE)
+        q_s[:, lanes] = (dot(x[...], vq[:, lanes]) + qb[0:1, lanes].astype(F32)).astype(BF)
+        k_s[:, lanes] = dot(x[...], vk[:, lanes]).astype(BF)
+        v_s[:, lanes] = (dot(x[...], vv[:, lanes]) + vb[0:1, lanes].astype(F32)).astype(BF)
+    for n, ref in enumerate((q_s, k_s, v_s)):
+        save(n, ref)
+    advance(last[2] + 4)
+    masks = head_masks()
+
+    def attend(hp, carry):
+        lanes = tiles(hp, 128)
+        for s in range(segs):
+            here = slice(s * 128, s * 128 + 128)
+            qs, ks, vs = q_s[here, lanes], k_s[here, lanes], v_s[here, lanes]
+            mixed = None
+            for h in range(2):
+                scores = dot_nt(qs * masks[h], ks)
+                top = jnp.max(scores, axis=-1, keepdims=True)
+                weight = jnp.exp((scores - top) * 0.125)
+                share = (weight * (1.0 / jnp.sum(weight, axis=-1, keepdims=True))).astype(BF)
+                p_s[hp, s, h] = share
+                part = dot(share, vs * masks[h])
+                mixed = part if mixed is None else mixed + part
+            o_s[here, lanes] = mixed.astype(BF)
+        return carry
+
+    pairs = width // 128
+    for g in range(pairs // 2):
+        lax.fori_loop(2 * g, 2 * g + 2, attend, 0)
+        advance(last[3] + 4 + g)
+    save(3, p_s)
+    save(4, o_s)
+    whole(3)
+
+    def out(t, carry):
+        lanes = tiles(t)
+        x1[:, lanes] = dot(o_s[...], vo[:, lanes]) + ob[0:1, lanes].astype(F32) + x[:, lanes].astype(F32)
+        return carry
+
+    lax.fori_loop(0, nt, out, 0)
+
+    def first(i, carry):
+        r = tiles(i, 64)
+        xhat, rstd = standard(x1[r, :])
+        x1[r, :] = xhat
+        r1[r, :] = jnp.broadcast_to(rstd, (64, 128))
+        hidden = xhat * g1[0:1, :].astype(F32) + c1[0:1, :].astype(F32)
+        h_s[r, :] = hidden.astype(BF)
+        x2[r, :] = hidden + b2[0:1, :].astype(F32)
+        return carry
+
+    lax.fori_loop(0, rows // 64, first, 0)
+    for n, ref in ((5, h_s), (8, x1), (9, r1)):
+        save(n, ref)
+    advance(last[4] + 3)
+    whole(4)
+
+    def ffn(t, carry):
+        lanes = tiles(t)
+        u = dot(h_s[...], vi[:, lanes]) + ib[0:1, lanes].astype(F32)
+        e, gp = gelu_parts(u)
+        e_s[:, lanes] = e.astype(BF)
+        gp_s[:, lanes] = gp.astype(BF)
+        return carry
+
+    groups = vi.shape[1] // TILE // 2
+    far = (dd, dx, dy)
+    for g in range(groups):
+        lax.fori_loop(2 * g, 2 * g + 2, ffn, 0)
+        advance(last[4] + 4 + g)
+    advance(count + 2)
+    heads_small(row_loads, first_rows, heads, segs)
+
+    def columns(w, dev, core):
+        wide = wins[w].shape[-1]
+        begin = window(dev)[0] if w < 3 else dev * wide
+        return pl.ds(pl.multiple_of(begin + core * (wide // 2), 128), wide // 2)
+
+    for k, peer in enumerate(far):
+        for w in range(4):
+            go(remote(
+                origins[w].at[1, :, columns(w, peer, c)], wins[w].at[d, :, cols(wins[w])],
+                win_send.at[k, w], win_recv.at[k, w], (peer, s),
+            ))
+        go(remote(ids, docs_all.at[d], ids_send.at[k], ids_recv.at[k], (peer, s)))
+    for j, i in enumerate(ahead):
+        go(remote(heads, cot_all.at[me], all_send.at[j], all_recv.at[j], (i // 8, i % 8)))
     for w in range(4):
         wloads[w].wait()
-        cp = pltpu.make_async_copy(wbounce[w], wins[w].at[d], wstore_sem.at[w])
+        cp = pltpu.make_async_copy(wbounce[w], wins[w].at[d], store_sem.at[w])
         cp.start()
         stores.append(cp)
     for src, dst, i in ((heads, cot_all.at[me], 4), (ids, docs_all.at[d], 5)):
-        cp = pltpu.make_async_copy(src, dst, wstore_sem.at[i])
+        cp = pltpu.make_async_copy(src, dst, store_sem.at[i])
         cp.start()
         stores.append(cp)
-    fwds, cores = [], []
-
-    def share(p, src, k):
-        cp = remote(slot(p, src), slot(p, src), core_send.at[k, p], core_recv.at[k, p], (d, other))
-        cp.start()
-        cores.append(cp)
-
-    for p in range(count):
-        got = remote(slot(p, first), slot(p, first), own_send.at[0, p], own_recv.at[0, p], (first, s))
-        got.wait_recv()
-        f = remote(slot(p, first), slot(p, first), fwd_send.at[p], fwd_recv.at[p], (second, s))
-        f.start()
-        fwds.append(f)
-        share(p, first, 0)
-        got = remote(slot(p, second), slot(p, second), own_send.at[1, p], own_recv.at[1, p], (second, s))
-        got.wait_recv()
-        share(p, second, 1)
-        if p > 0:
-            fwd_wait(p - 1, slot, fwd_send, fwd_recv, diagonal, second, s)
-            share(p - 1, diagonal, 2)
-    fwd_wait(count - 1, slot, fwd_send, fwd_recv, diagonal, second, s)
-    share(count - 1, diagonal, 2)
+    save(6, e_s)
+    save(7, gp_s)
+    whole(5)
+
+    def outer(t, carry):
+        lanes = tiles(t)
+        x2[:, lanes] += dot(e_s[...], v2[:, lanes])
+        return carry
+
+    lax.fori_loop(0, nt, outer, 0)
+
+    def second(i, carry):
+        r = tiles(i, 64)
+        xhat, rstd = standard(x2[r, :])
+        x2[r, :] = xhat
+        r2[r, :] = jnp.broadcast_to(rstd, (64, 128))
+        y_s[r, :] = (xhat * g2[0:1, :].astype(F32) + c2[0:1, :].astype(F32)).astype(BF)
+        return carry
+
+    lax.fori_loop(0, rows // 64, second, 0)
+    for n, ref in ((10, x2), (11, r2), (12, y_s)):
+        save(n, ref)
+    for s_ in range(segs):
+        cls_o[s_ : s_ + 1, :] = x2[s_ * 128 : s_ * 128 + 1, :] * g2[0:1, :].astype(F32) + c2[0:1, :].astype(F32)
+    wcores = []
     for k, peer in enumerate(far):
         for w in range(4):
             got = wins[w].at[peer, :, cols(wins[w])]
             remote(got, got, win_send.at[k, w], win_recv.at[k, w], (peer, s)).wait_recv()
             cp = remote(got, got, wcore_send.at[k, w], wcore_recv.at[k, w], (d, other))
             cp.start()
-            cores.append(cp)
+            wcores.append(cp)
         remote(ids, docs_all.at[peer], ids_send.at[k], ids_recv.at[k], (peer, s)).wait_recv()
     for j, i in enumerate(behind):
         remote(heads, cot_all.at[i], all_send.at[j], all_recv.at[j], (i // 8, i % 8)).wait_recv()
-    for cp in small:
+    for cp in started:
         cp.wait_send()
-    for a, b in owns:
-        a.wait_send()
-        b.wait_send()
-    for f in fwds:
-        f.wait_send()
-    for cp in cores:
+    for cp in wcores:
         cp.wait()
     for cp in stores:
         cp.wait()
 
 
-def fwd_wait(p, slot, fwd_send, fwd_recv, diagonal, second, s):
-    remote(slot(p, diagonal), slot(p, diagonal), fwd_send.at[p], fwd_recv.at[p], (second, s)).wait_recv()
-
-
-def gather(shards, cot, docs, collective_id):
+def heads_small(row_loads, first_rows, heads, segs):
+    for cp in row_loads:
+        cp.wait()
+    heads[...] = jnp.concatenate([first_rows[i].astype(F32)[0:1] for i in range(segs)], axis=0).astype(BF)
+
+
+def start(x, shards, cot, docs, vectors, collective_id):
+    cuts = (2, 2, 2, 1, 3, 4)
     pieces = []
     for i, w in enumerate(shards):
-        rows = w.shape[1]
-        parts = max(1, (rows * w.shape[2]) // (192 * 1536))
-        for p in range(parts):
-            pieces.append((i, p * rows // parts, rows // parts))
-    n, count = len(shards), len(pieces)
+        n = w.shape[1] // cuts[i]
+        pieces += [(i, p * n, n) for p in range(cuts[i])]
+    count = len(pieces)
     S, VM, dma = jax.ShapeDtypeStruct, pltpu.VMEM, pltpu.SemaphoreType.DMA
-    rows, width = shards[0].shape[1:]
-    segs = cot.shape[1] // 128
-    wins = [(rows, 256)] * 3 + [(rows, shards[4].shape[2] // 4)]
-    return pl.pallas_call(
-        functools.partial(gather_kernel, pieces, n, 0),
-        out_shape=[S((4,) + w.shape[1:], w.dtype) for w in shards]
+    V = pl.BlockSpec(memory_space=pltpu.VMEM)
+    part, width = shards[0].shape[1:]
+    rows = x.shape[0]
+    ff = shards[4].shape[2]
+    segs = rows // 128
+    wins = [(part, 256)] * 3 + [(part, ff // 4)]
+    low, full, wide, col = ((rows, width), BF), ((rows, width), F32), ((rows, ff), BF), ((rows, 128), F32)
+    saved = [low, low, low, ((width // 128, segs, 2, 128, 128), BF), low, low, wide, wide, full, col, full, col, low]
+    outs = pl.pallas_call(
+        functools.partial(start_kernel, pieces),
+        out_shape=[S((4 * w.shape[1], w.shape[2]), w.dtype) for w in shards]
         + [S((4,) + w, BF) for w in wins]
-        + [S((32, segs, width), BF), S((4,) + docs.shape, docs.dtype)],
-        in_specs=[ANY] * (n + 2),
-        out_specs=[ANY] * (n + 6),
-        scratch_shapes=[VM(w.shape[1:], w.dtype) for w in shards]
+        + [S((32, segs, width), BF), S((4,) + docs.shape, docs.dtype)]
+        + [S(*t) for t in saved]
+        + [S((segs, width), F32)],
+        in_specs=[V] * 10 + [ANY] * 8,
+        out_specs=[ANY] * 25 + [V],
+        scratch_shapes=[VM((4 * w.shape[1], w.shape[2]), w.dtype) for w in shards]
         + [VM(w, BF) for w in wins]
         + [VM((segs, 8, width), BF), VM((segs, width), BF), VM(docs.shape, docs.dtype)]
-        + [dma((n,)), dma((n,)), dma((2, count)), dma((2, count)), dma((count,)), dma((count,)), dma((3, count)), dma((3, count))]
-        + [dma((4,)), dma((6,)), dma((3, 4)), dma((3, 4)), dma((3, 4)), dma((3, 4)), dma((segs + 1,)), dma((31,)), dma((31,)), dma((3,)), dma((3,))],
-        compiler_params=pltpu.CompilerParams(collective_id=collective_id, has_side_effects=True),
-        name="gather_weights",
-    )(*shards, cot, docs)
+        + [VM(*t) for t in saved]
+        + [dma((6,)), dma((6, count)), dma((6, count)), dma((6, count)), dma((6, count)), dma((4,)), dma((6,))]
+        + [dma((3, 4)), dma((3, 4)), dma((3, 4)), dma((3, 4)), dma((segs + 1,)), dma((31,)), dma((31,)), dma((3,)), dma((3,)), dma((6,)), dma((13,))],
+        compiler_params=pltpu.CompilerParams(collective_id=collective_id, has_side_effects=True, vmem_limit_bytes=67043328),
+        name="gather_forward",
+    )(x, *vectors, *shards, cot, docs)
+    return outs[:6], outs[6:10], outs[10], outs[11], outs[12:24], outs[24], outs[25]
 
 
 def add_into(dst, a, b, rows):
@@ -760,7 +910,7 @@
             pltpu.VMEM((5,) + vec.shape, vec.dtype),
             dma((5,)), dma((5,)),
         ],
-        compiler_params=pltpu.CompilerParams(collective_id=collective_id, has_side_effects=True, vmem_limit_bytes=60 << 20),
+        compiler_params=pltpu.CompilerParams(collective_id=collective_id, has_side_effects=True, vmem_limit_bytes=67043328),
         name="reduce_grads",
     )(g, vec)
 
@@ -811,141 +961,6 @@
 
 def row_sum(v):
     return jnp.sum(v, axis=0, keepdims=True)
-
-
-def forward_kernel(x, wq, wk, wv, wo, wi, w2, qb, vb, ob, g1, c1, ib, b2, g2, c2,
-                   q_o, k_o, v_o, p_o, o_o, hb_o, e_o, gp_o, x1_o, r1_o, x2_o, r2_o, y_o, cls_o,
-                   vq, vk, vv, vo, vi, v2, x1, x2, in_sem, p_s, e_s, gp_s, out_sem):
-    loads = [
-        pltpu.make_async_copy(src, dst, in_sem.at[i])
-        for i, (src, dst) in enumerate(((wq, vq), (wk, vk), (wv, vv), (wo, vo), (wi, vi), (w2, v2)))
-    ]
-    for cp in loads:
-        cp.start()
-    rows, width = x.shape
-    segs = rows // 128
-    nt = width // TILE
-    loads[0].wait()
-    loads[1].wait()
-    loads[2].wait()
-
-    def qkv(t, carry):
-        lanes = tiles(t)
-        q_o[:, lanes] = (dot(x[...], vq[:, lanes]) + qb[0:1, lanes].astype(F32)).astype(BF)
-        k_o[:, lanes] = dot(x[...], vk[:, lanes]).astype(BF)
-        v_o[:, lanes] = (dot(x[...], vv[:, lanes]) + vb[0:1, lanes].astype(F32)).astype(BF)
-        return carry
-
-    lax.fori_loop(0, nt, qkv, 0)
-    masks = head_masks()
-
-    def attend(hp, carry):
-        lanes = tiles(hp, 128)
-        for s in range(segs):
-            here = slice(s * 128, s * 128 + 128)
-            qs, ks, vs = q_o[here, lanes], k_o[here, lanes], v_o[here, lanes]
-            mixed = None
-            for h in range(2):
-                scores = dot_nt(qs * masks[h], ks)
-                top = jnp.max(scores, axis=-1, keepdims=True)
-                weight = jnp.exp((scores - top) * 0.125)
-                share = (weight * (1.0 / jnp.sum(weight, axis=-1, keepdims=True))).astype(BF)
-                p_s[hp, s, h] = share
-                part = dot(share, vs * masks[h])
-                mixed = part if mixed is None else mixed + part
-            o_o[here, lanes] = mixed.astype(BF)
-        return carry
-
-    lax.fori_loop(0, width // 128, attend, 0)
-    p_copy = pltpu.make_async_copy(p_s, p_o, out_sem.at[0])
-    p_copy.start()
-    loads[3].wait()
-
-    def out(t, carry):
-        lanes = tiles(t)
-        x1[:, lanes] = dot(o_o[...], vo[:, lanes]) + ob[0:1, lanes].astype(F32) + x[:, lanes].astype(F32)
-        return carry
-
-    lax.fori_loop(0, nt, out, 0)
-
-    def first(i, carry):
-        r = tiles(i, 64)
-        xhat, rstd = standard(x1[r, :])
-        x1_o[r, :] = xhat
-        r1_o[r, :] = jnp.broadcast_to(rstd, (64, 128))
-        hidden = xhat * g1[0:1, :].astype(F32) + c1[0:1, :].astype(F32)
-        hb_o[r, :] = hidden.astype(BF)
-        x2[r, :] = hidden + b2[0:1, :].astype(F32)
-        return carry
-
-    lax.fori_loop(0, rows // 64, first, 0)
-    loads[4].wait()
-    loads[5].wait()
-
-    def ffn(t, carry):
-        lanes = tiles(t)
-        u = dot(hb_o[...], vi[:, lanes]) + ib[0:1, lanes].astype(F32)
-        e, gp = gelu_parts(u)
-        e_s[:, lanes] = e.astype(BF)
-        gp_s[:, lanes] = gp.astype(BF)
-        return carry
-
-    lax.fori_loop(0, vi.shape[1] // TILE, ffn, 0)
-    e_copy = pltpu.make_async_copy(e_s, e_o, out_sem.at[1])
-    gp_copy = pltpu.make_async_copy(gp_s, gp_o, out_sem.at[2])
-    e_copy.start()
-    gp_copy.start()
-
-    def outer(t, carry):
-        lanes = tiles(t)
-        x2[:, lanes] += dot(e_s[...], v2[:, lanes])
-        return carry
-
-    lax.fori_loop(0, nt, outer, 0)
-
-    def second(i, carry):
-        r = tiles(i, 64)
-        xhat, rstd = standard(x2[r, :])
-        x2_o[r, :] = xhat
-        r2_o[r, :] = jnp.broadcast_to(rstd, (64, 128))
-        y_o[r, :] = (xhat * g2[0:1, :].astype(F32) + c2[0:1, :].astype(F32)).astype(BF)
-        return carry
-
-    lax.fori_loop(0, rows // 64, second, 0)
-    for s in range(segs):
-        cls_o[s : s + 1, :] = x2_o[s * 128 : s * 128 + 1, :] * g2[0:1, :].astype(F32) + c2[0:1, :].astype(F32)
-    p_copy.wait()
-    e_copy.wait()
-    gp_copy.wait()
-
-
-def forward(x, weights, vectors):
-    rows, width = x.shape
-    ff = weights[4].shape[1]
-    segs, pairs = rows // 128, width // 128
-    S = jax.ShapeDtypeStruct
-    V = pl.BlockSpec(memory_space=pltpu.VMEM)
-    low, full = S((rows, width), BF), S((rows, width), F32)
-    wide = S((rows, ff), BF)
-    probs = S((pairs, segs, 2, 128, 128), BF)
-    col = S((rows, 128), F32)
-    return pl.pallas_call(
-        forward_kernel,
-        out_shape=[low, low, low, probs, low, low, wide, wide, full, col, full, col, low, S((segs, width), F32)],
-        in_specs=[V] + [ANY] * 6 + [V] * 9,
-        out_specs=[V, V, V, ANY, V, V, ANY, ANY, V, V, V, V, V, V],
-        scratch_shapes=[pltpu.VMEM(w.shape, BF) for w in weights]
-        + [pltpu.VMEM((rows, width), F32)] * 2
-        + [
-            pltpu.SemaphoreType.DMA((6,)),
-            pltpu.VMEM(probs.shape, BF),
-            pltpu.VMEM(wide.shape, BF),
-            pltpu.VMEM(wide.shape, BF),
-            pltpu.SemaphoreType.DMA((3,)),
-        ],
-        compiler_params=pltpu.CompilerParams(vmem_limit_bytes=60 << 20),
-        name="segment_forward",
-    )(x, *weights, *vectors)
 
 
 def backward_kernel(x, cot, dcl, q, k, v, p, o, hb, e, gp, x1, r1, x2, r2, y, z, wq, wk, wv, wo, wi, w2, g1, g2,
@@ -1108,7 +1123,7 @@
             pltpu.SemaphoreType.DMA((9,)),
             pltpu.SemaphoreType.DMA((2,)),
         ],
-        compiler_params=pltpu.CompilerParams(vmem_limit_bytes=63 << 20),
+        compiler_params=pltpu.CompilerParams(vmem_limit_bytes=67043328),
         name="segment_backward",
     )(x, cot, dcl, q, k, v, p, o, hb, e, gp, x1, r1, x2, r2, y, z, *weights, g1, g2)
 
@@ -1307,7 +1322,7 @@
             dma((6,)), dma((31,)), dma((31,)),
             dma((4,)), dma((4,)), dma((4,)), dma((4,)), dma((3,)), dma((3,)), dma((3,)), dma((3,)), dma((2,)),
         ],
-        compiler_params=pltpu.CompilerParams(collective_id=collective_id, has_side_effects=True, vmem_limit_bytes=48 << 20),
+        compiler_params=pltpu.CompilerParams(collective_id=collective_id, has_side_effects=True, vmem_limit_bytes=67043328),
         name="cross_block",
     )(cls, emb, cot_all, docs, wq, wk, wv, wi, out_w, outer_w, *vectors)
 
@@ -1370,7 +1385,7 @@
         in_specs=[V] * 12,
         out_specs=[V] * 16,
         scratch_shapes=[pltpu.VMEM((8, 768), F32)],
-        compiler_params=pltpu.CompilerParams(vmem_limit_bytes=48 << 20),
+        compiler_params=pltpu.CompilerParams(vmem_limit_bytes=67043328),
         name="finish_grads",
     )(red, vec, emb, xw, hw, ow, e, dqkv, du, da, df, vec1)
 
@@ -1398,11 +1413,8 @@
 ):
     weights = (query_weight, key_weight, value_weight, out_weight, inner_weight, outer_weight)
     vectors = (query_bias, value_bias, out_bias, first_gain, first_shift, inner_bias, outer_bias, second_gain, second_shift)
-    gathered = gather(weights, cotangent, doc_ids, 1)
-    full = [w.reshape(-1, w.shape[-1]) for w in gathered[:6]]
-    windows = [w.reshape(-1, w.shape[-1]) for w in gathered[6:10]]
-    cot_all, docs = gathered[10:]
-    *saved, y, cls = forward(inputs[0], full, vectors)
+    full, windows, cot_all, docs, saved, y, cls = start(inputs[0], weights, cotangent, doc_ids, vectors, 1)
+    windows = [w.reshape(-1, w.shape[-1]) for w in windows]
     crossed = cross(cls, segment_embed, cot_all, docs, *windows, out_weight, outer_weight, vectors, 2)
     grad, output, packed, vec = backward(
         inputs[0], cotangent[0], crossed[1], saved, y, crossed[0], full, first_gain, second_gain

time: 366 us -> 323 us (0.88)
  Pallas kernels: 344 us -> 322 us
  local copies, waits for them, and re-layouts: 18.7 us -> 0 us
    pallas_call x2 -> x1, Pallas kernels: 121 us -> 92.2 us  [start(): pl.pallas_call(functools.partial(start_kernel, pieces), out_shape=[S((4 *...]
    unnamed x76 -> x0, local copies, waits for them, and re-layouts: 18.7 us -> none
where the time goes in v3:
time: 323 us
  Pallas kernels  322 us (100%)
    pallas_call x1, Pallas kernels, reduce(): pl.pallas_call(functools.partial(reduce_kernel, nc, r), out_shape=[jax.Sh...  115 us
    pallas_call x1, Pallas kernels, start(): pl.pallas_call(functools.partial(start_kernel, pieces), out_shape=[S((4 *...  92.2 us
    pallas_call x1, Pallas kernels, cross(): pl.pallas_call(cross_kernel, out_shape=[S((8, 768), F32), S((8, 768), F32...  66.2 us
    pallas_call x1, Pallas kernels, backward(): pl.pallas_call(backward_kernel, out_shape=[S((rows, width), BF), S((rows,...  40 us
    pallas_call x1, Pallas kernels, finish(): pl.pallas_call(finish_kernel, out_shape=[square, line, square, square, li...  9.15 us

profile of v3, /device:TPU:1, one launch (start us, length us, event | category | flops | bytes accessed | tf_op | source)
XLA Modules:
  0.0 322.9 jit_solution(13942424004165195772)
XLA Ops:
  0.7 92.2 %gather_forward.1 = (bf16[768,768]{1,0:T(8,128)(2,1)}, bf16[768,768]{1,0:T(8,128)(2,1)}, bf16[768,768]{1,0:T(8,128)(2,1)}, bf16[768,768]{1,0:T(8,128)(2,1)}, bf1...) custom-call(bf16[512,768]{1,0:T(8,128)(2,1)} %bitcast.8, ...), custom_call_target="tpu_custom_call" | custom-call | tf_op jit(solution)/shard_map/gather_forward/pallas_call | solution.py:726
  92.9 66.2 %cross_block.1 = (f32[8,768]{1,0:T(8,128)}, f32[8,768]{1,0:T(8,128)}, bf16[128,256]{1,0:T(8,128)(2,1)}, bf16[128,256]{1,0:T(8,128)(2,1)}, bf16[128,256]{1,0:T(8,...) custom-call(f32[4,768]{1,0:T(4,128)} %get-tuple-element.78.cls, ...), custom_call_target="tpu_custom_call" | custom-call | tf_op jit(solution)/shard_map/cross_block/pallas_call | solution.py:1309
  159.1 40.0 %segment_backward.1 = (bf16[512,768]{1,0:T(8,128)(2,1)}, bf16[512,768]{1,0:T(8,128)(2,1)}, bf16[4,2304,768]{2,1,0:T(8,128)(2,1)}, f32[16,768]{1,0:T(8,128)}) custom-call(bf16[512,768]{1,0:T(8,128)(2,1)} %bitcast.9, bf16[512,768]{1,0:T(8,128)(2,1)} %bitcast.10, f32[8,768]{1,0:T(8,128)} %get-tuple-element.85.dcl, bf16[512,768]{1,0:T(8,128)(2,1)} %get-tuple-element.86.q, ...), custom_call_target="tpu_custom_call" | custom-call | tf_op jit(solution)/shard_map/segment_backward/pallas_call | solution.py:1109
  199.0 114.5 %reduce_grads.1 = (bf16[2304,768]{1,0:T(8,128)(2,1)}, f32[16,768]{1,0:T(8,128)}) custom-call(bf16[4,2304,768]{2,1,0:T(8,128)(2,1)} %get-tuple-element.108.g, f32[16,768]{1,0:T(8,128)} %get-tuple-element.109.vec), custom_call_target="tpu_custom_call" | custom-call | tf_op jit(solution)/shard_map/reduce_grads/pallas_call | solution.py:886
  313.6 9.1 %finish_grads.1 = (f32[2,192,768]{2,1,0:T(8,128)}, f32[2,192]{1,0:T(2,128)}, f32[2,192,768]{2,1,0:T(8,128)}, f32[2,192,768]{2,1,0:T(8,128)}, f32[2,192]{1,0:T(2,...) custom-call(bf16[2304,768]{1,0:T(8,128)(2,1)} %get-tuple-element.110, ...), custom_call_target="tpu_custom_call" | custom-call | tf_op jit(solution)/shard_map/finish_grads/pallas_call | solution.py:1379

commit v4 on v3

--- a/solution.py
+++ b/solution.py
@@ -424,15 +424,18 @@
     return me, ahead, behind
 
 
+AHEAD, LAG2, LAG4 = 3, 2, 4
+
+
 def start_kernel(pieces, *refs):
     x, (qb, vb, ob, g1, c1, ib, b2, g2, c2), refs = refs[0], refs[1:10], refs[10:]
-    shards, (cot, docs), refs = refs[:6], refs[6:8], refs[8:]
-    fulls, wins, (cot_all, docs_all), refs = refs[:6], refs[6:10], refs[10:12], refs[12:]
+    shards, docs, refs = refs[:6], refs[6], refs[7:]
+    fulls, wins, docs_all, refs = refs[:6], refs[6:10], refs[10], refs[11:]
     saved_o, y_o, cls_o, refs = refs[:12], refs[12], refs[13], refs[14:]
-    full, wbounce, (first_rows, heads, ids), refs = refs[:6], refs[6:10], refs[10:13], refs[13:]
+    full, wbounce, ids, refs = refs[:6], refs[6:10], refs[10], refs[11:]
     (q_s, k_s, v_s, p_s, o_s, h_s, e_s, gp_s, x1, r1, x2, r2), y_s, refs = refs[:12], refs[12], refs[13:]
     load_sem, link_send, link_recv, core_send, core_recv, wload_sem, store_sem, refs = *refs[:7], refs[7:]
-    win_send, win_recv, wcore_send, wcore_recv, row_sem, all_send, all_recv, ids_send, ids_recv, full_sem, out_sem = refs
+    win_send, win_recv, wcore_send, wcore_recv, ids_send, ids_recv, full_sem, out_sem = refs
     vq, vk, vv, vo, vi, v2 = full
     d, s = place()
     c = s % 2
@@ -446,8 +449,7 @@
     def either(a, b):
         return a * even + b * (1 - even)
 
-    me, ahead, behind = everyone(d, s)
-    segs = first_rows.shape[0]
+    segs = x.shape[0] // 128
     count = len(pieces)
     loads = [
         pltpu.make_async_copy(shards[i].at[0], full[i].at[pl.ds(pl.multiple_of(d * shards[i].shape[1], 64), shards[i].shape[1])], load_sem.at[i])
@@ -455,10 +457,8 @@
     ]
     for cp in loads:
         cp.start()
-    row_loads = [pltpu.make_async_copy(cot.at[0, pl.ds(i * 128, 8)], first_rows.at[i], row_sem.at[i]) for i in range(segs)]
-    row_loads.append(pltpu.make_async_copy(docs, ids, row_sem.at[segs]))
-    for cp in row_loads:
-        cp.start()
+    ids_load = pltpu.make_async_copy(docs, ids, load_sem.at[6])
+    ids_load.start()
     origins = (shards[0], shards[1], shards[2], shards[4])
     wloads = []
     for w in range(4):
@@ -467,7 +467,7 @@
         cp = pltpu.make_async_copy(origins[w].at[1, :, pl.ds(pl.multiple_of(at, 128), width)], wbounce[w], wload_sem.at[w])
         cp.start()
         wloads.append(cp)
-    greet([(i // 8, i % 8) for i in ahead])
+    greet([xpeer, ypeer, (dd, s), zpeer, (d, other)])
 
     def cols(ref):
         half = ref.shape[-1] // 2
@@ -475,12 +475,13 @@
 
     def mine(p, h):
         i, r0, rn = pieces[p]
-        return shards[i].at[0, pl.ds(r0 + h * (rn // 2), rn // 2), cols(shards[i])]
+        n = rn // 4
+        return shards[i].at[0, pl.ds(pl.multiple_of(r0 + (2 * h + c) * n, 16), n)]
 
     def slot(p, src, h):
         i, r0, rn = pieces[p]
-        at = src * shards[i].shape[1] + r0 + h * (rn // 2)
-        return full[i].at[pl.ds(pl.multiple_of(at, 16), rn // 2), cols(full[i])]
+        n = rn // 4
+        return full[i].at[pl.ds(pl.multiple_of(src * shards[i].shape[1] + r0 + (2 * h + c) * n, 16), n)]
 
     started, shared, stores = [], [], []
 
@@ -505,8 +506,25 @@
 
     loaded = set()
 
+    far = (dd, dx, dy)
+
+    def columns(w, dev, core):
+        wide = wins[w].shape[-1]
+        begin = window(dev)[0] if w < 3 else dev * wide
+        return pl.ds(pl.multiple_of(begin + core * (wide // 2), 128), wide // 2)
+
+    def cross_needs():
+        ids_load.wait()
+        for k, peer in enumerate(far):
+            for w in range(4):
+                go(remote(
+                    origins[w].at[1, :, columns(w, peer, c)], wins[w].at[d, :, cols(wins[w])],
+                    win_send.at[k, w], win_recv.at[k, w], (peer, s),
+                ))
+            go(remote(ids, docs_all.at[d], ids_send.at[k], ids_recv.at[k], (peer, s)))
+
     def step(p):
-        own(p + 3)
+        own(p + AHEAD)
         if p < count:
             i = pieces[p][0]
             if i not in loaded:
@@ -518,14 +536,18 @@
             go(link(2, p, ref, ref, xpeer))
             ref = slot(p, either(d, dx), 1)
             go(link(3, p, ref, ref, ypeer))
-        if 0 <= p - 1 < count:
+            if p == count - 1:
+                cross_needs()
+        n = p - LAG2
+        if 0 <= n < count:
             for kind, src, h in ((2, either(dx, dd), 0), (3, either(dy, dd), 1)):
-                ref = slot(p - 1, src, h)
-                arrived(kind, p - 1, ref)
-                go(link(kind + 2, p - 1, ref, ref, zpeer))
-        if 0 <= p - 2 < count:
-            arrived(4, p - 2, slot(p - 2, either(dd, dx), 0))
-            arrived(5, p - 2, slot(p - 2, either(dd, dy), 1))
+                ref = slot(n, src, h)
+                arrived(kind, n, ref)
+                go(link(kind + 2, n, ref, ref, zpeer))
+        n = p - LAG4
+        if 0 <= n < count:
+            arrived(4, n, slot(n, either(dd, dx), 0))
+            arrived(5, n, slot(n, either(dd, dy), 1))
 
     ready = set()
 
@@ -546,18 +568,18 @@
 
     rows, width = x.shape
     nt = width // TILE
-    for p in range(3):
+    for p in range(AHEAD):
         own(p)
     at = 0
 
     def advance(upto):
         nonlocal at
-        while at < min(upto, count + 2):
+        while at < min(upto, count + LAG4):
             step(at)
             at += 1
 
     last = {i: max(p for p in range(count) if pieces[p][0] == i) for i in range(6)}
-    advance(last[2] + 3)
+    advance(last[2] + LAG4 + 1)
     for i in range(3):
         whole(i)
 
@@ -568,7 +590,7 @@
         v_s[:, lanes] = (dot(x[...], vv[:, lanes]) + vb[0:1, lanes].astype(F32)).astype(BF)
     for n, ref in enumerate((q_s, k_s, v_s)):
         save(n, ref)
-    advance(last[2] + 4)
+    advance(last[2] + LAG4 + 2)
     masks = head_masks()
 
     def attend(hp, carry):
@@ -591,9 +613,10 @@
     pairs = width // 128
     for g in range(pairs // 2):
         lax.fori_loop(2 * g, 2 * g + 2, attend, 0)
-        advance(last[3] + 4 + g)
+        advance(last[2] + LAG4 + 3 + g)
     save(3, p_s)
     save(4, o_s)
+    advance(last[3] + LAG4 + 1)
     whole(3)
 
     def out(t, carry):
@@ -616,7 +639,7 @@
     lax.fori_loop(0, rows // 64, first, 0)
     for n, ref in ((5, h_s), (8, x1), (9, r1)):
         save(n, ref)
-    advance(last[4] + 3)
+    advance(last[4] + LAG4 + 1)
     whole(4)
 
     def ffn(t, carry):
@@ -628,33 +651,16 @@
         return carry
 
     groups = vi.shape[1] // TILE // 2
-    far = (dd, dx, dy)
     for g in range(groups):
         lax.fori_loop(2 * g, 2 * g + 2, ffn, 0)
-        advance(last[4] + 4 + g)
-    advance(count + 2)
-    heads_small(row_loads, first_rows, heads, segs)
-
-    def columns(w, dev, core):
-        wide = wins[w].shape[-1]
-        begin = window(dev)[0] if w < 3 else dev * wide
-        return pl.ds(pl.multiple_of(begin + core * (wide // 2), 128), wide // 2)
-
-    for k, peer in enumerate(far):
-        for w in range(4):
-            go(remote(
-                origins[w].at[1, :, columns(w, peer, c)], wins[w].at[d, :, cols(wins[w])],
-                win_send.at[k, w], win_recv.at[k, w], (peer, s),
-            ))
-        go(remote(ids, docs_all.at[d], ids_send.at[k], ids_recv.at[k], (peer, s)))
-    for j, i in enumerate(ahead):
-        go(remote(heads, cot_all.at[me], all_send.at[j], all_recv.at[j], (i // 8, i % 8)))
+        advance(last[4] + LAG4 + 2 + g)
+    advance(count + LAG4)
     for w in range(4):
         wloads[w].wait()
         cp = pltpu.make_async_copy(wbounce[w], wins[w].at[d], store_sem.at[w])
         cp.start()
         stores.append(cp)
-    for src, dst, i in ((heads, cot_all.at[me], 4), (ids, docs_all.at[d], 5)):
+    for src, dst, i in ((ids, docs_all.at[d], 4),):
         cp = pltpu.make_async_copy(src, dst, store_sem.at[i])
         cp.start()
         stores.append(cp)
@@ -691,8 +697,6 @@
             cp.start()
             wcores.append(cp)
         remote(ids, docs_all.at[peer], ids_send.at[k], ids_recv.at[k], (peer, s)).wait_recv()
-    for j, i in enumerate(behind):
-        remote(heads, cot_all.at[i], all_send.at[j], all_recv.at[j], (i // 8, i % 8)).wait_recv()
     for cp in started:
         cp.wait_send()
     for cp in wcores:
@@ -701,14 +705,8 @@
         cp.wait()
 
 
-def heads_small(row_loads, first_rows, heads, segs):
-    for cp in row_loads:
-        cp.wait()
-    heads[...] = jnp.concatenate([first_rows[i].astype(F32)[0:1] for i in range(segs)], axis=0).astype(BF)
-
-
-def start(x, shards, cot, docs, vectors, collective_id):
-    cuts = (2, 2, 2, 1, 3, 4)
+def start(x, shards, docs, vectors, collective_id):
+    cuts = (1, 1, 1, 1, 3, 4)
     pieces = []
     for i, w in enumerate(shards):
         n = w.shape[1] // cuts[i]
@@ -727,21 +725,21 @@
         functools.partial(start_kernel, pieces),
         out_shape=[S((4 * w.shape[1], w.shape[2]), w.dtype) for w in shards]
         + [S((4,) + w, BF) for w in wins]
-        + [S((32, segs, width), BF), S((4,) + docs.shape, docs.dtype)]
+        + [S((4,) + docs.shape, docs.dtype)]
         + [S(*t) for t in saved]
         + [S((segs, width), F32)],
-        in_specs=[V] * 10 + [ANY] * 8,
-        out_specs=[ANY] * 25 + [V],
+        in_specs=[V] * 10 + [ANY] * 7,
+        out_specs=[ANY] * 24 + [V],
         scratch_shapes=[VM((4 * w.shape[1], w.shape[2]), w.dtype) for w in shards]
         + [VM(w, BF) for w in wins]
-        + [VM((segs, 8, width), BF), VM((segs, width), BF), VM(docs.shape, docs.dtype)]
+        + [VM(docs.shape, docs.dtype)]
         + [VM(*t) for t in saved]
-        + [dma((6,)), dma((6, count)), dma((6, count)), dma((6, count)), dma((6, count)), dma((4,)), dma((6,))]
-        + [dma((3, 4)), dma((3, 4)), dma((3, 4)), dma((3, 4)), dma((segs + 1,)), dma((31,)), dma((31,)), dma((3,)), dma((3,)), dma((6,)), dma((13,))],
+        + [dma((7,)), dma((6, count)), dma((6, count)), dma((6, count)), dma((6, count)), dma((4,)), dma((5,))]
+        + [dma((3, 4)), dma((3, 4)), dma((3, 4)), dma((3, 4)), dma((3,)), dma((3,)), dma((6,)), dma((13,))],
         compiler_params=pltpu.CompilerParams(collective_id=collective_id, has_side_effects=True, vmem_limit_bytes=67043328),
         name="gather_forward",
-    )(x, *vectors, *shards, cot, docs)
-    return outs[:6], outs[6:10], outs[10], outs[11], outs[12:24], outs[24], outs[25]
+    )(x, *vectors, *shards, docs)
+    return outs[:6], outs[6:10], outs[10], outs[11:23], outs[23], outs[24]
 
 
 def add_into(dst, a, b, rows):
@@ -1128,11 +1126,11 @@
     )(x, cot, dcl, q, k, v, p, o, hb, e, gp, x1, r1, x2, r2, y, z, *weights, g1, g2)
 
 
-def cross_kernel(cls, emb, cot_all, docs, wq, wk, wv, wi, out_w, outer_w,
+def cross_kernel(cls, emb, docs, cot, wq, wk, wv, wi, out_w, outer_w,
                  qb, vb, ob, g1, c1, ib, b2, g2, c2,
                  z_o, dcl_o, xw_o, hw_o, ow_o, e_o, dqkv_o, du_o, da_o, df_o, vec_o, emb_o,
                  vq, vk, vv, vi, vo, v2, heads, xall, rows_s, p_s, dqkv_s, du_s, send1, got1, send2, got2,
-                 in_sem, all_send, all_recv, s1, r1, s2, r2, qs_send, qs_recv, us_send, us_recv, o_sem):
+                 in_sem, all_send, all_recv, first_rows, cots, cot_all, row_sem, cot_send, cot_recv, s1, r1, s2, r2, qs_send, qs_recv, us_send, us_recv, o_sem):
     d, s = place()
     c, first, second, other = plane_peers(d, s)
     start, off = window(d)
@@ -1151,6 +1149,9 @@
     ]
     for cp in loads:
         cp.start()
+    row_loads = [pltpu.make_async_copy(cot.at[0, pl.ds(i * 128, 8)], first_rows.at[i], row_sem.at[i]) for i in range(4)]
+    for cp in row_loads:
+        cp.start()
     vo[pl.ds(pl.multiple_of(192 * (1 - d % 2), 64), 64), :] = jnp.zeros((64, 768), BF)
     pick = lax.broadcasted_iota(jnp.int32, (8, 32), 0) + 4 * s == lax.broadcasted_iota(jnp.int32, (8, 32), 1)
     position = dot(pick.astype(BF), emb[...])
@@ -1162,10 +1163,14 @@
         cp.start()
         sent.append(cp)
     xall[me] = heads[...]
-    dys = []
-    for i in range(32):
-        rows_s[4 * i : 4 * i + 4, :] = cot_all[i].astype(F32)
-    dy = rows_s[...]
+    for cp in row_loads:
+        cp.wait()
+    cots[...] = jnp.concatenate([first_rows[i].astype(F32)[0:1] for i in range(4)], axis=0).astype(BF)
+    for j, i in enumerate(ahead):
+        cp = remote(cots, cot_all.at[me], cot_send.at[j], cot_recv.at[j], (i // 8, i % 8))
+        cp.start()
+        sent.append(cp)
+    cot_all[me] = cots[...]
     ids = lax.broadcasted_iota(jnp.int32, (8, 128), 1) // 32 * 1024
     ids = ids.astype(F32)
     lane = lax.broadcasted_iota(jnp.int32, (32, 128), 1)
@@ -1240,6 +1245,11 @@
     own = lax.broadcasted_iota(jnp.int32, (8, 128), 0) + 4 * me == lax.broadcasted_iota(jnp.int32, (8, 128), 1)
     own = own.astype(BF)
     z_o[...] = dot(own, z)
+    for j, i in enumerate(behind):
+        remote(cots, cot_all.at[i], cot_send.at[j], cot_recv.at[j], (i // 8, i % 8)).wait_recv()
+    for i in range(32):
+        rows_s[4 * i : 4 * i + 4, :] = cot_all[i].astype(F32)
+    dy = rows_s[...]
     vec_o[6:7, :] = row_sum(dy * xhat2)
     vec_o[7:8, :] = row_sum(dy)
     dr2 = standard_back(dy * vector(g2), xhat2, rstd2)
@@ -1301,7 +1311,7 @@
         cp.wait()
 
 
-def cross(cls, emb, cot_all, docs, wq, wk, wv, wi, out_w, outer_w, vectors, collective_id):
+def cross(cls, emb, cot, docs, wq, wk, wv, wi, out_w, outer_w, vectors, collective_id):
     S = jax.ShapeDtypeStruct
     V = pl.BlockSpec(memory_space=pltpu.VMEM)
     VM, dma = pltpu.VMEM, pltpu.SemaphoreType.DMA
@@ -1312,7 +1322,7 @@
             S((8, 768), F32), S((8, 768), F32), win, win, win, low, four, four, low, low,
             S((8, 768), F32), S((32, 768), F32),
         ],
-        in_specs=[V] * 4 + [ANY] * 6 + [V] * 9,
+        in_specs=[V] * 3 + [ANY] * 7 + [V] * 9,
         out_specs=[V] * 6 + [ANY] * 2 + [V] * 4,
         scratch_shapes=[
             VM((768, 256), BF), VM((768, 256), BF), VM((768, 256), BF), VM((768, 768), BF), VM((256, 768), BF), VM((768, 768), BF),
@@ -1320,11 +1330,12 @@
             VM((4, 128, 768), BF), VM((4, 128, 768), BF),
             VM((4, 128, 768), BF), VM((4, 128, 768), BF), VM((4, 128, 768), BF), VM((4, 128, 768), BF),
             dma((6,)), dma((31,)), dma((31,)),
+            VM((4, 8, 768), BF), VM((4, 768), BF), VM((32, 4, 768), BF), dma((4,)), dma((31,)), dma((31,)),
             dma((4,)), dma((4,)), dma((4,)), dma((4,)), dma((3,)), dma((3,)), dma((3,)), dma((3,)), dma((2,)),
         ],
         compiler_params=pltpu.CompilerParams(collective_id=collective_id, has_side_effects=True, vmem_limit_bytes=67043328),
         name="cross_block",
-    )(cls, emb, cot_all, docs, wq, wk, wv, wi, out_w, outer_w, *vectors)
+    )(cls, emb, docs, cot, wq, wk, wv, wi, out_w, outer_w, *vectors)
 
 
 def finish_kernel(red, vec, emb, xw, hw, ow, e, dqkv, du, da, df, vec1,
@@ -1413,9 +1424,9 @@
 ):
     weights = (query_weight, key_weight, value_weight, out_weight, inner_weight, outer_weight)
     vectors = (query_bias, value_bias, out_bias, first_gain, first_shift, inner_bias, outer_bias, second_gain, second_shift)
-    full, windows, cot_all, docs, saved, y, cls = start(inputs[0], weights, cotangent, doc_ids, vectors, 1)
+    full, windows, docs, saved, y, cls = start(inputs[0], weights, doc_ids, vectors, 1)
     windows = [w.reshape(-1, w.shape[-1]) for w in windows]
-    crossed = cross(cls, segment_embed, cot_all, docs, *windows, out_weight, outer_weight, vectors, 2)
+    crossed = cross(cls, segment_embed, cotangent, docs, *windows, out_weight, outer_weight, vectors, 2)
     grad, output, packed, vec = backward(
         inputs[0], cotangent[0], crossed[1], saved, y, crossed[0], full, first_gain, second_gain
     )

time: 323 us -> 305 us (0.944)
  Pallas kernels: 322 us -> 304 us
    pallas_call x1, Pallas kernels: 92.2 us -> 71.6 us  [start(): pl.pallas_call(functools.partial(start_kernel, pieces), out_shape=[S((4 *...]
where the time goes in v4:
time: 305 us
  Pallas kernels  304 us (100%)
    pallas_call x1, Pallas kernels, reduce(): pl.pallas_call(functools.partial(reduce_kernel, nc, r), out_shape=[jax.Sh...  115 us
    pallas_call x1, Pallas kernels, start(): pl.pallas_call(functools.partial(start_kernel, pieces), out_shape=[S((4 *...  71.6 us
    pallas_call x1, Pallas kernels, cross(): pl.pallas_call(cross_kernel, out_shape=[S((8, 768), F32), S((8, 768), F32...  69 us
    pallas_call x1, Pallas kernels, backward(): pl.pallas_call(backward_kernel, out_shape=[S((rows, width), BF), S((rows,...  40 us
    pallas_call x1, Pallas kernels, finish(): pl.pallas_call(finish_kernel, out_shape=[square, line, square, square, li...  9.15 us

profile of v4, /device:TPU:1, one launch (start us, length us, event | category | flops | bytes accessed | tf_op | source)
XLA Modules:
  0.0 305.1 jit_solution(8515142296880843384)
XLA Ops:
  0.7 71.6 %gather_forward.1 = (bf16[768,768]{1,0:T(8,128)(2,1)}, bf16[768,768]{1,0:T(8,128)(2,1)}, bf16[768,768]{1,0:T(8,128)(2,1)}, bf16[768,768]{1,0:T(8,128)(2,1)}, bf1...) custom-call(bf16[512,768]{1,0:T(8,128)(2,1)} %bitcast.8, ...), custom_call_target="tpu_custom_call" | custom-call | tf_op jit(solution)/shard_map/gather_forward/pallas_call | solution.py:724
  72.3 69.0 %cross_block.1 = (f32[8,768]{1,0:T(8,128)}, f32[8,768]{1,0:T(8,128)}, bf16[128,256]{1,0:T(8,128)(2,1)}, bf16[128,256]{1,0:T(8,128)(2,1)}, bf16[128,256]{1,0:T(8,...) custom-call(f32[4,768]{1,0:T(4,128)} %get-tuple-element.77.cls, ...), custom_call_target="tpu_custom_call" | custom-call | tf_op jit(solution)/shard_map/cross_block/pallas_call | solution.py:1319
  141.3 40.0 %segment_backward.1 = (bf16[512,768]{1,0:T(8,128)(2,1)}, bf16[512,768]{1,0:T(8,128)(2,1)}, bf16[4,2304,768]{2,1,0:T(8,128)(2,1)}, f32[16,768]{1,0:T(8,128)}) custom-call(bf16[512,768]{1,0:T(8,128)(2,1)} %bitcast.9, bf16[512,768]{1,0:T(8,128)(2,1)} %bitcast.10, f32[8,768]{1,0:T(8,128)} %get-tuple-element.83.dcl, bf16[512,768]{1,0:T(8,128)(2,1)} %get-tuple-element.84.q, ...), custom_call_target="tpu_custom_call" | custom-call | tf_op jit(solution)/shard_map/segment_backward/pallas_call | solution.py:1107
  181.3 114.5 %reduce_grads.1 = (bf16[2304,768]{1,0:T(8,128)(2,1)}, f32[16,768]{1,0:T(8,128)}) custom-call(bf16[4,2304,768]{2,1,0:T(8,128)(2,1)} %get-tuple-element.106.g, f32[16,768]{1,0:T(8,128)} %get-tuple-element.107.vec), custom_call_target="tpu_custom_call" | custom-call | tf_op jit(solution)/shard_map/reduce_grads/pallas_call | solution.py:884
  295.8 9.1 %finish_grads.1 = (f32[2,192,768]{2,1,0:T(8,128)}, f32[2,192]{1,0:T(2,128)}, f32[2,192,768]{2,1,0:T(8,128)}, f32[2,192,768]{2,1,0:T(8,128)}, f32[2,192]{1,0:T(2,...) custom-call(bf16[2304,768]{1,0:T(8,128)(2,1)} %get-tuple-element.108, ...), custom_call_target="tpu_custom_call" | custom-call | tf_op jit(solution)/shard_map/finish_grads/pallas_call | solution.py:1390

commit v5 on v4

--- a/solution.py
+++ b/solution.py
@@ -743,7 +743,7 @@
 
 
 def add_into(dst, a, b, rows):
-    step = 48
+    step = 48 if rows % 48 == 0 else 32
 
     def body(i, carry):
         r = pl.ds(pl.multiple_of(i * step, 16), step)
@@ -751,166 +751,6 @@
         return carry
 
     lax.fori_loop(0, rows // step, body, 0)
-
-
-def reduce_kernel(nc, r, g, vec, out, vec_out, own, recv0, recv1, recv2, recv3, recv4, fin, load_sem, out_sem,
-                  send0, rcv0, send1, rcv1, send2, rcv2, send3, rcv3, send4, rcv4, send5, rcv5, send6, rcv6, send7, rcv7, vsum, vgot, vsend, vrcv):
-    d, s = place()
-    c, first, second, other = plane_peers(d, s)
-    x, y = d % 2, d // 2
-    a = x * (1 - c) + y * c
-    b = y * (1 - c) + x * c
-    z = s // 2
-    z0, z1 = z % 2, z // 2
-    znear = (z + 1 - 2 * z0) * 2 + c
-    zfar = (z + 2 - 4 * z1) * 2 + c
-    h, q = r // 2, r // 4
-    greet([(first, s), (second, s), (d, other), (d, znear), (d, zfar)])
-
-    def quarter(aa, bb):
-        return aa * (1 + c) + bb * (2 - c)
-
-    def rows(core, k):
-        return pl.ds(pl.multiple_of(core * (nc * r) + k * r, 16), r)
-
-    started = []
-
-    def go(cp):
-        cp.start()
-        started.append(cp)
-
-    loads = []
-    for k in range(nc):
-        go(remote(g.at[:, rows(1 - c, k), :], recv0.at[k], send0.at[k], rcv0.at[k], (d, other)))
-        cp = pltpu.make_async_copy(g.at[:, rows(c, k), :], own.at[k], load_sem.at[k])
-        cp.start()
-        loads.append(cp)
-
-    def arrived(ref, sem):
-        pltpu.make_async_copy(ref, ref, sem).wait()
-
-    def piece(k, i0, i1):
-        return fin.at[c, k, pl.ds(pl.multiple_of(i0 * h + i1 * q, 16), q), :]
-
-    outs = []
-
-    def stage(t, k):
-        if t == 1:
-            arrived(recv0.at[k], rcv0.at[k])
-            loads[k].wait()
-            for bb in range(2):
-                away = quarter(1 - a, bb)
-                add_into(own.at[k, away], own.at[k, away], recv0.at[k, away], r)
-                go(remote(own.at[k, away], recv1.at[k, bb], send1.at[k, bb], rcv1.at[k, bb], (first, s)))
-            for bb in range(2):
-                keep = quarter(a, bb)
-                add_into(own.at[k, keep], own.at[k, keep], recv0.at[k, keep], r)
-        elif t == 2:
-            for bb in range(2):
-                arrived(recv1.at[k, bb], rcv1.at[k, bb])
-            away, keep = quarter(a, 1 - b), quarter(a, b)
-            add_into(own.at[k, away], own.at[k, away], recv1.at[k, 1 - b], r)
-            go(remote(own.at[k, away], recv2.at[k], send2.at[k], rcv2.at[k], (second, s)))
-            add_into(own.at[k, keep], own.at[k, keep], recv1.at[k, b], r)
-        elif t == 3:
-            arrived(recv2.at[k], rcv2.at[k])
-            keep = quarter(a, b)
-            away = pl.ds(pl.multiple_of((1 - z0) * h, 16), h)
-            mine = pl.ds(pl.multiple_of(z0 * h, 16), h)
-            add_into(own.at[k, keep, away], own.at[k, keep, away], recv2.at[k, away], h)
-            go(remote(own.at[k, keep, away], recv3.at[k], send3.at[k], rcv3.at[k], (d, znear)))
-            add_into(own.at[k, keep, mine], own.at[k, keep, mine], recv2.at[k, mine], h)
-        elif t == 4:
-            arrived(recv3.at[k], rcv3.at[k])
-            keep = quarter(a, b)
-            away = pl.ds(pl.multiple_of(z0 * h + (1 - z1) * q, 16), q)
-            mine = pl.ds(pl.multiple_of(z0 * h + z1 * q, 16), q)
-            raway = pl.ds(pl.multiple_of((1 - z1) * q, 16), q)
-            rmine = pl.ds(pl.multiple_of(z1 * q, 16), q)
-            add_into(own.at[k, keep, away], own.at[k, keep, away], recv3.at[k, raway], q)
-            go(remote(own.at[k, keep, away], recv4.at[k], send4.at[k], rcv4.at[k], (d, zfar)))
-            add_into(own.at[k, keep, mine], own.at[k, keep, mine], recv3.at[k, rmine], q)
-        elif t == 5:
-            arrived(recv4.at[k], rcv4.at[k])
-            keep = quarter(a, b)
-            mine = pl.ds(pl.multiple_of(z0 * h + z1 * q, 16), q)
-            add_into(piece(k, z0, z1), own.at[k, keep, mine], recv4.at[k], q)
-            go(remote(piece(k, z0, z1), piece(k, z0, z1), send5.at[k], rcv5.at[k], (d, zfar)))
-        elif t == 6:
-            arrived(piece(k, z0, 1 - z1), rcv5.at[k])
-            half = fin.at[c, k, pl.ds(pl.multiple_of(z0 * h, 16), h), :]
-            go(remote(half, half, send6.at[k], rcv6.at[k], (d, znear)))
-        elif t == 7:
-            half = fin.at[c, k, pl.ds(pl.multiple_of((1 - z0) * h, 16), h), :]
-            arrived(half, rcv6.at[k])
-            go(remote(fin.at[c, k], fin.at[c, k], send7.at[k], rcv7.at[k], (d, other)))
-            cp = pltpu.make_async_copy(fin.at[c, k], out.at[rows(c, k), :], out_sem.at[0, k])
-            cp.start()
-            outs.append(cp)
-        elif t == 8:
-            arrived(fin.at[1 - c, k], rcv7.at[k])
-            cp = pltpu.make_async_copy(fin.at[1 - c, k], out.at[rows(1 - c, k), :], out_sem.at[1, k])
-            cp.start()
-            outs.append(cp)
-
-    hops = [(d, other), (first, s), (second, s), (d, znear), (d, zfar)]
-    vsum[0] = vec[...]
-
-    def vector_hop(j):
-        if j > 0:
-            arrived(vgot.at[j - 1], vrcv.at[j - 1])
-            vsum[j] = vsum[j - 1] + vgot[j - 1]
-        if j < 5:
-            go(remote(vsum.at[j], vgot.at[j], vsend.at[j], vrcv.at[j], hops[j]))
-
-    for slot in range(nc + 8):
-        for t in range(8, 0, -1):
-            k = slot - (t - 1)
-            if 0 <= k < nc:
-                stage(t, k)
-        if slot < 6:
-            vector_hop(slot)
-    vec_out[...] = vsum[5]
-    for cp in started:
-        cp.wait_send()
-    for cp in outs:
-        cp.wait()
-
-
-def reduce(g, vec, nc, collective_id):
-    _, total, width = g.shape
-    r = total // 2 // nc
-    dma = pltpu.SemaphoreType.DMA
-    return pl.pallas_call(
-        functools.partial(reduce_kernel, nc, r),
-        out_shape=[jax.ShapeDtypeStruct((total, width), g.dtype), jax.ShapeDtypeStruct(vec.shape, vec.dtype)],
-        in_specs=[ANY, pl.BlockSpec(memory_space=pltpu.VMEM)],
-        out_specs=[ANY, pl.BlockSpec(memory_space=pltpu.VMEM)],
-        scratch_shapes=[
-            pltpu.VMEM((nc, 4, r, width), g.dtype),
-            pltpu.VMEM((nc, 4, r, width), g.dtype),
-            pltpu.VMEM((nc, 2, r, width), g.dtype),
-            pltpu.VMEM((nc, r, width), g.dtype),
-            pltpu.VMEM((nc, r // 2, width), g.dtype),
-            pltpu.VMEM((nc, r // 4, width), g.dtype),
-            pltpu.VMEM((2, nc, r, width), g.dtype),
-            dma((nc,)),
-            dma((2, nc)),
-            dma((nc,)), dma((nc,)),
-            dma((nc, 2)), dma((nc, 2)),
-            dma((nc,)), dma((nc,)),
-            dma((nc,)), dma((nc,)),
-            dma((nc,)), dma((nc,)),
-            dma((nc,)), dma((nc,)),
-            dma((nc,)), dma((nc,)),
-            dma((nc,)), dma((nc,)),
-            pltpu.VMEM((6,) + vec.shape, vec.dtype),
-            pltpu.VMEM((5,) + vec.shape, vec.dtype),
-            dma((5,)), dma((5,)),
-        ],
-        compiler_params=pltpu.CompilerParams(collective_id=collective_id, has_side_effects=True, vmem_limit_bytes=67043328),
-        name="reduce_grads",
-    )(g, vec)
 
 
 TILE = 256
@@ -961,99 +801,273 @@
     return jnp.sum(v, axis=0, keepdims=True)
 
 
-def backward_kernel(x, cot, dcl, q, k, v, p, o, hb, e, gp, x1, r1, x2, r2, y, z, wq, wk, wv, wo, wi, w2, g1, g2,
-                    dx_o, y_o, g_o, vec_o,
-                    vq, vk, vv, vo, vi, v2, e_s, gp_s, p_s, gs, dr2, acc, df, ht, da, do, dq, dk, dv, in_sem, out_sem):
-    loads = [
-        pltpu.make_async_copy(src, dst, in_sem.at[i])
-        for i, (src, dst) in enumerate(
-            ((w2, v2), (e, e_s), (gp, gp_s), (wi, vi), (wo, vo), (p, p_s), (wq, vq), (wk, vk), (wv, vv))
-        )
-    ]
+CHUNKS = [("rows", 0), ("cols", 0), ("rows", 1), ("cols", 1), ("rows", 2), ("cols", 2), ("mats", 3), ("mats", 0), ("mats", 1), ("mats", 2)]
+
+
+def backward_kernel(dcl, z, g1, g2, x, cot, q, k, v, p, o, hb, e, gp, x1, r1, x2, r2, y, wq, wk, wv, wo, wi, w2, *refs):
+    (dx_o, y_o, outer_o, inner_o, mats_o, vec_o), refs = refs[:6], refs[6:]
+    (xs, ds_, qs_, ks_, vs_, p_s, os_, hs, e_s, gp_s, x1s, r1s, acc, r2s, ys), refs = refs[:15], refs[15:]
+    (vi, v2, df, ht, vecs, g_rows, g_cols, g_mats), refs = refs[:8], refs[8:]
+    bufs, refs = refs[:18], refs[18:]
+    in_sem, w_sem, res_sem, out_sem, vsum, vgot, vsend, vrcv, send, recv = refs
+    dev, s = place()
+    c, first, second, other = plane_peers(dev, s)
+    px, py = dev % 2, dev // 2
+    a = px * (1 - c) + py * c
+    b = py * (1 - c) + px * c
+    z_at = s // 2
+    z0, z1 = z_at % 2, z_at // 2
+    znear = (z_at + 1 - 2 * z0) * 2 + c
+    zfar = (z_at + 2 - 4 * z1) * 2 + c
+    order = [(cot, ds_), (y, ys), (x2, acc), (r2, r2s), (hb, hs), (w2, v2), (e, e_s), (gp, gp_s), (wi, vi),
+             (x1, x1s), (r1, r1s), (o, os_), (p, p_s), (q, qs_), (k, ks_), (v, vs_), (x, xs)]
+    loads = [pltpu.make_async_copy(src, dst, in_sem.at[i]) for i, (src, dst) in enumerate(order)]
     for cp in loads:
         cp.start()
-    rows, width = x.shape
+    greet([(first, s), (second, s), (dev, other), (dev, znear), (dev, zfar)])
+    rows, width = xs.shape
     segs, nt = rows // 128, width // TILE
-    ff = vi.shape[1]
     share = width // 4
-    vec_o[...] = jnp.zeros_like(vec_o)
-
-    def second(i, carry):
+    started, outs, results = [], [], []
+
+    def go(cp):
+        cp.start()
+        started.append(cp)
+
+    def arrived(ref, sem):
+        pltpu.make_async_copy(ref, ref, sem).wait()
+
+    families = {"rows": 0, "cols": 1, "mats": 2}
+
+    def part(n, core, quarters):
+        kind, i = CHUNKS[n]
+        if kind == "rows":
+            return g_rows.at[quarters, pl.ds(pl.multiple_of(i * 256 + core * 128, 128), 128), :]
+        ref = g_cols if kind == "cols" else g_mats
+        half = ref.shape[-1] // 2
+        return ref.at[i, quarters, :, pl.ds(pl.multiple_of(core * half, 128), half)]
+
+    def buf(n, j):
+        kind, i = CHUNKS[n]
+        ref = bufs[families[kind] * 6 + j]
+        return ref.at[i] if j < 5 else ref.at[:, i]
+
+    def size(n):
+        return 128 if CHUNKS[n][0] == "rows" else 192
+
+    def own(n, quarter):
+        return part(n, c, quarter)
+
+    def fin(n, core, at=0, count=None):
+        kind, i = CHUNKS[n]
+        count = size(n) if count is None else count
+        return bufs[families[kind] * 6 + 5].at[core, i, pl.ds(pl.multiple_of(at, 16), count), :]
+
+    def quarter(aa, bb):
+        return aa * (1 + c) + bb * (2 - c)
+
+    def offer(n):
+        go(remote(part(n, 1 - c, slice(None)), buf(n, 0), send.at[0, n], recv.at[0, n], (dev, other)))
+
+    def write(n, core, i):
+        kind, at = CHUNKS[n]
+        src = bufs[families[kind] * 6 + 5].at[core, at]
+        if kind == "rows":
+            pairs_ = [(src, outer_o.at[pl.ds(pl.multiple_of(at * 256 + core * 128, 128), 128), :])]
+        elif kind == "mats":
+            pairs_ = [(src, mats_o.at[at, :, pl.ds(pl.multiple_of(core * 384, 128), 384)])]
+        else:
+            pairs_ = [
+                (src.at[:, j * 256 : j * 256 + 256], inner_o.at[:, pl.ds(pl.multiple_of((2 * core + j) * 768 + at * 256, 128), 256)])
+                for j in range(2)
+            ]
+        for j, (left, right) in enumerate(pairs_):
+            cp = pltpu.make_async_copy(left, right, out_sem.at[i, j, n])
+            cp.start()
+            outs.append(cp)
+
+    def stage(t, n):
+        r = size(n)
+        h, f = r // 2, r // 4
+        if t == 1:
+            got = buf(n, 0)
+            arrived(got, recv.at[0, n])
+            for bb in range(2):
+                away = quarter(1 - a, bb)
+                add_into(own(n, away), own(n, away), got.at[away], r)
+                go(remote(own(n, away), buf(n, 1).at[bb], send.at[1 + bb, n], recv.at[1 + bb, n], (first, s)))
+            for bb in range(2):
+                keep = quarter(a, bb)
+                add_into(own(n, keep), own(n, keep), got.at[keep], r)
+        elif t == 2:
+            got = buf(n, 1)
+            for bb in range(2):
+                arrived(got.at[bb], recv.at[1 + bb, n])
+            away, keep = quarter(a, 1 - b), quarter(a, b)
+            add_into(own(n, away), own(n, away), got.at[1 - b], r)
+            go(remote(own(n, away), buf(n, 2), send.at[3, n], recv.at[3, n], (second, s)))
+            add_into(own(n, keep), own(n, keep), got.at[b], r)
+        elif t == 3:
+            got = buf(n, 2)
+            arrived(got, recv.at[3, n])
+            keep = own(n, quarter(a, b))
+            away = pl.ds(pl.multiple_of((1 - z0) * h, 16), h)
+            mine = pl.ds(pl.multiple_of(z0 * h, 16), h)
+            add_into(keep.at[away], keep.at[away], got.at[away], h)
+            go(remote(keep.at[away], buf(n, 3), send.at[4, n], recv.at[4, n], (dev, znear)))
+            add_into(keep.at[mine], keep.at[mine], got.at[mine], h)
+        elif t == 4:
+            got = buf(n, 3)
+            arrived(got, recv.at[4, n])
+            keep = own(n, quarter(a, b))
+            away = pl.ds(pl.multiple_of(z0 * h + (1 - z1) * f, 16), f)
+            mine = pl.ds(pl.multiple_of(z0 * h + z1 * f, 16), f)
+            add_into(keep.at[away], keep.at[away], got.at[pl.ds(pl.multiple_of((1 - z1) * f, 16), f)], f)
+            go(remote(keep.at[away], buf(n, 4), send.at[5, n], recv.at[5, n], (dev, zfar)))
+            add_into(keep.at[mine], keep.at[mine], got.at[pl.ds(pl.multiple_of(z1 * f, 16), f)], f)
+        elif t == 5:
+            got = buf(n, 4)
+            arrived(got, recv.at[5, n])
+            mine = own(n, quarter(a, b)).at[pl.ds(pl.multiple_of(z0 * h + z1 * f, 16), f)]
+            done = fin(n, c, z0 * h + z1 * f, f)
+            add_into(done, mine, got, f)
+            go(remote(done, done, send.at[6, n], recv.at[6, n], (dev, zfar)))
+        elif t == 6:
+            arrived(fin(n, c, z0 * h + (1 - z1) * f, f), recv.at[6, n])
+            half = fin(n, c, z0 * h, h)
+            go(remote(half, half, send.at[7, n], recv.at[7, n], (dev, znear)))
+        elif t == 7:
+            arrived(fin(n, c, (1 - z0) * h, h), recv.at[7, n])
+            go(remote(fin(n, c), fin(n, c), send.at[8, n], recv.at[8, n], (dev, other)))
+            write(n, c, 0)
+        elif t == 8:
+            arrived(fin(n, 1 - c), recv.at[8, n])
+            write(n, 1 - c, 1)
+
+    nc = len(CHUNKS)
+
+    def slot(i):
+        for t in range(8, 0, -1):
+            n = i - (t - 1)
+            if 0 <= n < nc:
+                stage(t, n)
+
+    vecs[...] = jnp.zeros_like(vecs)
+    for i in range(4):
+        loads[i].wait()
+
+    def norm2(i, carry):
         gain_sum, shift_sum, bias_sum = carry
         r = tiles(i, 64)
-        dy, out = cot[r, :].astype(F32), y[r, :].astype(F32)
+        dy, out = ds_[r, :].astype(F32), ys[r, :].astype(F32)
         at = lax.broadcasted_iota(jnp.int32, (64, 1), 0) + i * 64
-        for s in range(segs):
-            dy = jnp.where(at == s * 128, dcl[s : s + 1, :], dy)
-            out = jnp.where(at == s * 128, z[s : s + 1, :], out)
-        y_o[r, :] = out.astype(BF)
-        xhat = x2[r, :]
-        back = standard_back(dy * g2[0:1, :].astype(F32), xhat, r2[r, 0:1])
-        dr2[r, :] = back
+        for j in range(segs):
+            dy = jnp.where(at == j * 128, dcl[j : j + 1, :], dy)
+            out = jnp.where(at == j * 128, z[j : j + 1, :], out)
+        ys[r, :] = out.astype(BF)
+        xhat = acc[r, :]
+        back = standard_back(dy * g2[0:1, :].astype(F32), xhat, r2s[r, 0:1])
+        acc[r, :] = back
         low = back.astype(BF)
         df[r, :] = low
         return (gain_sum + row_sum(dy * xhat), shift_sum + row_sum(dy), bias_sum + row_sum(low.astype(F32)))
 
     zero = jnp.zeros((1, width), F32)
-    sums = lax.fori_loop(0, rows // 64, second, (zero, zero, zero))
-    vec_o[6:7, :], vec_o[7:8, :], vec_o[5:6, :] = sums
-    ht[...] = hb[...].T
-    acc[...] = dr2[...]
-    for i in range(4):
+    sums = lax.fori_loop(0, rows // 64, norm2, (zero, zero, zero))
+    vecs[6:7, :], vecs[7:8, :], vecs[5:6, :] = sums
+    results.append(pltpu.make_async_copy(ys, y_o, res_sem.at[0]))
+    results[0].start()
+    loads[4].wait()
+    ht[...] = hs[...].T
+    for i in range(5, 9):
         loads[i].wait()
 
-    def ffn(t, carry):
-        wide = tiles(t)
-        block, lanes = t // nt, tiles(t % nt)
-        de = dot_nt(df[...], v2[wide, :]).astype(BF).astype(F32)
-        du = (de * gp_s[:, wide].astype(F32)).astype(BF)
-        vec_o[pl.ds(8 + block, 1), lanes] = row_sum(du.astype(F32))
-        back = dot_tn(e_s[:, wide], df[...])
-        gs[block, pl.ds(pl.multiple_of(8 * share + (t % nt) * TILE, TILE), TILE), :] = back.astype(BF)
-        inner = dot(ht[...], du).astype(BF)
-        for d in range(4):
-            gs[d, pl.ds(pl.multiple_of(4 * share + block * share, 64), share), lanes] = inner[d * share : d * share + share]
-        acc[...] += dot_nt(du, vi[:, wide])
-        return carry
-
-    lax.fori_loop(0, ff // TILE, ffn, 0)
-    half = 4 * share
-    copies = [pltpu.make_async_copy(gs.at[:, half:, :], g_o.at[:, half:, :], out_sem.at[0])]
-    copies[0].start()
-
-    def first(i, carry):
+    def ffn(j):
+        def body(block, carry):
+            wide = tiles(block * nt + j)
+            lanes = slice(j * TILE, j * TILE + TILE)
+            de = dot_nt(df[...], v2[wide, :]).astype(BF).astype(F32)
+            du = (de * gp_s[:, wide].astype(F32)).astype(BF)
+            vecs[pl.ds(8 + block, 1), lanes] = row_sum(du.astype(F32))
+            g_rows[block, lanes, :] = dot_tn(e_s[:, wide], df[...]).astype(BF)
+            inner = dot(ht[...], du).astype(BF)
+            for i in range(4):
+                g_cols[j, i, :, tiles(block)] = inner[i * share : i * share + share]
+            acc[...] += dot_nt(du, vi[:, wide])
+            return carry
+
+        return body
+
+    lax.fori_loop(0, 4, ffn(0), 0)
+    offer(0)
+    offer(1)
+    lax.fori_loop(0, 2, ffn(1), 0)
+    slot(0)
+    lax.fori_loop(2, 4, ffn(1), 0)
+    offer(2)
+    offer(3)
+    slot(1)
+    lax.fori_loop(0, 2, ffn(2), 0)
+    slot(2)
+    lax.fori_loop(2, 4, ffn(2), 0)
+    offer(4)
+    offer(5)
+    wloads = [
+        pltpu.make_async_copy(src, v2.at[i * width : i * width + width], w_sem.at[i])
+        for i, src in enumerate((wo, wq, wk, wv))
+    ]
+    for cp in wloads:
+        cp.start()
+    slot(3)
+    for i in range(9, 17):
+        loads[i].wait()
+
+    def norm1(i, carry):
         gain_sum, shift_sum, bias_sum = carry
         r = tiles(i, 64)
         dh = acc[r, :]
-        xhat = x1[r, :]
-        back = standard_back(dh * g1[0:1, :].astype(F32), xhat, r1[r, 0:1])
-        dr2[r, :] = back
+        xhat = x1s[r, :]
+        back = standard_back(dh * g1[0:1, :].astype(F32), xhat, r1s[r, 0:1])
+        acc[r, :] = back
         low = back.astype(BF)
-        da[r, :] = low
+        df[r, :] = low
         return (gain_sum + row_sum(dh * xhat), shift_sum + row_sum(dh), bias_sum + row_sum(low.astype(F32)))
 
-    sums = lax.fori_loop(0, rows // 64, first, (zero, zero, zero))
-    vec_o[3:4, :], vec_o[4:5, :], vec_o[2:3, :] = sums
-    loads[4].wait()
-    do[...] = dot_nt(da[...], vo[...]).astype(BF)
-
-    def spread(at, lhs, rhs):
-        back = dot_tn(lhs, rhs).astype(BF)
-        for d in range(4):
-            gs[d, at * share : at * share + share, :] = back[d * share : d * share + share]
-
-    spread(3, o[...], da[...])
-    loads[5].wait()
+    sums = lax.fori_loop(0, rows // 64, norm1, (zero, zero, zero))
+    vecs[3:4, :], vecs[4:5, :], vecs[2:3, :] = sums
+    ht[...] = os_[...].T
+
+    def weights(at, rhs):
+        def body(t, carry):
+            lanes = tiles(t)
+            back = dot(ht[...], rhs[:, lanes]).astype(BF)
+            for i in range(4):
+                g_mats[at, i, :, lanes] = back[i * share : i * share + share]
+            return carry
+
+        lax.fori_loop(0, nt, body, 0)
+
+    weights(3, df)
+    offer(6)
+    slot(4)
+    wloads[0].wait()
+
+    def mixed(t, carry):
+        lanes = tiles(t)
+        ds_[:, lanes] = dot_nt(df[...], v2[lanes, :]).astype(BF)
+        return carry
+
+    lax.fori_loop(0, nt, mixed, 0)
     masks = head_masks()
 
     def attend(hp, carry):
         lanes = tiles(hp, 128)
-        for s in range(segs):
-            here = slice(s * 128, s * 128 + 128)
-            qs, ks, vs, dos = q[here, lanes], k[here, lanes], v[here, lanes], do[here, lanes]
+        for j in range(segs):
+            here = slice(j * 128, j * 128 + 128)
+            qs, ks, vs, dos = qs_[here, lanes], ks_[here, lanes], vs_[here, lanes], ds_[here, lanes]
             dqs = dks = dvs = 0.0
             for h in range(2):
-                pl_ = p_s[hp, s, h]
+                pl_ = p_s[hp, j, h]
                 pf = pl_.astype(F32)
                 dom = dos * masks[h]
                 dp = dot_nt(dom, vs).astype(BF).astype(F32)
@@ -1061,69 +1075,94 @@
                 dqs += dot(ds, ks * masks[h])
                 dks += dot_tn(ds, qs * masks[h])
                 dvs += dot_tn(pl_, dom)
-            dq[here, lanes] = (dqs * 0.125).astype(BF)
-            dk[here, lanes] = (dks * 0.125).astype(BF)
-            dv[here, lanes] = dvs.astype(BF)
+            qs_[here, lanes] = (dqs * 0.125).astype(BF)
+            ks_[here, lanes] = (dks * 0.125).astype(BF)
+            vs_[here, lanes] = dvs.astype(BF)
         return carry
 
-    lax.fori_loop(0, width // 128, attend, 0)
-    vec_o[0:1, :] = row_sum(dq[...].astype(F32))
-    vec_o[1:2, :] = row_sum(dv[...].astype(F32))
-    ht[...] = x[...].T
-    for i in range(6, 9):
-        loads[i].wait()
-
-    def weights(at, rhs):
-        back = dot(ht[...], rhs[...]).astype(BF)
-        for d in range(4):
-            gs[d, at * share : at * share + share, :] = back[d * share : d * share + share]
-
-    weights(0, dq)
-    weights(1, dk)
-    weights(2, dv)
-    copies.append(pltpu.make_async_copy(gs.at[:, :half, :], g_o.at[:, :half, :], out_sem.at[1]))
-    copies[1].start()
+    lax.fori_loop(0, 3, attend, 0)
+    slot(5)
+    lax.fori_loop(3, width // 128, attend, 0)
+    vecs[0:1, :] = row_sum(qs_[...].astype(F32))
+    vecs[1:2, :] = row_sum(vs_[...].astype(F32))
+    ht[...] = xs[...].T
+    weights(0, qs_)
+    offer(7)
+    slot(6)
+    weights(1, ks_)
+    offer(8)
+    weights(2, vs_)
+    offer(9)
+    hops = [(dev, other), (first, s), (second, s), (dev, znear), (dev, zfar)]
+    vsum[0] = vecs[...]
+
+    def vector_hop(j):
+        if j > 0:
+            arrived(vgot.at[j - 1], vrcv.at[j - 1])
+            vsum[j] = vsum[j - 1] + vgot[j - 1]
+        if j < 5:
+            go(remote(vsum.at[j], vgot.at[j], vsend.at[j], vrcv.at[j], hops[j]))
+
+    slot(7)
+    vector_hop(0)
+    for i in range(1, 4):
+        wloads[i].wait()
 
     def source(t, carry):
         r = tiles(t)
-        dx = dr2[:, r] + dot_nt(dq[...], vq[r, :]) + dot_nt(dk[...], vk[r, :]) + dot_nt(dv[...], vv[r, :])
-        dx_o[:, r] = dx.astype(BF)
+        dx = acc[:, r]
+        for i, g in enumerate((qs_, ks_, vs_)):
+            dx += dot_nt(g[...], v2[pl.ds(pl.multiple_of((i + 1) * width + t * TILE, TILE), TILE), :])
+        xs[:, r] = dx.astype(BF)
         return carry
 
     lax.fori_loop(0, nt, source, 0)
-    for cp in copies:
+    results.append(pltpu.make_async_copy(xs, dx_o, res_sem.at[1]))
+    results[1].start()
+    for i in range(8, nc + 8):
+        slot(i)
+        if i < 13:
+            vector_hop(i - 7)
+    vec_o[...] = vsum[5]
+    for cp in started:
+        cp.wait_send()
+    for cp in outs + results:
         cp.wait()
 
 
-def backward(x, cot, dcl, saved, y, z, weights, g1, g2):
+def backward(x, cot, dcl, saved, y, z, weights, g1, g2, collective_id):
     q, k, v, p, o, hb, e, gp, x1, r1, x2, r2 = saved
     rows, width = x.shape
     ff = weights[4].shape[1]
-    S = jax.ShapeDtypeStruct
+    share, nc = width // 4, len(CHUNKS)
+    S, VM, dma = jax.ShapeDtypeStruct, pltpu.VMEM, pltpu.SemaphoreType.DMA
     V = pl.BlockSpec(memory_space=pltpu.VMEM)
-    packed = S((4, width // 4 * 4 + 2 * ff // 4, width), BF)
-    VM = pltpu.VMEM
-    low, full = VM((rows, width), BF), VM((rows, width), F32)
+    arrays = (x, cot, q, k, v, p, o, hb, e, gp, x1, r1, x2, r2, y)
+
+    def chunk(n, r, w):
+        return [VM(t, BF) for t in ((n, 4, r, w), (n, 2, r, w), (n, r, w), (n, r // 2, w), (n, r // 4, w), (2, n, r, w))]
+
     return pl.pallas_call(
         backward_kernel,
-        out_shape=[S((rows, width), BF), S((rows, width), BF), packed, S((16, width), F32)],
-        in_specs=[V, V, V, V, V, V, ANY, V, V, ANY, ANY, V, V, V, V, V, V] + [ANY] * 6 + [V] * 2,
-        out_specs=[V, V, ANY, V],
-        scratch_shapes=[VM(w.shape, BF) for w in weights]
+        out_shape=[
+            S((rows, width), BF), S((rows, width), BF), S((ff // 4, width), BF), S((share, ff), BF), S((4, share, width), BF),
+            S((16, width), F32),
+        ],
+        in_specs=[V] * 4 + [ANY] * 21,
+        out_specs=[ANY] * 5 + [V],
+        scratch_shapes=[VM(t.shape, t.dtype) for t in arrays]
         + [
-            VM((rows, ff), BF),
-            VM((rows, ff), BF),
-            VM(p.shape, BF),
-            VM(packed.shape, BF),
-            full, full, low,
-            VM((width, rows), BF),
-            low, low, low, low, low,
-            pltpu.SemaphoreType.DMA((9,)),
-            pltpu.SemaphoreType.DMA((2,)),
+            VM((width, ff), BF), VM((ff, width), BF), VM((rows, width), BF), VM((width, rows), BF), VM((16, width), F32),
+            VM((4, ff // 4, width), BF), VM((3, 4, share, ff // 3), BF), VM((4, 4, share, width), BF),
+        ]
+        + chunk(3, 128, width) + chunk(3, share, ff // 6) + chunk(4, share, width // 2)
+        + [
+            dma((17,)), dma((4,)), dma((2,)), dma((2, 2, nc)),
+            VM((6, 16, width), F32), VM((5, 16, width), F32), dma((5,)), dma((5,)), dma((9, nc)), dma((9, nc)),
         ],
-        compiler_params=pltpu.CompilerParams(vmem_limit_bytes=67043328),
-        name="segment_backward",
-    )(x, cot, dcl, q, k, v, p, o, hb, e, gp, x1, r1, x2, r2, y, z, *weights, g1, g2)
+        compiler_params=pltpu.CompilerParams(collective_id=collective_id, has_side_effects=True, vmem_limit_bytes=67043328),
+        name="backward_reduce",
+    )(dcl, z, g1, g2, *arrays, *weights)
 
 
 def cross_kernel(cls, emb, docs, cot, wq, wk, wv, wi, out_w, outer_w,
@@ -1338,8 +1377,18 @@
     )(cls, emb, docs, cot, wq, wk, wv, wi, out_w, outer_w, *vectors)
 
 
-def finish_kernel(red, vec, emb, xw, hw, ow, e, dqkv, du, da, df, vec1,
-                  gq, gqb, gk, gv, gvb, go, gob, gg1, gc1, gi, gib, g2_, gb2, gg2, gc2, gemb, vec_s):
+def finish_kernel(dx, y, outer, inner, mats, vec, emb, xw, hw, ow, e, dqkv, du, da, df, vec1,
+                  y_o, dx_o, gq, gqb, gk, gv, gvb, go, gob, gg1, gc1, gi, gib, g2_, gb2, gg2, gc2, gemb,
+                  vec_s, pass_s, pass_in, pass_out):
+    moves = [pltpu.make_async_copy(src, pass_s.at[i], pass_in.at[i]) for i, src in enumerate((y, dx))]
+    for cp in moves:
+        cp.start()
+    leaves = []
+    for i, dst in enumerate((y_o, dx_o)):
+        moves[i].wait()
+        cp = pltpu.make_async_copy(pass_s.at[i], dst, pass_out.at[i])
+        cp.start()
+        leaves.append(cp)
     d = lax.axis_index("dp")
     odd = d % 2 == 1
     start, _ = window(d)
@@ -1360,13 +1409,13 @@
     x, h, o = own(xw[...].astype(F32)).astype(BF), own(hw[...].astype(F32)).astype(BF), own(ow[...].astype(F32)).astype(BF)
     dq, dk, dv = whole(0), whole(1), whole(2)
     for at, (out, left, right) in enumerate(((gq, x, dq), (gk, x, dk), (gv, x, dv), (go, o, da[...]))):
-        out[0] = red[at * 192 : at * 192 + 192, :].astype(F32)
+        out[0] = mats[at].astype(F32)
         out[1] = dot_tn(left, right)
     for j in range(4):
         l = slice(j * 768, j * 768 + 768)
-        gi[0, :, l] = red[768 + j * 192 : 960 + j * 192, :].astype(F32)
+        gi[0, :, l] = inner[:, l].astype(F32)
         gi[1, :, l] = dot_tn(h, du[j])
-    g2_[0] = red[1536:2304, :].astype(F32)
+    g2_[0] = outer[...].astype(F32)
     g2_[1] = dot_tn(e[...], df[...])
     lanes = pl.ds(start, 256)
     mine = own(vec[:, lanes])
@@ -1380,25 +1429,29 @@
     gib[0:1, :] = vec[pl.ds(8 + d, 1), :]
     gib[1:2, :] = row_sum(du[d].astype(F32))
     gemb[...] = own(emb[:, lanes])
-
-
-def finish(red, vec, crossed):
+    for cp in leaves:
+        cp.wait()
+
+
+def finish(summed, crossed):
     (_, _, xw, hw, ow, e, dqkv, du, da, df, vec1, emb) = crossed
     S = jax.ShapeDtypeStruct
     V = pl.BlockSpec(memory_space=pltpu.VMEM)
     square, line = S((2, 192, 768), F32), S((2, 192), F32)
+    dx, y, outer, inner, mats, vec = summed
     return pl.pallas_call(
         finish_kernel,
         out_shape=[
+            S(y.shape, BF), S(dx.shape, BF),
             square, line, square, square, line, square, line, line, line,
             S((2, 192, 3072), F32), S((2, 768), F32), S((2, 768, 768), F32), line, line, line, S((32, 192), F32),
         ],
-        in_specs=[V] * 12,
-        out_specs=[V] * 16,
-        scratch_shapes=[pltpu.VMEM((8, 768), F32)],
+        in_specs=[ANY] * 2 + [V] * 14,
+        out_specs=[ANY] * 2 + [V] * 16,
+        scratch_shapes=[pltpu.VMEM((8, 768), F32), pltpu.VMEM((2,) + y.shape, BF), pltpu.SemaphoreType.DMA((2,)), pltpu.SemaphoreType.DMA((2,))],
         compiler_params=pltpu.CompilerParams(vmem_limit_bytes=67043328),
         name="finish_grads",
-    )(red, vec, emb, xw, hw, ow, e, dqkv, du, da, df, vec1)
+    )(dx, y, outer, inner, mats, vec, emb, xw, hw, ow, e, dqkv, du, da, df, vec1)
 
 
 def fast_shards(
@@ -1427,11 +1480,11 @@
     full, windows, docs, saved, y, cls = start(inputs[0], weights, doc_ids, vectors, 1)
     windows = [w.reshape(-1, w.shape[-1]) for w in windows]
     crossed = cross(cls, segment_embed, cotangent, docs, *windows, out_weight, outer_weight, vectors, 2)
-    grad, output, packed, vec = backward(
-        inputs[0], cotangent[0], crossed[1], saved, y, crossed[0], full, first_gain, second_gain
-    )
-    total, vec = reduce(packed, vec, 6, 3)
-    return (output[None], grad[None], *finish(total, vec, crossed))
+    summed = backward(
+        inputs[0], cotangent[0], crossed[1], saved, y, crossed[0], full, first_gain, second_gain, 3
+    )
+    output, grad, *gradients = finish(summed, crossed)
+    return (output[None], grad[None], *gradients)
 
 
 def solution(mesh):

time: 305 us -> 278 us (0.911)
  Pallas kernels: 304 us -> 277 us
    pallas_call x2 -> x1, Pallas kernels: 124 us -> 11 us  [finish(): pl.pallas_call(finish_kernel, out_shape=[S(y.shape, BF), S(dx.shape, BF),...]
    pallas_call x1, Pallas kernels: 40 us -> 125 us  [backward(): pl.pallas_call(backward_kernel, out_shape=[S((rows, width), BF), S((rows,...]
where the time goes in v5:
time: 278 us; the launch traced here: 277 us
  Pallas kernels  277 us (100%)
    pallas_call x1, Pallas kernels, backward(): pl.pallas_call(backward_kernel, out_shape=[S((rows, width), BF), S((rows,...  125 us
    pallas_call x1, Pallas kernels, start(): pl.pallas_call(functools.partial(start_kernel, pieces), out_shape=[S((4 *...  71.6 us
    pallas_call x1, Pallas kernels, cross(): pl.pallas_call(cross_kernel, out_shape=[S((8, 768), F32), S((8, 768), F32...  69.1 us
    pallas_call x1, Pallas kernels, finish(): pl.pallas_call(finish_kernel, out_shape=[S(y.shape, BF), S(dx.shape, BF),...  11 us

profile of v5, /device:TPU:1, one launch (start us, length us, event | category | flops | bytes accessed | tf_op | source)
XLA Modules:
  0.0 277.5 jit_solution(10962188412479072491)
XLA Ops:
  0.7 71.6 %gather_forward.1 = (bf16[768,768]{1,0:T(8,128)(2,1)}, bf16[768,768]{1,0:T(8,128)(2,1)}, bf16[768,768]{1,0:T(8,128)(2,1)}, bf16[768,768]{1,0:T(8,128)(2,1)}, bf1...) custom-call(bf16[512,768]{1,0:T(8,128)(2,1)} %bitcast.8, ...), custom_call_target="tpu_custom_call" | custom-call | tf_op jit(solution)/shard_map/gather_forward/pallas_call | solution.py:724
  72.3 69.1 %cross_block.1 = (f32[8,768]{1,0:T(8,128)}, f32[8,768]{1,0:T(8,128)}, bf16[128,256]{1,0:T(8,128)(2,1)}, bf16[128,256]{1,0:T(8,128)(2,1)}, bf16[128,256]{1,0:T(8,...) custom-call(f32[4,768]{1,0:T(4,128)} %get-tuple-element.79.cls, ...), custom_call_target="tpu_custom_call" | custom-call | tf_op jit(solution)/shard_map/cross_block/pallas_call | solution.py:1358
  141.4 124.9 %backward_reduce.1 = (bf16[512,768]{1,0:T(8,128)(2,1)}, bf16[512,768]{1,0:T(8,128)(2,1)}, bf16[768,768]{1,0:T(8,128)(2,1)}, bf16[192,3072]{1,0:T(8,128)(2,1)}, b...) custom-call(f32[8,768]{1,0:T(8,128)} %get-tuple-element.85.dcl, f32[8,768]{1,0:T(8,128)} %get-tuple-element.86.z, ...), custom_call_target="tpu_custom_call" | custom-call | tf_op jit(solution)/shard_map/backward_reduce/pallas_call | solution.py:1145
  266.3 11.0 %finish_grads.1 = (bf16[512,768]{1,0:T(8,128)(2,1)}, bf16[512,768]{1,0:T(8,128)(2,1)}, f32[2,192,768]{2,1,0:T(8,128)}, f32[2,192]{1,0:T(2,128)}, f32[2,192,768]{...) custom-call(bf16[512,768]{1,0:T(8,128)(2,1)} %get-tuple-element.106., ...), custom_call_target="tpu_custom_call" | custom-call | tf_op jit(solution)/shard_map/finish_grads/pallas_call | solution.py:1442

commit v6 on v5

--- a/solution.py
+++ b/solution.py
@@ -801,15 +801,16 @@
     return jnp.sum(v, axis=0, keepdims=True)
 
 
+LAGS = (0, 2, 3, 4, 5, 6, 7, 8)
 CHUNKS = [("rows", 0), ("cols", 0), ("rows", 1), ("cols", 1), ("rows", 2), ("cols", 2), ("mats", 3), ("mats", 0), ("mats", 1), ("mats", 2)]
 
 
-def backward_kernel(dcl, z, g1, g2, x, cot, q, k, v, p, o, hb, e, gp, x1, r1, x2, r2, y, wq, wk, wv, wo, wi, w2, *refs):
-    (dx_o, y_o, outer_o, inner_o, mats_o, vec_o), refs = refs[:6], refs[6:]
+def backward_kernel(dcl, z, g1, g2, du_own, dqkv_own, x, cot, q, k, v, p, o, hb, e, gp, x1, r1, x2, r2, y, wq, wk, wv, wo, wi, w2, *refs):
+    (dx_o, y_o, outer_o, inner_o, mats_o, du_all, dqkv_all, vec_o), refs = refs[:8], refs[8:]
     (xs, ds_, qs_, ks_, vs_, p_s, os_, hs, e_s, gp_s, x1s, r1s, acc, r2s, ys), refs = refs[:15], refs[15:]
     (vi, v2, df, ht, vecs, g_rows, g_cols, g_mats), refs = refs[:8], refs[8:]
     bufs, refs = refs[:18], refs[18:]
-    in_sem, w_sem, res_sem, out_sem, vsum, vgot, vsend, vrcv, send, recv = refs
+    in_sem, w_sem, res_sem, out_sem, vsum, vgot, vsend, vrcv, send, recv, kept, kept_sem, far_send, far_recv, near_send, near_recv = refs
     dev, s = place()
     c, first, second, other = plane_peers(dev, s)
     px, py = dev % 2, dev // 2
@@ -824,7 +825,7 @@
     loads = [pltpu.make_async_copy(src, dst, in_sem.at[i]) for i, (src, dst) in enumerate(order)]
     for cp in loads:
         cp.start()
-    greet([(first, s), (second, s), (dev, other), (dev, znear), (dev, zfar)])
+    greet([(first, s), (second, s), (3 - dev, s), (dev, other), (dev, znear), (dev, zfar)])
     rows, width = xs.shape
     segs, nt = rows // 128, width // TILE
     share = width // 4
@@ -836,6 +837,30 @@
 
     def arrived(ref, sem):
         pltpu.make_async_copy(ref, ref, sem).wait()
+
+    crossing = ((du_own, du_all), (dqkv_own, dqkv_all))
+    far = (3 - dev, first, second)
+    half_rows = pl.ds(pl.multiple_of(c * 64, 64), 64)
+    keeps, shared = [], []
+    for m, (src, dst) in enumerate(crossing):
+        for n, peer in enumerate(far):
+            go(remote(src.at[half_rows], dst.at[dev, half_rows], far_send.at[m, n], far_recv.at[m, n], (peer, s)))
+        cp = pltpu.make_async_copy(src, kept.at[m], kept_sem.at[0, m])
+        cp.start()
+        keeps.append(cp)
+
+    def cross_share():
+        for m, (src, dst) in enumerate(crossing):
+            for n, peer in enumerate(far):
+                got = dst.at[peer, half_rows]
+                remote(got, got, far_send.at[m, n], far_recv.at[m, n], (peer, s)).wait_recv()
+                cp = remote(got, got, near_send.at[m, n], near_recv.at[m, n], (dev, other))
+                cp.start()
+                shared.append(cp)
+            keeps[m].wait()
+            cp = pltpu.make_async_copy(kept.at[m], dst.at[dev], kept_sem.at[1, m])
+            cp.start()
+            outs.append(cp)
 
     families = {"rows": 0, "cols": 1, "mats": 2}
 
@@ -948,7 +973,7 @@
 
     def slot(i):
         for t in range(8, 0, -1):
-            n = i - (t - 1)
+            n = i - LAGS[t - 1]
             if 0 <= n < nc:
                 stage(t, n)
 
@@ -1001,6 +1026,7 @@
     lax.fori_loop(0, 4, ffn(0), 0)
     offer(0)
     offer(1)
+    cross_share()
     lax.fori_loop(0, 2, ffn(1), 0)
     slot(0)
     lax.fori_loop(2, 4, ffn(1), 0)
@@ -1119,24 +1145,26 @@
     lax.fori_loop(0, nt, source, 0)
     results.append(pltpu.make_async_copy(xs, dx_o, res_sem.at[1]))
     results[1].start()
-    for i in range(8, nc + 8):
+    for i in range(8, nc + LAGS[7]):
         slot(i)
         if i < 13:
             vector_hop(i - 7)
     vec_o[...] = vsum[5]
     for cp in started:
         cp.wait_send()
-    for cp in outs + results:
+    for cp in outs + results + shared:
         cp.wait()
 
 
-def backward(x, cot, dcl, saved, y, z, weights, g1, g2, collective_id):
+def backward(x, cot, crossed, saved, y, weights, g1, g2, collective_id):
     q, k, v, p, o, hb, e, gp, x1, r1, x2, r2 = saved
     rows, width = x.shape
     ff = weights[4].shape[1]
     share, nc = width // 4, len(CHUNKS)
     S, VM, dma = jax.ShapeDtypeStruct, pltpu.VMEM, pltpu.SemaphoreType.DMA
     V = pl.BlockSpec(memory_space=pltpu.VMEM)
+    z, dcl, dqkv, du = crossed[0], crossed[1], crossed[6], crossed[7]
+    four = S((4,) + du.shape, BF)
     arrays = (x, cot, q, k, v, p, o, hb, e, gp, x1, r1, x2, r2, y)
 
     def chunk(n, r, w):
@@ -1146,10 +1174,10 @@
         backward_kernel,
         out_shape=[
             S((rows, width), BF), S((rows, width), BF), S((ff // 4, width), BF), S((share, ff), BF), S((4, share, width), BF),
-            S((16, width), F32),
+            four, four, S((16, width), F32),
         ],
-        in_specs=[V] * 4 + [ANY] * 21,
-        out_specs=[ANY] * 5 + [V],
+        in_specs=[V] * 4 + [ANY] * 23,
+        out_specs=[ANY] * 7 + [V],
         scratch_shapes=[VM(t.shape, t.dtype) for t in arrays]
         + [
             VM((width, ff), BF), VM((ff, width), BF), VM((rows, width), BF), VM((width, rows), BF), VM((16, width), F32),
@@ -1159,22 +1187,22 @@
         + [
             dma((17,)), dma((4,)), dma((2,)), dma((2, 2, nc)),
             VM((6, 16, width), F32), VM((5, 16, width), F32), dma((5,)), dma((5,)), dma((9, nc)), dma((9, nc)),
+            VM((2,) + du.shape, BF), dma((2, 2)), dma((2, 3)), dma((2, 3)), dma((2, 3)), dma((2, 3)),
         ],
         compiler_params=pltpu.CompilerParams(collective_id=collective_id, has_side_effects=True, vmem_limit_bytes=67043328),
         name="backward_reduce",
-    )(dcl, z, g1, g2, *arrays, *weights)
+    )(dcl, z, g1, g2, du, dqkv, *arrays, *weights)
 
 
 def cross_kernel(cls, emb, docs, cot, wq, wk, wv, wi, out_w, outer_w,
                  qb, vb, ob, g1, c1, ib, b2, g2, c2,
                  z_o, dcl_o, xw_o, hw_o, ow_o, e_o, dqkv_o, du_o, da_o, df_o, vec_o, emb_o,
-                 vq, vk, vv, vi, vo, v2, heads, xall, rows_s, p_s, dqkv_s, du_s, send1, got1, send2, got2,
-                 in_sem, all_send, all_recv, first_rows, cots, cot_all, row_sem, cot_send, cot_recv, s1, r1, s2, r2, qs_send, qs_recv, us_send, us_recv, o_sem):
+                 vq, vk, vv, vi, vo, v2, heads, xall, rows_s, p_s, part_s, total_s, send1, got1, send2, got2,
+                 in_sem, all_send, all_recv, first_rows, cots, cot_all, row_sem, cot_send, cot_recv, s1, r1, s2, r2, s3, r3):
     d, s = place()
     c, first, second, other = plane_peers(d, s)
     start, off = window(d)
     me, ahead, behind = everyone(d, s)
-    far = [3 - d, first, second]
     lane_w = pl.ds(start, 256)
     loads = [
         pltpu.make_async_copy(src, dst, in_sem.at[i])
@@ -1205,10 +1233,6 @@
     for cp in row_loads:
         cp.wait()
     cots[...] = jnp.concatenate([first_rows[i].astype(F32)[0:1] for i in range(4)], axis=0).astype(BF)
-    for j, i in enumerate(ahead):
-        cp = remote(cots, cot_all.at[me], cot_send.at[j], cot_recv.at[j], (i // 8, i % 8))
-        cp.start()
-        sent.append(cp)
     cot_all[me] = cots[...]
     ids = lax.broadcasted_iota(jnp.int32, (8, 128), 1) // 32 * 1024
     ids = ids.astype(F32)
@@ -1221,13 +1245,19 @@
     allowed = across == across.T
     for j, i in enumerate(behind):
         remote(heads, xall.at[i], all_send.at[j], all_recv.at[j], (i // 8, i % 8)).wait_recv()
+    for j, i in enumerate(ahead):
+        cp = remote(cots, cot_all.at[me], cot_send.at[j], cot_recv.at[j], (i // 8, i % 8))
+        cp.start()
+        sent.append(cp)
     for i in range(32):
         rows_s[4 * i : 4 * i + 4, :] = xall[i].astype(F32)
     xf = rows_s[...]
     x = xf.astype(BF)
 
     def total(n, partial):
-        send1[n] = partial.astype(BF)
+        half = pl.ds(pl.multiple_of(c * 64, 64), 64)
+        part_s[...] = partial
+        send1[n] = part_s[half, :].astype(BF)
         one = remote(send1.at[n], got1.at[n], s1.at[n], r1.at[n], (first, s))
         one.start()
         one.wait_recv()
@@ -1236,9 +1266,12 @@
         two = remote(send2.at[n], got2.at[n], s2.at[n], r2.at[n], (second, s))
         two.start()
         two.wait_recv()
-        sent.append(one)
-        sent.append(two)
-        return send2[n].astype(F32) + got2[n].astype(F32)
+        total_s[n, half, :] = send2[n].astype(F32) + got2[n].astype(F32)
+        three = remote(total_s.at[n, half], total_s.at[n, half], s3.at[n], r3.at[n], (d, other))
+        three.start()
+        three.wait_recv()
+        sent.extend((one, two, three))
+        return total_s[n]
 
     def vector(ref, lanes=slice(None)):
         return ref[1:2, lanes].astype(F32)
@@ -1296,12 +1329,8 @@
     df_o[...] = df
     vec_o[5:6, :] = row_sum(df.astype(F32))
     du = (dot_nt(df, v2[...]).astype(BF).astype(F32) * gp).astype(BF)
-    du_s[d] = du
+    du_o[...] = du
     dh = dr2 + total(2, dot_nt(du, vi[...]))
-    for n, peer in enumerate(far):
-        cp = remote(du_s.at[d], du_s.at[d], us_send.at[n], us_recv.at[n], (peer, s))
-        cp.start()
-        sent.append(cp)
     vec_o[3:4, :] = row_sum(dh * xhat1)
     vec_o[4:5, :] = row_sum(dh)
     dr1 = standard_back(dh * vector(g1), xhat1, rstd1)
@@ -1326,51 +1355,39 @@
         dks.append((dkp * 0.125).astype(BF))
         dvs.append(dvp.astype(BF))
     dq, dk, dv = (jnp.concatenate(t, axis=1) for t in (dqs, dks, dvs))
-    dqkv_s[d, :, 0:256] = dq
-    dqkv_s[d, :, 256:512] = dk
-    dqkv_s[d, :, 512:768] = dv
+    dqkv_o[:, 0:256] = dq
+    dqkv_o[:, 256:512] = dk
+    dqkv_o[:, 512:768] = dv
     dx = dr1 + total(3, dot_nt(dq, vq[...]) + dot_nt(dk, vk[...]) + dot_nt(dv, vv[...]))
-    for n, peer in enumerate(far):
-        cp = remote(dqkv_s.at[d], dqkv_s.at[d], qs_send.at[n], qs_recv.at[n], (peer, s))
-        cp.start()
-        sent.append(cp)
     dcl = dx.astype(BF)
     dcl_o[...] = dot(own, dcl)
     back = dcl.astype(F32)
     emb_o[...] = back[0:32] + back[32:64] + back[64:96] + back[96:128]
-    for n, peer in enumerate(far):
-        remote(du_s.at[peer], du_s.at[peer], us_send.at[n], us_recv.at[n], (peer, s)).wait_recv()
-        remote(dqkv_s.at[peer], dqkv_s.at[peer], qs_send.at[n], qs_recv.at[n], (peer, s)).wait_recv()
-    outs = [pltpu.make_async_copy(du_s, du_o, o_sem.at[0]), pltpu.make_async_copy(dqkv_s, dqkv_o, o_sem.at[1])]
-    for cp in outs:
-        cp.start()
     for cp in sent:
         cp.wait_send()
-    for cp in outs:
-        cp.wait()
 
 
 def cross(cls, emb, cot, docs, wq, wk, wv, wi, out_w, outer_w, vectors, collective_id):
     S = jax.ShapeDtypeStruct
     V = pl.BlockSpec(memory_space=pltpu.VMEM)
     VM, dma = pltpu.VMEM, pltpu.SemaphoreType.DMA
-    low, win, four = S((128, 768), BF), S((128, 256), BF), S((4, 128, 768), BF)
+    low, win = S((128, 768), BF), S((128, 256), BF)
     return pl.pallas_call(
         cross_kernel,
         out_shape=[
-            S((8, 768), F32), S((8, 768), F32), win, win, win, low, four, four, low, low,
+            S((8, 768), F32), S((8, 768), F32), win, win, win, low, low, low, low, low,
             S((8, 768), F32), S((32, 768), F32),
         ],
         in_specs=[V] * 3 + [ANY] * 7 + [V] * 9,
-        out_specs=[V] * 6 + [ANY] * 2 + [V] * 4,
+        out_specs=[V] * 12,
         scratch_shapes=[
             VM((768, 256), BF), VM((768, 256), BF), VM((768, 256), BF), VM((768, 768), BF), VM((256, 768), BF), VM((768, 768), BF),
             VM((4, 768), BF), VM((32, 4, 768), BF), VM((128, 768), F32), VM((4, 128, 128), BF),
-            VM((4, 128, 768), BF), VM((4, 128, 768), BF),
-            VM((4, 128, 768), BF), VM((4, 128, 768), BF), VM((4, 128, 768), BF), VM((4, 128, 768), BF),
+            VM((128, 768), F32), VM((4, 128, 768), F32),
+            VM((4, 64, 768), BF), VM((4, 64, 768), BF), VM((4, 64, 768), BF), VM((4, 64, 768), BF),
             dma((6,)), dma((31,)), dma((31,)),
             VM((4, 8, 768), BF), VM((4, 768), BF), VM((32, 4, 768), BF), dma((4,)), dma((31,)), dma((31,)),
-            dma((4,)), dma((4,)), dma((4,)), dma((4,)), dma((3,)), dma((3,)), dma((3,)), dma((3,)), dma((2,)),
+            dma((4,)), dma((4,)), dma((4,)), dma((4,)), dma((4,)), dma((4,)),
         ],
         compiler_params=pltpu.CompilerParams(collective_id=collective_id, has_side_effects=True, vmem_limit_bytes=67043328),
         name="cross_block",
@@ -1378,8 +1395,8 @@
 
 
 def finish_kernel(dx, y, outer, inner, mats, vec, emb, xw, hw, ow, e, dqkv, du, da, df, vec1,
-                  y_o, dx_o, gq, gqb, gk, gv, gvb, go, gob, gg1, gc1, gi, gib, g2_, gb2, gg2, gc2, gemb,
-                  vec_s, pass_s, pass_in, pass_out):
+                  y_o, dx_o, gq_o, gqb, gk_o, gv_o, gvb, go_o, gob, gg1, gc1, gi_o, gib, g2_o, gb2, gg2, gc2, gemb,
+                  vec_s, pass_s, gq, gk, gv, go, gi, g2_, pass_in, pass_out, big_out):
     moves = [pltpu.make_async_copy(src, pass_s.at[i], pass_in.at[i]) for i, src in enumerate((y, dx))]
     for cp in moves:
         cp.start()
@@ -1408,15 +1425,23 @@
 
     x, h, o = own(xw[...].astype(F32)).astype(BF), own(hw[...].astype(F32)).astype(BF), own(ow[...].astype(F32)).astype(BF)
     dq, dk, dv = whole(0), whole(1), whole(2)
-    for at, (out, left, right) in enumerate(((gq, x, dq), (gk, x, dk), (gv, x, dv), (go, o, da[...]))):
+    def leave(src, dst, n):
+        cp = pltpu.make_async_copy(src, dst, big_out.at[n])
+        cp.start()
+        leaves.append(cp)
+
+    for at, (out, dst, left, right) in enumerate(((gq, gq_o, x, dq), (gk, gk_o, x, dk), (gv, gv_o, x, dv), (go, go_o, o, da[...]))):
         out[0] = mats[at].astype(F32)
         out[1] = dot_tn(left, right)
+        leave(out, dst, at)
     for j in range(4):
         l = slice(j * 768, j * 768 + 768)
         gi[0, :, l] = inner[:, l].astype(F32)
         gi[1, :, l] = dot_tn(h, du[j])
+        leave(gi.at[:, :, l], gi_o.at[:, :, l], 4 + j)
     g2_[0] = outer[...].astype(F32)
     g2_[1] = dot_tn(e[...], df[...])
+    leave(g2_, g2_o, 8)
     lanes = pl.ds(start, 256)
     mine = own(vec[:, lanes])
     vec_s[...] = vec1[...]
@@ -1434,11 +1459,11 @@
 
 
 def finish(summed, crossed):
-    (_, _, xw, hw, ow, e, dqkv, du, da, df, vec1, emb) = crossed
+    (_, _, xw, hw, ow, e, _, _, da, df, vec1, emb) = crossed
     S = jax.ShapeDtypeStruct
     V = pl.BlockSpec(memory_space=pltpu.VMEM)
     square, line = S((2, 192, 768), F32), S((2, 192), F32)
-    dx, y, outer, inner, mats, vec = summed
+    dx, y, outer, inner, mats, du, dqkv, vec = summed
     return pl.pallas_call(
         finish_kernel,
         out_shape=[
@@ -1447,8 +1472,10 @@
             S((2, 192, 3072), F32), S((2, 768), F32), S((2, 768, 768), F32), line, line, line, S((32, 192), F32),
         ],
         in_specs=[ANY] * 2 + [V] * 14,
-        out_specs=[ANY] * 2 + [V] * 16,
-        scratch_shapes=[pltpu.VMEM((8, 768), F32), pltpu.VMEM((2,) + y.shape, BF), pltpu.SemaphoreType.DMA((2,)), pltpu.SemaphoreType.DMA((2,))],
+        out_specs=[ANY, ANY, ANY, V, ANY, ANY, V, ANY, V, V, V, ANY, V, ANY, V, V, V, V],
+        scratch_shapes=[pltpu.VMEM((8, 768), F32), pltpu.VMEM((2,) + y.shape, BF)]
+        + [pltpu.VMEM(t.shape, F32) for t in (square, square, square, square, S((2, 192, 3072), F32), S((2, 768, 768), F32))]
+        + [pltpu.SemaphoreType.DMA((2,)), pltpu.SemaphoreType.DMA((2,)), pltpu.SemaphoreType.DMA((9,))],
         compiler_params=pltpu.CompilerParams(vmem_limit_bytes=67043328),
         name="finish_grads",
     )(dx, y, outer, inner, mats, vec, emb, xw, hw, ow, e, dqkv, du, da, df, vec1)
@@ -1481,7 +1508,7 @@
     windows = [w.reshape(-1, w.shape[-1]) for w in windows]
     crossed = cross(cls, segment_embed, cotangent, docs, *windows, out_weight, outer_weight, vectors, 2)
     summed = backward(
-        inputs[0], cotangent[0], crossed[1], saved, y, crossed[0], full, first_gain, second_gain, 3
+        inputs[0], cotangent[0], crossed, saved, y, full, first_gain, second_gain, 3
     )
     output, grad, *gradients = finish(summed, crossed)
     return (output[None], grad[None], *gradients)

time: 278 us -> 245 us (0.88)
  Pallas kernels: 277 us -> 244 us
    pallas_call x1, Pallas kernels: 69.1 us -> 50.8 us  [cross(): pl.pallas_call(cross_kernel, out_shape=[S((8, 768), F32), S((8, 768), F32...]
    pallas_call x1, Pallas kernels: 125 us -> 111 us  [backward(): pl.pallas_call(backward_kernel, out_shape=[S((rows, width), BF), S((rows,...]
where the time goes in v6:
time: 245 us
  Pallas kernels  244 us (100%)
    pallas_call x1, Pallas kernels, backward(): pl.pallas_call(backward_kernel, out_shape=[S((rows, width), BF), S((rows,...  111 us
    pallas_call x1, Pallas kernels, start(): pl.pallas_call(functools.partial(start_kernel, pieces), out_shape=[S((4 *...  71.6 us
    pallas_call x1, Pallas kernels, cross(): pl.pallas_call(cross_kernel, out_shape=[S((8, 768), F32), S((8, 768), F32...  50.8 us
    pallas_call x1, Pallas kernels, finish(): pl.pallas_call(finish_kernel, out_shape=[S(y.shape, BF), S(dx.shape, BF),...  10.8 us

profile of v6, /device:TPU:1, one launch (start us, length us, event | category | flops | bytes accessed | tf_op | source)
XLA Modules:
  0.0 244.7 jit_solution(18332157426979592894)
XLA Ops:
  0.7 71.6 %gather_forward.1 = (bf16[768,768]{1,0:T(8,128)(2,1)}, bf16[768,768]{1,0:T(8,128)(2,1)}, bf16[768,768]{1,0:T(8,128)(2,1)}, bf16[768,768]{1,0:T(8,128)(2,1)}, bf1...) custom-call(bf16[512,768]{1,0:T(8,128)(2,1)} %bitcast.8, ...), custom_call_target="tpu_custom_call" | custom-call | tf_op jit(solution)/shard_map/gather_forward/pallas_call | solution.py:724
  72.3 50.8 %cross_block.1 = (f32[8,768]{1,0:T(8,128)}, f32[8,768]{1,0:T(8,128)}, bf16[128,256]{1,0:T(8,128)(2,1)}, bf16[128,256]{1,0:T(8,128)(2,1)}, bf16[128,256]{1,0:T(8,...) custom-call(f32[4,768]{1,0:T(4,128)} %get-tuple-element.81.cls, ...), custom_call_target="tpu_custom_call" | custom-call | tf_op jit(solution)/shard_map/cross_block/pallas_call | solution.py:1375
  123.2 110.6 %backward_reduce.1 = (bf16[512,768]{1,0:T(8,128)(2,1)}, bf16[512,768]{1,0:T(8,128)(2,1)}, bf16[768,768]{1,0:T(8,128)(2,1)}, bf16[192,3072]{1,0:T(8,128)(2,1)}, b...) custom-call(f32[8,768]{1,0:T(8,128)} %get-tuple-element.87.dcl, ...), custom_call_target="tpu_custom_call" | custom-call | tf_op jit(solution)/shard_map/backward_reduce/pallas_call | solution.py:1173
  233.8 10.8 %finish_grads.1 = (bf16[512,768]{1,0:T(8,128)(2,1)}, bf16[512,768]{1,0:T(8,128)(2,1)}, f32[2,192,768]{2,1,0:T(8,128)}, f32[2,192]{1,0:T(2,128)}, f32[2,192,768]{...) custom-call(bf16[512,768]{1,0:T(8,128)(2,1)} %get-tuple-element.110., ...), custom_call_target="tpu_custom_call" | custom-call | tf_op jit(solution)/shard_map/finish_grads/pallas_call | solution.py:1467

commit v7 on v6

--- a/solution.py
+++ b/solution.py
@@ -802,7 +802,7 @@
 
 
 LAGS = (0, 2, 3, 4, 5, 6, 7, 8)
-CHUNKS = [("rows", 0), ("cols", 0), ("rows", 1), ("cols", 1), ("rows", 2), ("cols", 2), ("mats", 3), ("mats", 0), ("mats", 1), ("mats", 2)]
+CHUNKS = [("rows", 0), ("rows", 1), ("rows", 2), ("cols", 0), ("cols", 1), ("cols", 2), ("mats", 3), ("mats", 0), ("mats", 1), ("mats", 2)]
 
 
 def backward_kernel(dcl, z, g1, g2, du_own, dqkv_own, x, cot, q, k, v, p, o, hb, e, gp, x1, r1, x2, r2, y, wq, wk, wv, wo, wi, w2, *refs):
@@ -820,7 +820,7 @@
     z0, z1 = z_at % 2, z_at // 2
     znear = (z_at + 1 - 2 * z0) * 2 + c
     zfar = (z_at + 2 - 4 * z1) * 2 + c
-    order = [(cot, ds_), (y, ys), (x2, acc), (r2, r2s), (hb, hs), (w2, v2), (e, e_s), (gp, gp_s), (wi, vi),
+    order = [(cot, ds_), (y, ys), (x2, acc), (r2, r2s), (e, e_s), (hb, hs), (w2, v2), (gp, gp_s), (wi, vi),
              (x1, x1s), (r1, r1s), (o, os_), (p, p_s), (q, qs_), (k, ks_), (v, vs_), (x, xs)]
     loads = [pltpu.make_async_copy(src, dst, in_sem.at[i]) for i, (src, dst) in enumerate(order)]
     for cp in loads:
@@ -842,9 +842,13 @@
     far = (3 - dev, first, second)
     half_rows = pl.ds(pl.multiple_of(c * 64, 64), 64)
     keeps, shared = [], []
+
+    def cross_send():
+        for m, (src, dst) in enumerate(crossing):
+            for n, peer in enumerate(far):
+                go(remote(src.at[half_rows], dst.at[dev, half_rows], far_send.at[m, n], far_recv.at[m, n], (peer, s)))
+
     for m, (src, dst) in enumerate(crossing):
-        for n, peer in enumerate(far):
-            go(remote(src.at[half_rows], dst.at[dev, half_rows], far_send.at[m, n], far_recv.at[m, n], (peer, s)))
         cp = pltpu.make_async_copy(src, kept.at[m], kept_sem.at[0, m])
         cp.start()
         keeps.append(cp)
@@ -972,7 +976,7 @@
     nc = len(CHUNKS)
 
     def slot(i):
-        for t in range(8, 0, -1):
+        for t in (1, 2, 3, 4, 5, 6, 7, 8):
             n = i - LAGS[t - 1]
             if 0 <= n < nc:
                 stage(t, n)
@@ -1003,8 +1007,25 @@
     results.append(pltpu.make_async_copy(ys, y_o, res_sem.at[0]))
     results[0].start()
     loads[4].wait()
+
+    def outer(j):
+        def body(block, carry):
+            g_rows[block, j * TILE : j * TILE + TILE, :] = dot_tn(e_s[:, tiles(block * nt + j)], df[...]).astype(BF)
+            return carry
+
+        return body
+
+    lax.fori_loop(0, 4, outer(0), 0)
+    offer(0)
+    lax.fori_loop(0, 4, outer(1), 0)
+    offer(1)
+    slot(0)
+    lax.fori_loop(0, 4, outer(2), 0)
+    offer(2)
+    slot(1)
+    loads[5].wait()
     ht[...] = hs[...].T
-    for i in range(5, 9):
+    for i in range(6, 9):
         loads[i].wait()
 
     def ffn(j):
@@ -1014,7 +1035,6 @@
             de = dot_nt(df[...], v2[wide, :]).astype(BF).astype(F32)
             du = (de * gp_s[:, wide].astype(F32)).astype(BF)
             vecs[pl.ds(8 + block, 1), lanes] = row_sum(du.astype(F32))
-            g_rows[block, lanes, :] = dot_tn(e_s[:, wide], df[...]).astype(BF)
             inner = dot(ht[...], du).astype(BF)
             for i in range(4):
                 g_cols[j, i, :, tiles(block)] = inner[i * share : i * share + share]
@@ -1024,19 +1044,13 @@
         return body
 
     lax.fori_loop(0, 4, ffn(0), 0)
-    offer(0)
-    offer(1)
-    cross_share()
+    offer(3)
+    slot(2)
     lax.fori_loop(0, 2, ffn(1), 0)
-    slot(0)
+    slot(3)
     lax.fori_loop(2, 4, ffn(1), 0)
-    offer(2)
-    offer(3)
-    slot(1)
-    lax.fori_loop(0, 2, ffn(2), 0)
-    slot(2)
-    lax.fori_loop(2, 4, ffn(2), 0)
     offer(4)
+    lax.fori_loop(0, 4, ffn(2), 0)
     offer(5)
     wloads = [
         pltpu.make_async_copy(src, v2.at[i * width : i * width + width], w_sem.at[i])
@@ -1044,7 +1058,7 @@
     ]
     for cp in wloads:
         cp.start()
-    slot(3)
+    slot(4)
     for i in range(9, 17):
         loads[i].wait()
 
@@ -1075,7 +1089,7 @@
 
     weights(3, df)
     offer(6)
-    slot(4)
+    slot(5)
     wloads[0].wait()
 
     def mixed(t, carry):
@@ -1107,14 +1121,14 @@
         return carry
 
     lax.fori_loop(0, 3, attend, 0)
-    slot(5)
+    slot(6)
     lax.fori_loop(3, width // 128, attend, 0)
     vecs[0:1, :] = row_sum(qs_[...].astype(F32))
     vecs[1:2, :] = row_sum(vs_[...].astype(F32))
     ht[...] = xs[...].T
     weights(0, qs_)
     offer(7)
-    slot(6)
+    slot(7)
     weights(1, ks_)
     offer(8)
     weights(2, vs_)
@@ -1129,7 +1143,7 @@
         if j < 5:
             go(remote(vsum.at[j], vgot.at[j], vsend.at[j], vrcv.at[j], hops[j]))
 
-    slot(7)
+    slot(8)
     vector_hop(0)
     for i in range(1, 4):
         wloads[i].wait()
@@ -1145,10 +1159,13 @@
     lax.fori_loop(0, nt, source, 0)
     results.append(pltpu.make_async_copy(xs, dx_o, res_sem.at[1]))
     results[1].start()
-    for i in range(8, nc + LAGS[7]):
+    for i in range(9, nc + LAGS[7]):
         slot(i)
-        if i < 13:
-            vector_hop(i - 7)
+        if i < 14:
+            vector_hop(i - 8)
+        if i == nc + 1:
+            cross_send()
+    cross_share()
     vec_o[...] = vsum[5]
     for cp in started:
         cp.wait_send()

time: 245 us -> 239 us (0.976)
  Pallas kernels: 244 us -> 238 us
    pallas_call x1, Pallas kernels: 111 us -> 104 us  [backward(): pl.pallas_call(backward_kernel, out_shape=[S((rows, width), BF), S((rows,...]
where the time goes in v7:
time: 239 us
  Pallas kernels  238 us (100%)
    pallas_call x1, Pallas kernels, backward(): pl.pallas_call(backward_kernel, out_shape=[S((rows, width), BF), S((rows,...  104 us
    pallas_call x1, Pallas kernels, start(): pl.pallas_call(functools.partial(start_kernel, pieces), out_shape=[S((4 *...  71.6 us
    pallas_call x1, Pallas kernels, cross(): pl.pallas_call(cross_kernel, out_shape=[S((8, 768), F32), S((8, 768), F32...  50.8 us
    pallas_call x1, Pallas kernels, finish(): pl.pallas_call(finish_kernel, out_shape=[S(y.shape, BF), S(dx.shape, BF),...  10.8 us

profile of v7, /device:TPU:1, one launch (start us, length us, event | category | flops | bytes accessed | tf_op | source)
XLA Modules:
  0.0 238.5 jit_solution(5734246418253105716)
XLA Ops:
  0.7 71.6 %gather_forward.1 = (bf16[768,768]{1,0:T(8,128)(2,1)}, bf16[768,768]{1,0:T(8,128)(2,1)}, bf16[768,768]{1,0:T(8,128)(2,1)}, bf16[768,768]{1,0:T(8,128)(2,1)}, bf1...) custom-call(bf16[512,768]{1,0:T(8,128)(2,1)} %bitcast.8, ...), custom_call_target="tpu_custom_call" | custom-call | tf_op jit(solution)/shard_map/gather_forward/pallas_call | solution.py:724
  72.3 50.8 %cross_block.1 = (f32[8,768]{1,0:T(8,128)}, f32[8,768]{1,0:T(8,128)}, bf16[128,256]{1,0:T(8,128)(2,1)}, bf16[128,256]{1,0:T(8,128)(2,1)}, bf16[128,256]{1,0:T(8,...) custom-call(f32[4,768]{1,0:T(4,128)} %get-tuple-element.81.cls, ...), custom_call_target="tpu_custom_call" | custom-call | tf_op jit(solution)/shard_map/cross_block/pallas_call | solution.py:1392
  123.2 104.4 %backward_reduce.1 = (bf16[512,768]{1,0:T(8,128)(2,1)}, bf16[512,768]{1,0:T(8,128)(2,1)}, bf16[768,768]{1,0:T(8,128)(2,1)}, bf16[192,3072]{1,0:T(8,128)(2,1)}, b...) custom-call(f32[8,768]{1,0:T(8,128)} %get-tuple-element.87.dcl, ...), custom_call_target="tpu_custom_call" | custom-call | tf_op jit(solution)/shard_map/backward_reduce/pallas_call | solution.py:1190
  227.5 10.8 %finish_grads.1 = (bf16[512,768]{1,0:T(8,128)(2,1)}, bf16[512,768]{1,0:T(8,128)(2,1)}, f32[2,192,768]{2,1,0:T(8,128)}, f32[2,192]{1,0:T(2,128)}, f32[2,192,768]{...) custom-call(bf16[512,768]{1,0:T(8,128)(2,1)} %get-tuple-element.110., ...), custom_call_target="tpu_custom_call" | custom-call | tf_op jit(solution)/shard_map/finish_grads/pallas_call | solution.py:1484

commit v8 on v7

--- a/solution.py
+++ b/solution.py
@@ -1411,18 +1411,16 @@
     )(cls, emb, docs, cot, wq, wk, wv, wi, out_w, outer_w, *vectors)
 
 
-def finish_kernel(dx, y, outer, inner, mats, vec, emb, xw, hw, ow, e, dqkv, du, da, df, vec1,
+def finish_kernel(dx, y, outer_h, inner_h, mats_h, vec, emb, xw, hw, ow, e, dqkv, du, da, df, vec1,
                   y_o, dx_o, gq_o, gqb, gk_o, gv_o, gvb, go_o, gob, gg1, gc1, gi_o, gib, g2_o, gb2, gg2, gc2, gemb,
-                  vec_s, pass_s, gq, gk, gv, go, gi, g2_, pass_in, pass_out, big_out):
+                  vec_s, pass_s, gq, gk, gv, go, gi, g2_, outer, inner, mats, pass_in, pass_out, big_out, sum_in):
+    sums = [pltpu.make_async_copy(src, dst, sum_in.at[i]) for i, (src, dst) in enumerate(((mats_h, mats), (inner_h, inner), (outer_h, outer)))]
+    for cp in sums:
+        cp.start()
     moves = [pltpu.make_async_copy(src, pass_s.at[i], pass_in.at[i]) for i, src in enumerate((y, dx))]
     for cp in moves:
         cp.start()
     leaves = []
-    for i, dst in enumerate((y_o, dx_o)):
-        moves[i].wait()
-        cp = pltpu.make_async_copy(pass_s.at[i], dst, pass_out.at[i])
-        cp.start()
-        leaves.append(cp)
     d = lax.axis_index("dp")
     odd = d % 2 == 1
     start, _ = window(d)
@@ -1447,18 +1445,28 @@
         cp.start()
         leaves.append(cp)
 
+    sums[0].wait()
     for at, (out, dst, left, right) in enumerate(((gq, gq_o, x, dq), (gk, gk_o, x, dk), (gv, gv_o, x, dv), (go, go_o, o, da[...]))):
         out[0] = mats[at].astype(F32)
         out[1] = dot_tn(left, right)
         leave(out, dst, at)
+    for i, dst in enumerate((y_o, dx_o)):
+        moves[i].wait()
+        cp = pltpu.make_async_copy(pass_s.at[i], dst, pass_out.at[i])
+        cp.start()
+        leaves.append(cp)
+    sums[1].wait()
     for j in range(4):
         l = slice(j * 768, j * 768 + 768)
         gi[0, :, l] = inner[:, l].astype(F32)
         gi[1, :, l] = dot_tn(h, du[j])
         leave(gi.at[:, :, l], gi_o.at[:, :, l], 4 + j)
-    g2_[0] = outer[...].astype(F32)
-    g2_[1] = dot_tn(e[...], df[...])
-    leave(g2_, g2_o, 8)
+    sums[2].wait()
+    for j in range(3):
+        r = slice(j * 256, j * 256 + 256)
+        g2_[0, r] = outer[r, :].astype(F32)
+        g2_[1, r] = dot_tn(e[:, r], df[...])
+        leave(g2_.at[:, r], g2_o.at[:, r], 8 + j)
     lanes = pl.ds(start, 256)
     mine = own(vec[:, lanes])
     vec_s[...] = vec1[...]
@@ -1488,11 +1496,12 @@
             square, line, square, square, line, square, line, line, line,
             S((2, 192, 3072), F32), S((2, 768), F32), S((2, 768, 768), F32), line, line, line, S((32, 192), F32),
         ],
-        in_specs=[ANY] * 2 + [V] * 14,
+        in_specs=[ANY] * 5 + [V] * 11,
         out_specs=[ANY, ANY, ANY, V, ANY, ANY, V, ANY, V, V, V, ANY, V, ANY, V, V, V, V],
         scratch_shapes=[pltpu.VMEM((8, 768), F32), pltpu.VMEM((2,) + y.shape, BF)]
         + [pltpu.VMEM(t.shape, F32) for t in (square, square, square, square, S((2, 192, 3072), F32), S((2, 768, 768), F32))]
-        + [pltpu.SemaphoreType.DMA((2,)), pltpu.SemaphoreType.DMA((2,)), pltpu.SemaphoreType.DMA((9,))],
+        + [pltpu.VMEM(t.shape, BF) for t in (outer, inner, mats)]
+        + [pltpu.SemaphoreType.DMA((2,)), pltpu.SemaphoreType.DMA((2,)), pltpu.SemaphoreType.DMA((11,)), pltpu.SemaphoreType.DMA((3,))],
         compiler_params=pltpu.CompilerParams(vmem_limit_bytes=67043328),
         name="finish_grads",
     )(dx, y, outer, inner, mats, vec, emb, xw, hw, ow, e, dqkv, du, da, df, vec1)

time: 239 us -> 238 us (level)
  no operation moved by 1% of the time
where the time goes in v8:
time: 238 us
  Pallas kernels  237 us (100%)
    pallas_call x1, Pallas kernels, backward(): pl.pallas_call(backward_kernel, out_shape=[S((rows, width), BF), S((rows,...  104 us
    pallas_call x1, Pallas kernels, start(): pl.pallas_call(functools.partial(start_kernel, pieces), out_shape=[S((4 *...  71.6 us
    pallas_call x1, Pallas kernels, cross(): pl.pallas_call(cross_kernel, out_shape=[S((8, 768), F32), S((8, 768), F32...  50.8 us
    pallas_call x1, Pallas kernels, finish(): pl.pallas_call(finish_kernel, out_shape=[S(y.shape, BF), S(dx.shape, BF),...  9.96 us

profile of v8, /device:TPU:1, one launch (start us, length us, event | category | flops | bytes accessed | tf_op | source)
XLA Modules:
  0.0 237.7 jit_solution(16864974332036170501)
XLA Ops:
  0.7 71.6 %gather_forward.1 = (bf16[768,768]{1,0:T(8,128)(2,1)}, bf16[768,768]{1,0:T(8,128)(2,1)}, bf16[768,768]{1,0:T(8,128)(2,1)}, bf16[768,768]{1,0:T(8,128)(2,1)}, bf1...) custom-call(bf16[512,768]{1,0:T(8,128)(2,1)} %bitcast.8, ...), custom_call_target="tpu_custom_call" | custom-call | tf_op jit(solution)/shard_map/gather_forward/pallas_call | solution.py:724
  72.3 50.8 %cross_block.1 = (f32[8,768]{1,0:T(8,128)}, f32[8,768]{1,0:T(8,128)}, bf16[128,256]{1,0:T(8,128)(2,1)}, bf16[128,256]{1,0:T(8,128)(2,1)}, bf16[128,256]{1,0:T(8,...) custom-call(f32[4,768]{1,0:T(4,128)} %get-tuple-element.81.cls, ...), custom_call_target="tpu_custom_call" | custom-call | tf_op jit(solution)/shard_map/cross_block/pallas_call | solution.py:1392
  123.2 104.4 %backward_reduce.1 = (bf16[512,768]{1,0:T(8,128)(2,1)}, bf16[512,768]{1,0:T(8,128)(2,1)}, bf16[768,768]{1,0:T(8,128)(2,1)}, bf16[192,3072]{1,0:T(8,128)(2,1)}, b...) custom-call(f32[8,768]{1,0:T(8,128)} %get-tuple-element.87.dcl, ...), custom_call_target="tpu_custom_call" | custom-call | tf_op jit(solution)/shard_map/backward_reduce/pallas_call | solution.py:1190
  227.5 10.0 %finish_grads.1 = (bf16[512,768]{1,0:T(8,128)(2,1)}, bf16[512,768]{1,0:T(8,128)(2,1)}, f32[2,192,768]{2,1,0:T(8,128)}, f32[2,192]{1,0:T(2,128)}, f32[2,192,768]{...) custom-call(bf16[512,768]{1,0:T(8,128)(2,1)} %get-tuple-element.110., ...), custom_call_target="tpu_custom_call" | custom-call | tf_op jit(solution)/shard_map/finish_grads/pallas_call | solution.py:1492
